TPU v7x, 32 devices: a whole 2x2x4 slice. The times are simulated.
32 devices in a mesh: dp: 8 (over z, y), mp: 4 (over x, core).
Axes of the slice: x: 2, y: 2, z: 4, core: 2. Of those that a mesh axis runs over, the one named last changes fastest.
Arguments:
- tokens: bfloat16 [16384, 1024], P(('dp', 'mp')), may hold values from -60 to 60
- cotangent: bfloat16 [16384, 1024], P(('dp', 'mp')), may hold values from -6 to 6
- item_lengths: int32 [128], P('dp'), may hold values from 49 to 196, as said below
- item_group: int32 [128], P('dp'), may hold values from 0 to 7
- group_count: int32 [8], replicated, may hold values from 1 to 4
- grid_scale: float32 [8], replicated, may hold values from 0.5 to 2
- norm_gain: float32 [1024], replicated, may hold values from 0.5 to 1.5
- norm_shift: float32 [1024], replicated, may hold values from -2 to 2
- query_weight: bfloat16 [1024, 1024], P(None, 'mp'), may hold values from -0.1875 to 0.1875
- query_bias: float32 [1024], P('mp'), may hold values from -2 to 2
- key_weight: bfloat16 [1024, 1024], P(None, 'mp'), may hold values from -0.1875 to 0.1875
- value_weight: bfloat16 [1024, 1024], P(None, 'mp'), may hold values from -0.1875 to 0.1875
- value_bias: float32 [1024], P('mp'), may hold values from -2 to 2
- output_weight: bfloat16 [1024, 1024], P('mp'), may hold values from -1.5 to 1.5
- output_bias: float32 [1024], replicated, may hold values from -2 to 2
- hidden_gain: float32 [1024], replicated, may hold values from 0.5 to 1.5
- hidden_shift: float32 [1024], replicated, may hold values from -2 to 2
- up_weight: bfloat16 [1024, 4096], P(None, 'mp'), may hold values from -0.1875 to 0.1875
- up_bias: float32 [4096], P('mp'), may hold values from -2 to 2
- down_weight: bfloat16 [4096, 1024], P('mp'), may hold values from -0.09375 to 0.09375
- down_bias: float32 [1024], replicated, may hold values from -2 to 2
Outputs:
- layer_output: bfloat16 [16384, 1024], P(('dp', 'mp'))
- tokens_grad: float32 [16384, 1024], P(('dp', 'mp'))
- norm_gain_grad: float32 [1024], replicated
- norm_shift_grad: float32 [1024], replicated
- query_weight_grad: float32 [1024, 1024], P(None, 'mp')
- query_bias_grad: float32 [1024], P('mp')
- key_weight_grad: float32 [1024, 1024], P(None, 'mp')
- value_weight_grad: float32 [1024, 1024], P(None, 'mp')
- value_bias_grad: float32 [1024], P('mp')
- output_weight_grad: float32 [1024, 1024], P('mp')
- output_bias_grad: float32 [1024], replicated
- hidden_gain_grad: float32 [1024], replicated
- hidden_shift_grad: float32 [1024], replicated
- up_weight_grad: float32 [1024, 4096], P(None, 'mp')
- up_bias_grad: float32 [4096], P('mp')
- down_weight_grad: float32 [4096, 1024], P('mp')
- down_bias_grad: float32 [1024], replicated
Inputs may be any that keep to these rules, and one draw needn't show every extreme that they name: `item_lengths`: the items of a slice take its first 1960 rows: items 2i and 2i + 1 of a slice have lengths that add up to 245, and every slice has one pair of lengths 196 and 49.
All inputs are finite; a program needn't handle non-finite values.
Results may differ from a plain program's by a relative error of at most 0.018.
Values may be sent and summed in bfloat16 or wider, within the bound.
A program may use at most 192 MiB of HBM per device.

v0:
```python
import functools
import math

import jax
import jax.numpy as jnp
from jax import lax
from jax.sharding import PartitionSpec as P

D = 1024
HEAD_DIM = 64
SIDE = 14
PAIRS = 8
PAIR_LEN = 245
TOK_DEV = 2048


def normalize(values, gain, shift):
    center = values - jnp.mean(values, axis=-1, keepdims=True)
    spread = jnp.mean(center * center, axis=-1, keepdims=True)
    return center * lax.rsqrt(spread + 1e-06) * gain + shift


def position_table(position, row_scale):
    quarter = D // 4
    frequency = jnp.exp(-math.log(10000.0) * jnp.arange(quarter, dtype=jnp.float32) / quarter)
    across = (position // SIDE).astype(jnp.float32) * row_scale
    sideways = (position % SIDE).astype(jnp.float32) * row_scale
    first_angle = across[..., None] * frequency
    second_angle = sideways[..., None] * frequency
    return jnp.concatenate(
        [jnp.sin(first_angle), jnp.cos(first_angle), jnp.sin(second_angle), jnp.cos(second_angle)],
        axis=-1,
    )


def owners_of(row_ids, item_ends):
    return jnp.sum((row_ids[:, None] >= item_ends[None, :]).astype(jnp.int32), axis=1)


def contract_rows(first_matrix, second_matrix):
    return lax.dot_general(
        first_matrix, second_matrix, (((0,), (0,)), ((), ())), preferred_element_type=jnp.float32
    )


def contract_cols(first_matrix, second_matrix):
    return lax.dot_general(
        first_matrix, second_matrix, (((1,), (1,)), ((), ())), preferred_element_type=jnp.float32
    )


def window_starts():
    return [pair_index * PAIR_LEN for pair_index in range(PAIRS)] + [TOK_DEV - 256]


def to_windows(values):
    return jnp.stack(
        [
            lax.slice_in_dim(values, first_row, first_row + 256, axis=0)
            for first_row in window_starts()
        ]
    )


def from_windows(blocks):
    padding = TOK_DEV - PAIRS * PAIR_LEN
    kept = blocks[:PAIRS, :PAIR_LEN].reshape((PAIRS * PAIR_LEN,) + blocks.shape[2:])
    return jnp.concatenate([kept, blocks[PAIRS, 256 - padding :]], axis=0)


def masked_scores(query_heads, key_heads, owner_rows, factor):
    scores = (
        jnp.einsum("qhd,khd->hqk", query_heads, key_heads, preferred_element_type=jnp.float32)
        * factor
    )
    same_item = owner_rows[:, None] == owner_rows[None, :]
    return jnp.where(same_item[None], scores, -1e30)


def attend_forward(queries, keys_all, values_all, owner_all, factor):
    total_rows, head_width = queries.shape
    head_count = head_width // HEAD_DIM

    def one_window(query_rows, key_rows, value_rows, owner_rows):
        query_heads = query_rows.reshape(256, head_count, HEAD_DIM)
        key_heads = key_rows.reshape(256, head_count, HEAD_DIM)
        value_heads = value_rows.reshape(256, head_count, HEAD_DIM)
        scores = masked_scores(query_heads, key_heads, owner_rows, factor)
        row_top = jnp.max(scores, axis=-1, keepdims=True)
        weights = jnp.exp(scores - row_top)
        totals = jnp.sum(weights, axis=-1, keepdims=True)
        weights_low = (weights / totals).astype(jnp.bfloat16)
        context = jnp.einsum(
            "hqk,khd->qhd", weights_low, value_heads, preferred_element_type=jnp.float32
        )
        return (context.reshape(256, head_width), (row_top + jnp.log(totals))[:, :, 0])

    contexts, logsum = jax.vmap(one_window)(
        to_windows(queries), to_windows(keys_all), to_windows(values_all), to_windows(owner_all)
    )
    return (from_windows(contexts), logsum)


def attend_backward(queries, keys_all, values_all, grad_context, logsum, owner_all, factor):
    total_rows, head_width = queries.shape
    head_count = head_width // HEAD_DIM

    def one_window(query_rows, key_rows, value_rows, grad_rows, owner_rows, logsum_rows):
        query_heads = query_rows.reshape(256, head_count, HEAD_DIM)
        key_heads = key_rows.reshape(256, head_count, HEAD_DIM)
        value_heads = value_rows.reshape(256, head_count, HEAD_DIM)
        grad_heads = grad_rows.reshape(256, head_count, HEAD_DIM)
        scores = masked_scores(query_heads, key_heads, owner_rows, factor)
        weights_soft = jnp.exp(scores - logsum_rows[:, :, None])
        grad_soft = jnp.einsum(
            "qhd,khd->hqk", grad_heads, value_heads, preferred_element_type=jnp.float32
        )
        center = jnp.sum(weights_soft * grad_soft, axis=-1, keepdims=True)
        grad_scores = (weights_soft * (grad_soft - center)).astype(jnp.bfloat16)
        grad_query = (
            jnp.einsum("hqk,khd->qhd", grad_scores, key_heads, preferred_element_type=jnp.float32)
            * factor
        )
        grad_key = (
            jnp.einsum("hqk,qhd->khd", grad_scores, query_heads, preferred_element_type=jnp.float32)
            * factor
        )
        grad_value = jnp.einsum(
            "hqk,qhd->khd",
            weights_soft.astype(jnp.bfloat16),
            grad_heads,
            preferred_element_type=jnp.float32,
        )
        return (
            grad_query.astype(jnp.bfloat16).reshape(256, head_width),
            grad_key.astype(jnp.bfloat16).reshape(256, head_width),
            grad_value.astype(jnp.bfloat16).reshape(256, head_width),
        )

    grad_queries, grad_keys, grad_values = jax.vmap(one_window)(
        to_windows(queries),
        to_windows(keys_all),
        to_windows(values_all),
        to_windows(grad_context),
        to_windows(owner_all),
        logsum,
    )
    return (from_windows(grad_queries), from_windows(grad_keys), from_windows(grad_values))


def shards(
    tokens,
    cotangent,
    item_lengths,
    item_group,
    group_count,
    grid_scale,
    norm_gain,
    norm_shift,
    query_weight,
    query_bias,
    key_weight,
    value_weight,
    value_bias,
    output_weight,
    output_bias,
    hidden_gain,
    hidden_shift,
    up_weight,
    up_bias,
    down_weight,
    down_bias,
):
    shard_count = lax.axis_size("mp")
    shard_index = lax.axis_index("mp")
    slice_count = lax.axis_size("dp")
    rows_here = tokens.shape[0]
    slice_rows = rows_here * shard_count
    item_count = item_lengths.shape[0]
    item_ends = jnp.cumsum(item_lengths)
    starts = item_ends - item_lengths
    owner_all = owners_of(jnp.arange(slice_rows, dtype=jnp.int32), item_ends)
    local_ids = shard_index * rows_here + jnp.arange(rows_here, dtype=jnp.int32)
    owner_here = owners_of(local_ids, item_ends)
    member = owner_here[:, None] == jnp.arange(item_count, dtype=jnp.int32)[None, :]
    member_f = member.astype(jnp.float32)
    position = local_ids - jnp.sum(jnp.where(member, starts[None, :], 0), axis=1)
    chosen = item_group[:, None] == jnp.arange(group_count.shape[0], dtype=jnp.int32)[None, :]
    item_scale = jnp.sum(jnp.where(chosen, grid_scale[None, :], 0.0), axis=1)
    item_weight = jnp.sum(jnp.where(chosen, group_count[None, :], 0), axis=1).astype(jnp.float32)
    valid_rows = (owner_here < item_count).astype(jnp.float32)
    grid_table = (
        position_table(position, jnp.sum(member_f * item_scale[None, :], axis=1))
        * valid_rows[:, None]
    )
    tokens_f = tokens.astype(jnp.float32)
    weighted = tokens_f * valid_rows[:, None]
    sum_first, sum_second, weight_total = lax.psum(
        (
            jnp.sum(weighted, axis=0),
            jnp.sum(weighted * tokens_f, axis=0),
            jnp.sum(item_weight, keepdims=True) / shard_count,
        ),
        ("dp", "mp"),
    )
    count_valid = slice_count * PAIRS * PAIR_LEN
    column_mean = sum_first / count_valid
    spread = sum_second / count_valid - column_mean * column_mean
    inverse = lax.rsqrt(spread + 1e-05)
    standard = (tokens_f - column_mean) * inverse
    stream = standard + grid_table
    row_weight = jnp.sum(member_f * item_weight[None, :], axis=1) / (
        weight_total / (slice_count * item_count)
    )
    normed = normalize(stream, norm_gain, norm_shift).astype(jnp.bfloat16)
    normed_all = lax.all_gather(normed, "mp", axis=0, tiled=True)
    factor = 1.0 / math.sqrt(HEAD_DIM)
    queries = (
        jnp.dot(normed_all, query_weight, preferred_element_type=jnp.float32) + query_bias
    ).astype(jnp.bfloat16)
    keys_all = jnp.dot(normed_all, key_weight, preferred_element_type=jnp.float32).astype(
        jnp.bfloat16
    )
    values_all = (
        jnp.dot(normed_all, value_weight, preferred_element_type=jnp.float32) + value_bias
    ).astype(jnp.bfloat16)
    context, logsum = attend_forward(queries, keys_all, values_all, owner_all, factor)
    context_low = context.astype(jnp.bfloat16)
    attended = (
        lax.psum_scatter(
            jnp.dot(context_low, output_weight, preferred_element_type=jnp.float32).astype(
                jnp.bfloat16
            ),
            "mp",
            scatter_dimension=0,
            tiled=True,
        ).astype(jnp.float32)
        + output_bias
    )
    middle = stream + attended
    hidden_in = normalize(middle, hidden_gain, hidden_shift).astype(jnp.bfloat16)
    hidden_all = lax.all_gather(hidden_in, "mp", axis=0, tiled=True)
    preact = jnp.dot(hidden_all, up_weight, preferred_element_type=jnp.float32) + up_bias
    active = jax.nn.gelu(preact, approximate=False).astype(jnp.bfloat16)
    mixed = (
        lax.psum_scatter(
            jnp.dot(active, down_weight, preferred_element_type=jnp.float32).astype(jnp.bfloat16),
            "mp",
            scatter_dimension=0,
            tiled=True,
        ).astype(jnp.float32)
        + down_bias
    )
    layer_output = (middle + mixed).astype(jnp.bfloat16)
    grad_out = cotangent.astype(jnp.float32) * row_weight[:, None]
    grad_mixed = grad_out.astype(jnp.bfloat16)
    grad_mixed_all = lax.all_gather(grad_mixed, "mp", axis=0, tiled=True)
    down_weight_grad = contract_rows(active, grad_mixed_all)
    grad_active = contract_cols(grad_mixed_all, down_weight)
    gelu_pull = jax.vjp(functools.partial(jax.nn.gelu, approximate=False), preact)[1]
    grad_pre = gelu_pull(grad_active)[0].astype(jnp.bfloat16)
    up_bias_grad = jnp.sum(grad_pre.astype(jnp.float32), axis=0)
    up_weight_grad = contract_rows(hidden_all, grad_pre)
    grad_hidden = lax.psum_scatter(
        contract_cols(grad_pre, up_weight).astype(jnp.bfloat16),
        "mp",
        scatter_dimension=0,
        tiled=True,
    ).astype(jnp.float32)
    hidden_pull = jax.vjp(normalize, middle, hidden_gain, hidden_shift)[1]
    grad_middle, hidden_gain_part, hidden_shift_part = hidden_pull(grad_hidden)
    grad_middle = grad_middle + grad_out
    grad_attended = grad_middle.astype(jnp.bfloat16)
    grad_attended_all = lax.all_gather(grad_attended, "mp", axis=0, tiled=True)
    output_weight_grad = contract_rows(context_low, grad_attended_all)
    grad_context = contract_cols(grad_attended_all, output_weight).astype(jnp.bfloat16)
    grad_queries, grad_keys, grad_values = attend_backward(
        queries, keys_all, values_all, grad_context, logsum, owner_all, factor
    )
    query_bias_grad = jnp.sum(grad_queries.astype(jnp.float32), axis=0)
    value_bias_grad = jnp.sum(grad_values.astype(jnp.float32), axis=0)
    query_weight_grad = contract_rows(normed_all, grad_queries)
    key_weight_grad = contract_rows(normed_all, grad_keys)
    value_weight_grad = contract_rows(normed_all, grad_values)
    query_part = contract_cols(grad_queries, query_weight)
    key_part = contract_cols(grad_keys, key_weight)
    value_part = contract_cols(grad_values, value_weight)
    grad_normed = lax.psum_scatter(
        (query_part + key_part + value_part).astype(jnp.bfloat16),
        "mp",
        scatter_dimension=0,
        tiled=True,
    ).astype(jnp.float32)
    norm_pull = jax.vjp(normalize, stream, norm_gain, norm_shift)[1]
    grad_stream, norm_gain_part, norm_shift_part = norm_pull(grad_normed)
    grad_stream = grad_stream + grad_middle
    (
        sum_grad,
        sum_cross,
        norm_gain_grad,
        norm_shift_grad,
        hidden_gain_grad,
        hidden_shift_grad,
        output_bias_grad,
        down_bias_grad,
    ) = lax.psum(
        (
            jnp.sum(grad_stream, axis=0),
            jnp.sum(grad_stream * standard, axis=0),
            norm_gain_part,
            norm_shift_part,
            hidden_gain_part,
            hidden_shift_part,
            jnp.sum(grad_attended.astype(jnp.float32), axis=0),
            jnp.sum(grad_mixed.astype(jnp.float32), axis=0),
        ),
        ("dp", "mp"),
    )
    tokens_grad = inverse * (
        grad_stream - valid_rows[:, None] / count_valid * (sum_grad + sum_cross * standard)
    )
    (
        query_weight_grad,
        query_bias_grad,
        key_weight_grad,
        value_weight_grad,
        value_bias_grad,
        output_weight_grad,
        up_weight_grad,
        up_bias_grad,
        down_weight_grad,
    ) = lax.psum(
        (
            query_weight_grad,
            query_bias_grad,
            key_weight_grad,
            value_weight_grad,
            value_bias_grad,
            output_weight_grad,
            up_weight_grad,
            up_bias_grad,
            down_weight_grad,
        ),
        "dp",
    )
    return (
        layer_output,
        tokens_grad,
        norm_gain_grad,
        norm_shift_grad,
        query_weight_grad,
        query_bias_grad,
        key_weight_grad,
        value_weight_grad,
        value_bias_grad,
        output_weight_grad,
        output_bias_grad,
        hidden_gain_grad,
        hidden_shift_grad,
        up_weight_grad,
        up_bias_grad,
        down_weight_grad,
        down_bias_grad,
    )


def solution(mesh):
    return jax.shard_map(
        shards,
        mesh=mesh,
        in_specs=(
            P(("dp", "mp"), None),
            P(("dp", "mp"), None),
            P("dp"),
            P("dp"),
            P(),
            P(),
            P(),
            P(),
            P(None, "mp"),
            P("mp"),
            P(None, "mp"),
            P(None, "mp"),
            P("mp"),
            P("mp", None),
            P(),
            P(),
            P(),
            P(None, "mp"),
            P("mp"),
            P("mp", None),
            P(),
        ),
        out_specs=(
            P(("dp", "mp"), None),
            P(("dp", "mp"), None),
            P(),
            P(),
            P(None, "mp"),
            P("mp"),
            P(None, "mp"),
            P(None, "mp"),
            P("mp"),
            P("mp", None),
            P(),
            P(),
            P(),
            P(None, "mp"),
            P("mp"),
            P("mp", None),
            P(),
        ),
        check_vma=False,
    )
```

profile of v0, /device:TPU:1, one launch (start us, length us, event | category | flops | bytes accessed | tf_op | source)
XLA Modules:
  0.0 938.8 jit_solution(6641082775959108144)
XLA Ops:
  14.3 41.6 %all-reduce.1 = (f32[1024]{0:T(1024)S(1)}, f32[1024]{0:T(1024)S(1)}, f32[1]{0:T(128)}) all-reduce(f32[1024]{0:T(1024)S(1)} %get-tuple-element.24, f32[1024]{0:T(1024)S(1)} %get-tuple-element.23, f32[1]{0:T(128)} %bitcast.41), channel_id=1, replica_groups=mesh['dp'=8,'mp'=4] {'dp','mp'}, use_global_device_ids=true, to_apply=%region_5.6 | all-reduce | flops 2049 | bytes 16392 | tf_op jit(solution)/shard_map/psum | solution.py:198
  56.6 3.7 multiply_sine_fusion.1
  65.0 34.4 %all-gather.5.cloned.1.call-done = bf16[2048,1024]{1,0:T(8,128)(2,1)} async-done(((bf16[512,1024]{1,0:T(8,128)(2,1)}), bf16[2048,1024]{1,0:T(8,128)(2,1)}) %all-gather.5.cloned.1.call-update) | async-done | bytes 4194320 | tf_op jit(solution)/shard_map/all_gather | solution.py:216
  99.3 3.6 convolution_convert_fusion.4
  119.1 4.7 convolution_convert_fusion
  123.9 44.2 %reduce-scatter.5.cloned.1.call-done = bf16[512,1024]{1,0:T(8,128)(2,1)} async-done(((bf16[2048,1024]{1,0:T(8,128)(2,1)}), bf16[512,1024]{1,0:T(8,128)(2,1)}) %reduce-scatter.5.cloned.1.call-update) | async-done | bytes 1048592 | tf_op jit(solution)/shard_map/reduce_scatter | solution.py:230
  175.0 33.0 %all-gather.7.cloned.1.call-done = bf16[2048,1024]{1,0:T(8,128)(2,1)} async-done(((bf16[512,1024]{1,0:T(8,128)(2,1)}), bf16[2048,1024]{1,0:T(8,128)(2,1)}) %all-gather.7.cloned.1.call-update) | async-done | bytes 4194320 | tf_op jit(solution)/shard_map/all_gather | solution.py:242
  208.1 11.4 %fusion.73 = f32[2048,1024]{1,0:T(8,128)} fusion(bf16[2048,1024]{1,0:T(8,128)(2,1)} %all-gather.7.cloned.1.call-done, bf16[1024,1024]{1,0:T(8,128)(2,1)} %param.38), kind=kOutput, calls=%fused_computation.196 | convolution fusion | flops 4294967296 | bytes 14680064 | tf_op jit(solution)/shard_map/dot_general | solution.py:243
  219.5 25.2 %all-gather.9.cloned.1.call-done = bf16[2048,1024]{1,0:T(8,128)(2,1)} async-done(((bf16[512,1024]{1,0:T(8,128)(2,1)}), bf16[2048,1024]{1,0:T(8,128)(2,1)}) %all-gather.9.cloned.1.call-update) | async-done | bytes 4194320 | tf_op jit(solution)/shard_map/all_gather | solution.py:257
  244.7 27.1 %convert_reduce_fusion = (f32[1024]{0:T(1024)S(1)}, bf16[2048,1024]{1,0:T(8,128)(2,1)S(1)}, f32[2048,1024]{1,0:T(8,128)}) fusion(f32[2048,1024]{1,0:T(8,128)} %fusion.73, f32[1024]{0:T(1024)S(1)} %copy-done.57, bf16[2048,1024]{1,0:T(8,128)(2,1)} %all-gather.9.cloned.1.call-done, bf16[1024,1024]{1,0:T(8,128)(2,1)S(1)} %copy-done), kind=kOutput, calls=%fused_computation.8 | convolution fusion | flops 4452252672 | bytes 27271168 | tf_op jit(solution)/shard_map/dot_general | solution.py:47
  273.9 6.2 convolution_convert_fusion.1
  280.2 10.3 %multiply_convert_fusion.1 = bf16[2048,1024]{1,0:T(8,128)(2,1)} fusion(f32[2048,1024]{1,0:T(8,128)} %get-tuple-element.52, f32[2048,1024]{1,0:T(8,128)} %fusion.73, f32[1024]{0:T(1024)S(1)} %copy-done.57), kind=kLoop, calls=%fused_computation.11 | loop fusion | flops 8388608 | bytes 20975616 | tf_op jit(solution)/shard_map/convert_element_type | solution.py:244
  290.5 8.5 convolution_convert_fusion.2
  299.6 24.8 %reduce-scatter.9.cloned.1.call-done = bf16[512,1024]{1,0:T(8,128)(2,1)} async-done(((bf16[2048,1024]{1,0:T(8,128)(2,1)}), bf16[512,1024]{1,0:T(8,128)(2,1)}) %reduce-scatter.9.cloned.1.call-update) | async-done | bytes 1048592 | tf_op jit(solution)/shard_map/reduce_scatter | solution.py:264
  324.4 2.7 fusion.31
  327.1 44.2 %reduce-scatter.7.cloned.1.call-done = bf16[512,1024]{1,0:T(8,128)(2,1)} async-done(((bf16[2048,1024]{1,0:T(8,128)(2,1)}), bf16[512,1024]{1,0:T(8,128)(2,1)}) %reduce-scatter.7.cloned.1.call-update) | async-done | bytes 1048592 | tf_op jit(solution)/shard_map/reduce_scatter | solution.py:246
  371.3 4.1 fusion.63
  377.2 35.0 %all-gather.11.cloned.1.call-done = bf16[2048,1024]{1,0:T(8,128)(2,1)} async-done(((bf16[512,1024]{1,0:T(8,128)(2,1)}), bf16[2048,1024]{1,0:T(8,128)(2,1)}) %all-gather.11.cloned.1.call-update) | async-done | bytes 4194320 | tf_op jit(solution)/shard_map/all_gather | solution.py:274
  412.2 3.7 convolution_convert_fusion.3
  416.5 5.6 fusion.34
  423.7 4.7 multiply_reduce_fusion
  428.4 11.4 %multiply_convert_fusion = bf16[9,4,256,256]{2,3,1,0:T(8,128)(2,1)} fusion(f32[9,4,256,256]{2,3,1,0:T(8,128)} %get-tuple-element.125, f32[9,4,256,256]{2,3,1,0:T(8,128)} %copy-done.1, f32[9,4,256]{2,1,0:T(4,128)S(1)} %get-tuple-element.124, f32[9,4,256]{2,1,0:T(4,128)S(1)} %log_add_fusion), kind=kLoop, calls=%fused_computation.1 | loop fusion | flops 9437184 | bytes 23666688 | tf_op jit(solution)/shard_map/vmap()/convert_element_type | solution.py:119
  439.8 4.0 multiply_convert_fusion.2
  462.8 3.3 add_convert_fusion
  466.4 10.1 %fusion.74 = f32[1024,1024]{1,0:T(8,128)} fusion(bf16[2048,1024]{1,0:T(8,128)(2,1)} %all-gather.7.cloned.1.call-done, bf16[2048,1024]{1,0:T(8,128)(2,1)} %copy-done.65), kind=kOutput, calls=%fused_computation.197 | convolution fusion | flops 4294967296 | bytes 12582912 | tf_op jit(solution)/shard_map/dot_general | solution.py:41
  476.5 6.1 fusion.75
  494.3 18.7 %all-reduce.2 = (f32[256]{0:T(256)}, f32[256]{0:T(256)}, f32[1024]{0:T(1024)}) all-reduce(f32[256]{0:T(256)S(1)} %convert_reduce_fusion.6, f32[256]{0:T(256)S(1)} %convert_reduce_fusion.5, f32[1024]{0:T(1024)S(1)} %get-tuple-element.50), channel_id=1, replica_groups=mesh['dp'=8,'mp'=4] {'dp'}, use_global_device_ids=true, to_apply=%region_39.40 | all-reduce | flops 1536 | bytes 12288 | tf_op jit(solution)/shard_map/psum | solution.py:332
  513.1 2.7 convert_reduce_fusion.1
  517.6 3.7 fusion.59
  521.3 46.4 %all-reduce = (f32[1024]{0:T(1024)S(1)}, f32[1024]{0:T(1024)S(1)}, f32[1024]{0:T(1024)}, f32[1024]{0:T(1024)}, f32[1024]{0:T(1024)}, /*index=5*/f32[1024]{0:T(1024)}, f32[1024]{0:T(1024)}, f32[1024]{0:T(1024)}) all-reduce(f32[1024]{0:T(1024)S(1)} %get-tuple-element.22, ...), channel_id=1, replica_groups=mesh['dp'=8,'mp'=4] {'dp','mp'}, use_global_device_ids=true, to_apply=%region_32.33 | all-reduce | flops 8192 | bytes 65536 | tf_op jit(solution)/shard_map/psum | solution.py:306
  567.8 3.5 fusion.29
  571.2 349.6 %all-reduce.6.cloned.1.call-done = (f32[1024,256]{1,0:T(8,128)}, f32[1024,256]{1,0:T(8,128)}, f32[1024,256]{1,0:T(8,128)}, f32[256,1024]{1,0:T(8,128)}, f32[1024,1024]{1,0:T(8,128)}, /*index=5*/f32[1024,1024]{1,0:T(8,128)}) async-done(((f32[1024,256]{1,0:T(8,128)}, f32[1024,256]{1,0:T(8,128)}, f32[1024,256]{1,0:T(8,128)}, f32[256,1024]{1,0:T(8,128)}, f32[1024,1024]{1,0:T(8,128)}, ...) | async-done | bytes 12582928 | tf_op jit(solution)/shard_map/psum | solution.py:332
  (278 shorter events, 84.1 us)
Async XLA Ops:
  7.2 237.5 %copy-start = (bf16[1024,1024]{1,0:T(8,128)(2,1)S(1)}, bf16[1024,1024]{1,0:T(8,128)(2,1)}, u32[]{:S(2)}) copy-start(bf16[1024,1024]{1,0:T(8,128)(2,1)} %param.40) | copy-start | bytes 6291460
  7.2 53.1 %copy-start.8 = (bf16[512,1024]{1,0:T(8,128)(2,1)S(1)}, bf16[512,1024]{1,0:T(8,128)(2,1)}, u32[]{:S(2)}) copy-start(bf16[512,1024]{1,0:T(8,128)(2,1)} %param.21) | copy-start | bytes 3145732
  7.2 92.1 %all-gather.5.cloned.1.call-start = ((), (), s32[]{:S(2)}) async-start(), calls=%async_computation.4 | async-start | bytes 5242880 | tf_op jit(solution)/shard_map/all_gather | solution.py:216
  62.2 37.1 %copy-start.31 = (bf16[1024,256]{1,0:T(8,128)(2,1)S(1)}, bf16[1024,256]{1,0:T(8,128)(2,1)}, u32[]{:S(2)}) copy-start(bf16[1024,256]{1,0:T(8,128)(2,1)} %param.31) | copy-start | bytes 1572868
  63.7 104.4 %reduce-scatter.5.cloned.1.call-start = ((), (), s32[]{:S(2)}) async-start(), calls=%async_computation.5 | async-start | bytes 5242880 | tf_op jit(solution)/shard_map/reduce_scatter | solution.py:230
  117.6 6.2 copy-start.36
  123.8 44.3 %copy-start.56 = (f32[1024]{0:T(1024)S(1)}, f32[1024]{0:T(1024)}, u32[]{:S(2)}) copy-start(f32[1024]{0:T(1024)} %param.35) | copy-start | bytes 12292
  123.8 84.2 %all-gather.7.cloned.1.call-start = ((), (), s32[]{:S(2)}) async-start(), calls=%async_computation.6 | async-start | bytes 5242880 | tf_op jit(solution)/shard_map/all_gather | solution.py:242
  173.0 71.6 %all-gather.9.cloned.1.call-start = ((), (), s32[]{:S(2)}) async-start(), calls=%async_computation.8 | async-start | bytes 5242880 | tf_op jit(solution)/shard_map/all_gather | solution.py:257
  175.0 69.7 %copy-start.57 = (f32[1024]{0:T(1024)S(1)}, f32[1024]{0:T(1024)}, u32[]{:S(2)}) copy-start(f32[1024]{0:T(1024)} %param.39) | copy-start | bytes 12292
  175.0 149.4 %reduce-scatter.9.cloned.1.call-start = ((), (), s32[]{:S(2)}) async-start(), calls=%async_computation.9 | async-start | bytes 5242880 | tf_op jit(solution)/shard_map/reduce_scatter | solution.py:264
  244.7 29.2 %copy-start.62 = (bf16[1024,1024]{1,0:T(8,128)(2,1)S(1)}, bf16[1024,1024]{1,0:T(8,128)(2,1)}, u32[]{:S(2)}) copy-start(bf16[1024,1024]{1,0:T(8,128)(2,1)} %param.38) | copy-start | bytes 6291460
  280.2 91.2 %reduce-scatter.7.cloned.1.call-start = ((), (), s32[]{:S(2)}) async-start(), calls=%async_computation.7 | async-start | bytes 5242880 | tf_op jit(solution)/shard_map/reduce_scatter | solution.py:246
  299.1 72.3 %copy-start.53 = (f32[1024]{0:T(1024)S(1)}, f32[1024]{0:T(1024)}, u32[]{:S(2)}) copy-start(f32[1024]{0:T(1024)} %param.41) | copy-start | bytes 12292
  299.1 113.1 %all-gather.11.cloned.1.call-start = ((), (), s32[]{:S(2)}) async-start(), calls=%async_computation.10 | async-start | bytes 5242880 | tf_op jit(solution)/shard_map/all_gather | solution.py:274
  377.1 136.0 %reduce-scatter.11.cloned.1.call-start = ((), (), s32[]{:S(2)}) async-start(), calls=%async_computation.11 | async-start | bytes 5242880 | tf_op jit(solution)/shard_map/reduce_scatter | solution.py:288
  412.2 11.0 %slice-start = ((s8[9437184]{0:T(1024)(128)(4,1)}), s8[4194304]{0:T(1024)(128)(4,1)S(1)}, s32[]{:S(2)}) async-start(s8[9437184]{0:T(1024)(128)(4,1)} %bitcast.102), calls=%async_computation.13 | async-start | bytes 8388608
  415.9 7.3 slice-start.1
  416.5 6.7 slice-start.2
  428.4 11.4 %copy-start.17 = (bf16[9,256,4,64]{1,3,2,0:T(8,128)(2,1)S(1)}, bf16[9,256,4,64]{1,3,2,0:T(8,128)(2,1)}, u32[]{:S(2)}) copy-start(bf16[9,256,4,64]{1,3,2,0:T(8,128)(2,1)} %copy-done.16) | copy-start | bytes 3538948
  450.9 4.9 copy-start.21
  466.1 454.7 %all-reduce.6.cloned.1.call-start = ((), (), s32[]{:S(2)}) async-start(), calls=%async_computation.12 | async-start | bytes 25165824 | tf_op jit(solution)/shard_map/psum | solution.py:332
  466.4 10.1 %copy-start.22 = (bf16[2048,1024]{1,0:T(8,128)(2,1)S(1)}, bf16[2048,1024]{1,0:T(8,128)(2,1)}, u32[]{:S(2)}) copy-start(bf16[2048,1024]{1,0:T(8,128)(2,1)} %multiply_convert_fusion.1) | copy-start | bytes 12582916
  466.4 10.1 %copy-start.60 = (bf16[2048,1024]{1,0:T(8,128)(2,1)S(1)}, bf16[2048,1024]{1,0:T(8,128)(2,1)}, u32[]{:S(2)}) copy-start(bf16[2048,1024]{1,0:T(8,128)(2,1)} %all-gather.9.cloned.1.call-done) | copy-start | bytes 12582916
  476.5 6.1 copy-start.25
  476.5 6.1 copy-start.37
  476.5 6.1 copy-start.61
  492.5 20.6 %copy-start.39 = (f32[512]{0:T(512)S(1)}, f32[512]{0:T(512)}, u32[]{:S(2)}) copy-start(f32[512]{0:T(512)} %copy-done.38) | copy-start | bytes 6148
  492.5 20.6 %copy-start.41 = (f32[1024]{0:T(1024)S(1)}, f32[1024]{0:T(1024)}, u32[]{:S(2)}) copy-start(f32[1024]{0:T(1024)} %param.27) | copy-start | bytes 12292
  494.0 21.8 %copy-start.50 = (f32[512]{0:T(512)S(1)}, f32[512]{0:T(512)}, u32[]{:S(2)}) copy-start(f32[512]{0:T(512)} %copy-done.49) | copy-start | bytes 6148
  494.0 21.8 %copy-start.48 = (f32[512]{0:T(512)S(1)}, f32[512]{0:T(512)}, u32[]{:S(2)}) copy-start(f32[512]{0:T(512)} %copy-done.47) | copy-start | bytes 6148
  517.6 50.1 %copy-start.52 = (f32[512]{0:T(512)S(1)}, f32[512]{0:T(512)}, u32[]{:S(2)}) copy-start(f32[512]{0:T(512)} %get-tuple-element.53) | copy-start | bytes 6148
  (46 other events, 109.5 us)
Sparse Core Ops, SparseCore 0:
  63.8 35.5 all-gather.4
  124.0 44.0 reduce-scatter.4
  173.1 34.8 all-gather.6
  210.1 34.4 all-gather.8
  280.3 44.0 reduce-scatter.8
  326.8 44.4 reduce-scatter.6
  377.2 34.9 all-gather.10
  466.3 44.1 reduce-scatter.10
  517.0 403.7 all-reduce.5
where the time goes:
time: 946 us; the launch traced here: 939 us
  waiting for transfers between devices  591 us (62%)
  matrix products  119 us (13%)
  blocking collectives  107 us (11%)
  other arithmetic  62.7 us (7%)
  local copies, waits for them, and re-layouts  41.6 us (4%)
  between operations  16.5 us (2%)
    psum x1, waiting for transfers between devices, shards(): lax.psum((query_weight_grad, query_bias_grad, key_weight_grad, value_weig...  350 us
    psum x1, blocking collectives, shards(): lax.psum((jnp.sum(grad_stream, axis=0), jnp.sum(grad_stream * standard, a...  46.4 us
    dot_general x6, matrix products, contract_cols(): lax.dot_general(first_matrix, second_matrix, (((1,), (1,)), ((), ())), pr...  44.4 us
    reduce_scatter x1, waiting for transfers between devices, shards(): lax.psum_scatter(jnp.dot(context_low, output_weight, preferred_element_ty...  44.2 us
    reduce_scatter x1, waiting for transfers between devices, shards(): lax.psum_scatter(jnp.dot(active, down_weight, preferred_element_type=jnp....  44.2 us
    psum x1, blocking collectives, shards(): lax.psum((jnp.sum(weighted, axis=0), jnp.sum(weighted * tokens_f, axis=0)...  41.6 us
    all_gather x1, waiting for transfers between devices, shards(): grad_attended_all = lax.all_gather(grad_attended, 'mp', axis=0, tiled=True)  35 us
    all_gather x1, waiting for transfers between devices, shards(): normed_all = lax.all_gather(normed, 'mp', axis=0, tiled=True)  34.4 us
  transfers between devices with their start and end apart: 9, of which 8 were waited for; matrix products, arithmetic and copies ran while one was open for 8% of the time, Pallas kernels for 0%

commit v1 on v0

v1 whole, which is shorter than its diff:
```python
import functools
import math

import jax
import jax.numpy as jnp
from jax import lax
from jax.experimental import pallas as pl
from jax.experimental.pallas import tpu as pltpu
from jax.sharding import PartitionSpec as P

D = 1024
HEAD_DIM = 64
SIDE = 14
PAIRS = 8
PAIR_LEN = 245
WINDOW = 256
BF = jnp.bfloat16
F32 = jnp.float32
PADDING = 88


def dot(a, b):
    return lax.dot_general(a, b, (((1,), (0,)), ((), ())), preferred_element_type=F32)


def dot_rows(a, b):
    return lax.dot_general(a, b, (((0,), (0,)), ((), ())), preferred_element_type=F32)


def dot_cols(a, b):
    return lax.dot_general(a, b, (((1,), (1,)), ((), ())), preferred_element_type=F32)


def swap_mp(v, mask):
    count = lax.axis_size("mp")
    return lax.ppermute(v, "mp", [(i, i ^ mask) for i in range(count)])


def swap_dp(v, mask):
    count = lax.axis_size("dp")
    return lax.ppermute(v, "dp", [(i, i ^ mask) for i in range(count)])


def dp_bits():
    return lax.axis_size("dp").bit_length() - 1


def all_sum(v):
    v = v + swap_mp(v, 1) + swap_mp(v, 2) + swap_mp(v, 3)
    bit = 0
    bits = dp_bits()
    while bit < bits:
        if bit + 1 < bits:
            v = v + swap_dp(v, 1 << bit) + swap_dp(v, 2 << bit) + swap_dp(v, 3 << bit)
            bit += 2
        else:
            v = v + swap_dp(v, 1 << bit)
            bit += 1
    return v


def dp_bit(bit):
    return (lax.axis_index("dp") >> bit) & 1


def join(mine, other, bit):
    return jnp.where(
        dp_bit(bit) == 0,
        jnp.concatenate([mine, other], axis=0),
        jnp.concatenate([other, mine], axis=0),
    )


def chunk_index():
    index = jnp.int32(0)
    for bit in range(dp_bits()):
        index = index * 2 + dp_bit(bit)
    return index


def fetch_across(w):
    rows = w.shape[0] // lax.axis_size("dp")
    mine = lax.dynamic_slice_in_dim(w, chunk_index() * rows, rows, axis=0)
    got = swap_mp(mine, 2)
    for bit in reversed(range(dp_bits())):
        got = join(got, swap_dp(got, 1 << bit), bit)
    return got


def reduce_pieces(pieces):
    half = pieces[1].shape[0]
    got = swap_mp(jnp.concatenate([pieces[1], pieces[3]], axis=0), 1)
    across = pieces[2].astype(F32) + got[half:].astype(F32)
    own = pieces[0].astype(F32) + got[:half].astype(F32)
    total = own + swap_mp(across.astype(BF), 2).astype(F32)
    for bit in range(dp_bits()):
        size = total.shape[0] // 2
        side = dp_bit(bit)
        send = lax.dynamic_slice_in_dim(total, (1 - side) * size, size, axis=0).astype(BF)
        keep = lax.dynamic_slice_in_dim(total, side * size, size, axis=0)
        total = keep + swap_dp(send, 1 << bit).astype(F32)
    total = total.astype(BF)
    for bit in reversed(range(dp_bits())):
        total = join(total, swap_dp(total, 1 << bit), bit)
    return total.astype(F32)


def stats(v):
    mean = jnp.mean(v, axis=-1, keepdims=True)
    center = v - mean
    spread = jnp.mean(center * center, axis=-1, keepdims=True)
    inverse = lax.rsqrt(spread + 1e-06)
    return center * inverse, inverse


def norm_back(grad, unit, inverse, gain):
    f = grad * gain
    return inverse * (
        f
        - jnp.mean(f, axis=-1, keepdims=True)
        - unit * jnp.mean(f * unit, axis=-1, keepdims=True)
    )


def blocks_of(rows):
    return [(first, min(WINDOW, rows - first)) for first in range(0, rows, WINDOW)]


def head_scores(qkv_ref, same, first, size, h, width):
    q = qkv_ref[first : first + size, h * HEAD_DIM : (h + 1) * HEAD_DIM]
    k = qkv_ref[first : first + size, width + h * HEAD_DIM : width + (h + 1) * HEAD_DIM]
    v = qkv_ref[first : first + size, 2 * width + h * HEAD_DIM : 2 * width + (h + 1) * HEAD_DIM]
    scores = jnp.where(same, dot_cols(q, k) * (1.0 / math.sqrt(HEAD_DIM)), -1e30)
    weights = jnp.exp(scores - jnp.max(scores, axis=-1, keepdims=True))
    weights = weights * (1.0 / jnp.sum(weights, axis=-1, keepdims=True))
    return q, k, v, weights


def attend_kernel(qkv_ref, col_ref, row_ref, out_ref):
    rows, width = out_ref.shape
    for first, size in blocks_of(rows):
        same = col_ref[first : first + size, :] == row_ref[:, first : first + size]
        for h in range(width // HEAD_DIM):
            q, k, v, weights = head_scores(qkv_ref, same, first, size, h, width)
            out_ref[first : first + size, h * HEAD_DIM : (h + 1) * HEAD_DIM] = dot(
                weights.astype(BF), v
            ).astype(BF)


def attend_back_kernel(qkv_ref, grad_ref, col_ref, row_ref, out_ref):
    rows, width = grad_ref.shape
    factor = 1.0 / math.sqrt(HEAD_DIM)
    for first, size in blocks_of(rows):
        same = col_ref[first : first + size, :] == row_ref[:, first : first + size]
        for h in range(width // HEAD_DIM):
            q, k, v, weights = head_scores(qkv_ref, same, first, size, h, width)
            grad = grad_ref[first : first + size, h * HEAD_DIM : (h + 1) * HEAD_DIM]
            soft = dot_cols(grad, v)
            center = jnp.sum(weights * soft, axis=-1, keepdims=True)
            grad_scores = (weights * (soft - center)).astype(BF)
            for part, value in enumerate(
                (
                    dot(grad_scores, k) * factor,
                    dot_rows(grad_scores, q) * factor,
                    dot_rows(weights.astype(BF), grad),
                )
            ):
                lane = part * width + h * HEAD_DIM
                out_ref[first : first + size, lane : lane + HEAD_DIM] = value.astype(BF)


def attend(qkv, owner_col, owner_row, groups):
    rows, width = qkv.shape[0], qkv.shape[1] // (3 * groups)
    return pl.pallas_call(
        attend_kernel,
        grid=(groups,),
        in_specs=[
            pl.BlockSpec((rows, 3 * width), lambda r: (0, r)),
            pl.BlockSpec((rows, 1), lambda r: (0, 0)),
            pl.BlockSpec((1, rows), lambda r: (0, 0)),
        ],
        out_specs=pl.BlockSpec((rows, width), lambda r: (0, r)),
        out_shape=jax.ShapeDtypeStruct((rows, groups * width), BF),
        name="attend",
    )(qkv, owner_col, owner_row)


def attend_back(qkv, grad, owner_col, owner_row, groups):
    rows, width = grad.shape[0], grad.shape[1] // groups
    return pl.pallas_call(
        attend_back_kernel,
        grid=(groups,),
        in_specs=[
            pl.BlockSpec((rows, 3 * width), lambda r: (0, r)),
            pl.BlockSpec((rows, width), lambda r: (0, r)),
            pl.BlockSpec((rows, 1), lambda r: (0, 0)),
            pl.BlockSpec((1, rows), lambda r: (0, 0)),
        ],
        out_specs=pl.BlockSpec((rows, 3 * width), lambda r: (0, r)),
        out_shape=jax.ShapeDtypeStruct((rows, 3 * groups * width), BF),
        name="attend_back",
    )(qkv, grad, owner_col, owner_row)


def gelu_parts(preact):
    phi = 0.5 * (1.0 + lax.erf(preact * (1.0 / math.sqrt(2.0))))
    slope = phi + preact * jnp.exp(-0.5 * preact * preact) * (1.0 / math.sqrt(2.0 * math.pi))
    return (preact * phi).astype(BF), slope


HALO = 80
MESH = pl.DeviceIdType.MESH


def places():
    mp = lax.axis_index("mp")
    dp = lax.axis_index("dp")
    y = dp % 2
    z = dp // 2
    sibling = mp + 1 - 2 * (mp % 2)
    opposite = mp + 2 - 4 * (mp // 2)
    across = opposite + 1 - 2 * (mp % 2)
    mp_peers = [{"mp": sibling}, {"mp": opposite}, {"mp": across}]
    y_peer = {"dp": dp + 1 - 2 * y}
    z_places = [(z + m) % 4 for m in (1, 2, 3)]
    z_peers = [{"dp": place * 2 + y} for place in z_places]
    return mp, y, z, mp_peers, y_peer, z_places, z_peers


def greet(peers):
    barrier = pltpu.get_barrier_semaphore()
    for peer in peers:
        pl.semaphore_signal(barrier, inc=1, device_id=peer, device_id_type=MESH)
    pl.semaphore_wait(barrier, len(peers))


def remote(source, target, send, recv, peer):
    return pltpu.make_async_remote_copy(
        src_ref=source,
        dst_ref=target,
        send_sem=send,
        recv_sem=recv,
        device_id=peer,
        device_id_type=MESH,
    )


def loop(count, body):
    def step(i, carry):
        body(i)
        return carry

    lax.fori_loop(0, count, step, 0)


def block_rows(i, size):
    return pl.ds(pl.multiple_of(i * size, size), size)


def start_all(copies):
    for copy in copies:
        copy.start()


def wait_recv_all(copies):
    for copy in copies:
        copy.wait_recv()


def item_of_rows(row, lengths, mp):
    window = row >> 8
    offset = row & (WINDOW - 1)
    length = jnp.where(window == 0, lengths[4 * mp], lengths[4 * mp + 2])
    second = jnp.where(offset >= length, 1, 0)
    in_pair = (window < 2) & (offset < PAIR_LEN)
    is_padding = (window == 2) & (offset < PADDING) & (mp == 3)
    return 2 * window + second, offset - second * length, in_pair, is_padding


def owner_of_rows(row, lengths, mp):
    item, _, in_pair, is_padding = item_of_rows(row, lengths, mp)
    return jnp.where(in_pair, item, jnp.where(is_padding, 16, -1))


def choose_item(item, values):
    result = jnp.where(item == 0, values[0], 0.0)
    for j in (1, 2, 3):
        result = jnp.where(item == j, values[j], result)
    return result


def joined(tiles, first):
    return jnp.concatenate([tiles[first + j : first + j + 1, :] for j in range(8)], axis=1)


def forward_kernel(
    lengths,
    groups,
    counts,
    scales,
    gain,
    shift,
    output_bias,
    hidden_gain,
    hidden_shift,
    query_bias,
    value_bias,
    up_bias,
    tokens_ref,
    cotangent_ref,
    query_ref,
    key_ref,
    value_ref,
    output_ref,
    up_ref,
    down_ref,
    tokens_out,
    cotangent_out,
    sums_out,
    stream_out,
    middle_out,
    normed_out,
    qkv_out,
    context_out,
    hidden_out,
    grad_mixed_out,
    active_out,
    grad_pre_out,
    wqkv_out,
    wo_out,
    wup_out,
    wdown_out,
    tokens_ext,
    cotangent_ext,
    tokens,
    cotangent,
    stream,
    middle,
    normed,
    qkv,
    context,
    hidden,
    grad_mixed,
    active,
    grad_pre,
    wqkv,
    wo,
    wup,
    wdown,
    sums,
    bias,
    part,
    from_mp,
    from_y,
    from_z,
    own_sem,
    halo_sem,
    store_sem,
    stat_send,
    stat_recv,
    bias_send,
    bias_recv,
    pair_send,
    pair_recv,
    x_send,
    x_recv,
    z_send,
    z_recv,
    y_send,
    y_recv,
    fwd_send,
    fwd_recv,
):
    mp, y, z, mp_peers, y_peer, z_places, z_peers = places()
    sibling, opposite, _ = mp_peers
    rows_here = tokens_ref.shape[0]
    rows = tokens.shape[0]
    width = query_ref.shape[1]
    blocks = rows // 32

    items = [
        (key_ref, 0, D, wqkv, width, width, False),
        (value_ref, 0, D, wqkv, 2 * width, width, False),
        (query_ref, 0, D, wqkv, 0, width, True),
        (output_ref, 0, width, wo, 0, D, False),
        (up_ref, 0, D // 2, wup, 0, D, False),
        (up_ref, D // 2, D // 2, wup, 0, D, False),
        (down_ref, 3 * D // 4, D // 4, wdown, 0, D, False),
        (down_ref, 0, 3 * D // 4, wdown, 0, D, True),
    ]
    KEY, VALUE, QUERY, OUTPUT, UP_A, UP_B, DOWN_A, DOWN_B = range(8)

    def source(i, start, size):
        return items[i][0].at[pl.ds(items[i][1] + start, size)]

    def place(i, r, start, size):
        _, first, _, ref, column, columns, _ = items[i]
        return ref.at[r, pl.ds(first + start, size), pl.ds(column, columns)]

    def part_of(i, first, eighths):
        size = items[i][2] // 8
        return pl.multiple_of(first * size, size), eighths * size

    own_copies = [
        pltpu.make_async_copy(
            source(i, 0, items[i][2]), place(i, 0, 0, items[i][2]), own_sem.at[i]
        )
        for i in range(8)
    ]
    pair_copies = [
        remote(
            source(i, 0, items[i][2]),
            place(i, 1, 0, items[i][2]),
            pair_send.at[i],
            pair_recv.at[i],
            sibling,
        )
        for i in range(8)
    ]

    def x_copy(i):
        start, size = (0, items[i][2]) if items[i][6] else part_of(i, y * 4 + z, 1)
        return remote(
            source(i, start, size), place(i, 2, start, size), x_send.at[i], x_recv.at[i], opposite
        )

    def z_copies(i):
        start, size = part_of(i, y * 4 + z, 1)
        view = place(i, 2, start, size)
        return [
            remote(view, view, z_send.at[i, m], z_recv.at[i, m], peer)
            for m, peer in enumerate(z_peers)
        ]

    def y_copy(i):
        start, size = part_of(i, y * 4, 4)
        view = place(i, 2, start, size)
        return remote(view, view, y_send.at[i], y_recv.at[i], y_peer)

    def fwd_copy(i):
        size = items[i][2]
        return remote(
            place(i, 2, 0, size), place(i, 3, 0, size), fwd_send.at[i], fwd_recv.at[i], sibling
        )

    def x_to_z(i):
        x_copy(i).wait_recv()
        start_all(z_copies(i))

    def z_to_y(i):
        wait_recv_all(z_copies(i))
        y_copy(i).start()

    def y_to_pair(i):
        (x_copy(i) if items[i][6] else y_copy(i)).wait_recv()
        fwd_copy(i).start()

    keep = [
        pltpu.make_async_copy(ref, ext.at[pl.ds(HALO, rows_here)], halo_sem.at[which, 2])
        for which, (ref, ext) in enumerate(
            ((tokens_ref, tokens_ext), (cotangent_ref, cotangent_ext))
        )
    ]
    start_all(keep)
    start_all(own_copies)
    bias[0, 0:1, :] = query_bias[...]
    bias[0, 1:2, :] = value_bias[...]
    for j in range(4):
        bias[0, 2 + j : 3 + j, :] = up_bias[:, j * width : (j + 1) * width]
    bias[0, 6:8, :] = jnp.zeros((2, width), F32)

    weights = [counts[groups[4 * mp + j]].astype(F32) for j in range(4)]
    weight_part = weights[0] + weights[1] + weights[2] + weights[3]
    keep[0].wait()

    def add_rows(i, carry):
        block = tokens_ext[pl.ds(pl.multiple_of(HALO + i * 16, 16), 16), :].astype(F32)
        row = mp * rows_here + i * 16 + lax.broadcasted_iota(jnp.int32, (16, 1), 0)
        kept = jnp.where(row < PAIRS * PAIR_LEN, block, 0.0)
        return carry[0] + kept, carry[1] + kept * block

    zero = jnp.zeros((16, D), F32)
    first, second = lax.fori_loop(0, rows_here // 16, add_rows, (zero, zero))
    first = jnp.sum(first, axis=0, keepdims=True)
    second = jnp.sum(second, axis=0, keepdims=True)
    for j in range(8):
        part[0, j : j + 1, :] = first[:, j * 128 : (j + 1) * 128]
        part[0, 8 + j : 9 + j, :] = second[:, j * 128 : (j + 1) * 128]
    part[0, 16:24, :] = jnp.zeros((8, 128), F32) + weight_part
    greet(mp_peers + [y_peer] + z_peers)

    def exchange(stage, peers, slots):
        copies = [
            remote(
                part.at[stage],
                slots.at[m],
                stat_send.at[stage, m],
                stat_recv.at[stage, m],
                peer,
            )
            for m, peer in enumerate(peers)
        ]
        start_all(copies)
        return copies

    def total(stage, copies, slots):
        value = part[stage]
        for m, copy in enumerate(copies):
            copy.wait_recv()
            value = value + slots[m]
        return value

    sums_a = exchange(0, mp_peers, from_mp)
    after = {"mp": (mp + 1) % 4}
    halo_copies = [
        remote(
            ref.at[pl.ds(rows_here - HALO, HALO)],
            ext.at[pl.ds(0, HALO)],
            halo_sem.at[which, 0],
            halo_sem.at[which, 1],
            after,
        )
        for which, (ref, ext) in enumerate(
            ((tokens_ref, tokens_ext), (cotangent_ref, cotangent_ext))
        )
    ]
    bias_copies = [
        remote(bias.at[0], bias.at[r + 1], bias_send.at[r], bias_recv.at[r], peer)
        for r, peer in enumerate(mp_peers)
    ]
    start_all(halo_copies + bias_copies)
    start_all([x_copy(i) for i in range(8)])
    start_all([pair_copies[i] for i in (QUERY, KEY, VALUE, OUTPUT, UP_A, UP_B, DOWN_A, DOWN_B)])
    part[1] = total(0, sums_a, from_mp)
    sums_b = exchange(1, [y_peer], from_y)

    place_id = lax.broadcasted_iota(jnp.int32, (64, 1), 0)
    table_scale = choose_item(
        place_id >> 4, [scales[groups[4 * mp + j]] for j in range(4)]
    )
    quarter = D // 4
    lane = lax.broadcasted_iota(jnp.int32, (1, quarter), 1).astype(F32)
    frequency = jnp.exp(-math.log(10000.0) * lane / quarter)
    angle = ((place_id & 15).astype(F32) * table_scale) * frequency
    table = jnp.concatenate([jnp.sin(angle), jnp.cos(angle)], axis=1)
    row = lax.broadcasted_iota(jnp.int32, (rows, 64), 0)
    column = lax.broadcasted_iota(jnp.int32, (rows, 64), 1)
    item, position, in_pair, _ = item_of_rows(row, lengths, mp)
    across = (position * 9363) >> 17
    for half, code in enumerate((across, position - SIDE * across)):
        chosen = jnp.where(in_pair & (column == item * 16 + code), 1.0, 0.0)
        stream[:, half * 2 * quarter : (half + 1) * 2 * quarter] = lax.dot_general(
            chosen,
            table,
            (((1,), (0,)), ((), ())),
            precision=lax.Precision.HIGHEST,
            preferred_element_type=F32,
        )
    part[2] = total(1, sums_b, from_y)
    sums_c = exchange(2, z_peers, from_z)
    x_to_z(KEY)
    x_to_z(VALUE)

    wait_recv_all(halo_copies)
    keep[1].wait()
    own_len = 2 * PAIR_LEN
    row = lax.broadcasted_iota(jnp.int32, (rows, HALO + rows_here), 0)
    column = lax.broadcasted_iota(jnp.int32, (rows, HALO + rows_here), 1)
    window = row >> 8
    offset = row & (WINDOW - 1)
    wanted = HALO - (rows_here - own_len) * mp + window * PAIR_LEN + offset
    tail = jnp.where(mp == 3, HALO + rows_here - PADDING, 4096) + offset
    wanted = jnp.where(window < 2, jnp.where(offset < PAIR_LEN, wanted, -1), tail)
    chosen = jnp.where(column == wanted, 1.0, 0.0).astype(BF)
    tokens[...] = dot(chosen, tokens_ext[...]).astype(BF)
    cotangent[...] = dot(chosen, cotangent_ext[...]).astype(BF)
    sums[...] = total(2, sums_c, from_z)

    slices = lax.axis_size("dp")
    count_valid = slices * PAIRS * PAIR_LEN
    column_mean = joined(sums, 0) / count_valid
    spread = joined(sums, 8) / count_valid - column_mean * column_mean
    inverse = lax.rsqrt(spread + 1e-05)
    mean_weight = sums[16:17, 0:1] / (slices * 16)

    def first_norm(i):
        here = block_rows(i, 32)
        value = (tokens[here, :].astype(F32) - column_mean) * inverse + stream[here, :]
        stream[here, :] = value
        unit, _ = stats(value)
        normed[here, :] = (unit * gain[...] + shift[...]).astype(BF)
        row = i * 32 + lax.broadcasted_iota(jnp.int32, (32, 1), 0)
        item, _, in_pair, _ = item_of_rows(row, lengths, mp)
        row_weight = jnp.where(in_pair, choose_item(item, weights), 0.0) / mean_weight
        grad_mixed[here, :] = (cotangent[here, :].astype(F32) * row_weight).astype(BF)

    loop(blocks, first_norm)

    def store(i, value, ref):
        return pltpu.make_async_copy(value, ref, store_sem.at[i])

    stores = [
        store(0, tokens, tokens_out),
        store(1, cotangent, cotangent_out),
        store(2, sums, sums_out),
        store(3, stream, stream_out),
        store(4, normed, normed_out),
        store(5, grad_mixed, grad_mixed_out),
        store(6, qkv, qkv_out),
        store(7, context, context_out),
        store(8, wqkv, wqkv_out),
        store(9, middle, middle_out),
        store(10, hidden, hidden_out),
        store(11, wo, wo_out),
        store(12, active, active_out),
        store(13, grad_pre, grad_pre_out),
        store(14, wup, wup_out),
        store(15, wdown, wdown_out),
    ]
    start_all(stores[:6])

    for copy in bias_copies:
        copy.wait_recv()

    def head_group(r):
        @pl.when(r == 0)
        def _():
            for i in (QUERY, KEY, VALUE):
                own_copies[i].wait()

        @pl.when(r == 1)
        def _():
            for i in (OUTPUT, UP_A, UP_B, DOWN_A):
                x_to_z(i)
            for i in (QUERY, KEY, VALUE):
                pair_copies[i].wait_recv()

        @pl.when(r == 2)
        def _():
            for i in (QUERY, KEY, VALUE):
                y_to_pair(i)
            z_to_y(OUTPUT)

        @pl.when(r == 3)
        def _():
            for i in (QUERY, KEY, VALUE):
                fwd_copy(i).wait_recv()
            y_to_pair(OUTPUT)

        base = r * 3 * width
        for n in range(3):
            value = dot(normed[...], wqkv[r, :, n * width : (n + 1) * width])
            if n != 1:
                value = value + bias[r, n // 2 : n // 2 + 1, :]
            qkv[:, pl.ds(pl.multiple_of(base + n * width, width), width)] = value.astype(BF)

        @pl.when(r == 0)
        def _():
            z_to_y(KEY)
            z_to_y(VALUE)

        def head_pair(p):
            lanes = [
                pl.ds(pl.multiple_of(base + n * width + p * 128, 128), 128) for n in range(3)
            ]
            target = pl.ds(pl.multiple_of(r * width + p * 128, 128), 128)
            for first, size in blocks_of(rows):
                here = pl.ds(first, size)
                same = owner_of_rows(
                    first + lax.broadcasted_iota(jnp.int32, (size, 1), 0), lengths, mp
                ) == owner_of_rows(
                    first + lax.broadcasted_iota(jnp.int32, (1, size), 1), lengths, mp
                )
                q, k, v = [qkv[here, lane] for lane in lanes]
                results = []
                for h in range(2):
                    cut = slice(h * HEAD_DIM, (h + 1) * HEAD_DIM)
                    low = softmax_rows(q[:, cut], k[:, cut], same).astype(BF)
                    results.append(dot(low, v[:, cut]).astype(BF))
                context[here, target] = jnp.concatenate(results, axis=1)

        loop(width // 128, head_pair)

    loop(4, head_group)
    start_all(stores[6:9])
    z_to_y(UP_A)

    own_copies[OUTPUT].wait()
    pair_copies[OUTPUT].wait_recv()
    fwd_copy(OUTPUT).wait_recv()

    def attention_output(n):
        columns = block_rows(n, 256)
        value = stream[:, columns] + output_bias[:, columns]
        for r in range(4):
            value = value + dot(context[:, r * width : (r + 1) * width], wo[r, :, columns])
        middle[:, columns] = value

    loop(4, attention_output)

    def second_norm(i):
        here = block_rows(i, 32)
        unit, _ = stats(middle[here, :])
        hidden[here, :] = (unit * hidden_gain[...] + hidden_shift[...]).astype(BF)

    loop(blocks, second_norm)
    start_all(stores[9:12])

    def hidden_group(r):
        @pl.when(r == 0)
        def _():
            for i in (UP_A, UP_B, DOWN_A, DOWN_B):
                own_copies[i].wait()
            z_to_y(UP_B)

        @pl.when(r == 1)
        def _():
            y_to_pair(UP_A)
            z_to_y(DOWN_A)
            for i in (UP_A, UP_B, DOWN_A, DOWN_B):
                pair_copies[i].wait_recv()

        @pl.when(r == 2)
        def _():
            for i in (DOWN_B, UP_B, DOWN_A):
                y_to_pair(i)

        @pl.when(r == 3)
        def _():
            for i in (UP_A, UP_B, DOWN_A, DOWN_B):
                fwd_copy(i).wait_recv()

        def hidden_tile(n):
            columns = block_rows(n, 256)
            target = pl.ds(pl.multiple_of(r * D + n * 256, 256), 256)
            preact = dot(hidden[...], wup[r, :, columns]) + bias[r, pl.ds(2 + n, 1), :]
            value, slope = gelu_parts(preact)
            active[:, target] = value
            grad = dot_cols(grad_mixed[...], wdown[r, columns, :])
            grad_pre[:, target] = (grad * slope).astype(BF)

        loop(4, hidden_tile)

    loop(4, hidden_group)
    start_all(stores[12:])

    for i in range(8):
        pair_copies[i].wait_send()
        x_copy(i).wait_send()
        fwd_copy(i).wait_send()
        if not items[i][6]:
            for copy in z_copies(i):
                copy.wait_send()
            y_copy(i).wait_send()
    for copy in bias_copies + halo_copies + sums_a + sums_b + sums_c:
        copy.wait_send()
    for copy in stores:
        copy.wait()


def softmax_rows(q, k, same):
    scores = jnp.where(same, dot_cols(q, k) * (1.0 / math.sqrt(HEAD_DIM)), -1e30)
    weights = jnp.exp(scores - jnp.max(scores, axis=-1, keepdims=True))
    return weights * (1.0 / jnp.sum(weights, axis=-1, keepdims=True))


def forward(smalls, vectors, tokens, cotangent, weights, rows):
    width = weights[0].shape[1]
    shape = jax.ShapeDtypeStruct
    full = shape((rows, D), F32)
    low = shape((rows, D), BF)
    wide = shape((rows, 4 * D), BF)
    outs = (
        low,
        low,
        shape((24, 128), F32),
        full,
        full,
        low,
        shape((rows, 12 * width), BF),
        low,
        low,
        low,
        wide,
        wide,
        shape((4, D, 3 * width), BF),
        shape((4, width, D), BF),
        shape((4, D, D), BF),
        shape((4, D, D), BF),
    )
    scratch = [shape((HALO + tokens.shape[0], D), BF)] * 2 + [
        low,
        low,
        full,
        full,
        low,
        outs[6],
        low,
        low,
        low,
        wide,
        wide,
    ]
    scratch += list(outs[12:]) + [
        shape((24, 128), F32),
        shape((4, 8, width), F32),
        shape((3, 24, 128), F32),
        shape((3, 24, 128), F32),
        shape((1, 24, 128), F32),
        shape((3, 24, 128), F32),
    ]
    dma = pltpu.SemaphoreType.DMA
    any_space = pl.BlockSpec(memory_space=pl.ANY)
    return pl.pallas_call(
        forward_kernel,
        out_shape=outs,
        in_specs=[pl.BlockSpec(memory_space=pltpu.SMEM)] * 4
        + [pl.BlockSpec(memory_space=pltpu.VMEM)] * 8
        + [any_space] * 8,
        out_specs=(any_space,) * len(outs),
        scratch_shapes=[pltpu.VMEM(v.shape, v.dtype) for v in scratch]
        + [
            dma((8,)),
            dma((2, 3)),
            dma((16,)),
            dma((3, 3)),
            dma((3, 3)),
            dma((3,)),
            dma((3,)),
            dma((8,)),
            dma((8,)),
            dma((8,)),
            dma((8,)),
            dma((8, 3)),
            dma((8, 3)),
            dma((8,)),
            dma((8,)),
            dma((8,)),
            dma((8,)),
        ],
        compiler_params=pltpu.CompilerParams(
            collective_id=1, has_side_effects=True, vmem_limit_bytes=67043328
        ),
        name="forward",
    )(*smalls, *vectors, tokens, cotangent, *weights)


CHUNK = 256
STAGE_DELAY = (0, 1, 3, 5, 7, 9, 11)


def gradient_kernel(
    active_ref,
    grad_mixed_ref,
    hidden_ref,
    grad_pre_ref,
    context_ref,
    grad_attended_ref,
    grad_qkv_ref,
    normed_ref,
    out_ref,
    active,
    grad_mixed,
    hidden,
    grad_pre,
    context,
    grad_attended,
    grad_qkv,
    normed,
    made,
    pair,
    across,
    over_y,
    over_z,
    final,
    load_sem,
    pair_send,
    pair_recv,
    across_send,
    across_recv,
    y_send,
    y_recv,
    z_send,
    z_recv,
    back_z_send,
    back_z_recv,
    back_y_send,
    back_y_recv,
    out_sem,
):
    mp = lax.axis_index("mp")
    dp = lax.axis_index("dp")
    y = dp % 2
    z = dp // 2
    sibling = {"mp": mp + 1 - 2 * (mp % 2)}
    opposite = {"mp": mp + 2 - 4 * (mp // 2)}
    y_peer = {"dp": dp + 1 - 2 * y}
    z_places = [(z + m) % 4 for m in (1, 2, 3)]
    z_peers = [{"dp": place * 2 + y} for place in z_places]
    half = CHUNK // 2
    eighth = CHUNK // 8
    chunks = final.shape[0]
    width = final.shape[2]

    loads = [
        pltpu.make_async_copy(source, target, load_sem.at[i])
        for i, (source, target) in enumerate(
            (
                (active_ref, active),
                (grad_mixed_ref, grad_mixed),
                (hidden_ref, hidden),
                (grad_pre_ref, grad_pre),
                (context_ref, context),
                (grad_attended_ref, grad_attended),
                (grad_qkv_ref, grad_qkv),
                (normed_ref, normed),
            )
        )
    ]
    for load in loads:
        load.start()
    barrier = pltpu.get_barrier_semaphore()
    for peer in [sibling, opposite, y_peer] + z_peers:
        pl.semaphore_signal(barrier, inc=1, device_id=peer, device_id_type=MESH)
    pl.semaphore_wait(barrier, 6)

    def pair_copy(c):
        return pltpu.make_async_remote_copy(
            src_ref=made.at[c % 2, pl.ds(0, 2)],
            dst_ref=pair.at[c],
            send_sem=pair_send.at[c],
            recv_sem=pair_recv.at[c],
            device_id=sibling,
            device_id_type=MESH,
        )

    def across_copy(c):
        return pltpu.make_async_remote_copy(
            src_ref=pair.at[c, 1],
            dst_ref=across.at[c],
            send_sem=across_send.at[c],
            recv_sem=across_recv.at[c],
            device_id=opposite,
            device_id_type=MESH,
        )

    def y_copy(c):
        return pltpu.make_async_remote_copy(
            src_ref=across.at[c, pl.ds(pl.multiple_of((1 - y) * half, half), half)],
            dst_ref=over_y.at[c],
            send_sem=y_send.at[c],
            recv_sem=y_recv.at[c],
            device_id=y_peer,
            device_id_type=MESH,
        )

    def z_copies(c):
        return [
            pltpu.make_async_remote_copy(
                src_ref=over_y.at[c, pl.ds(pl.multiple_of(place * eighth, eighth), eighth)],
                dst_ref=over_z.at[c, m],
                send_sem=z_send.at[c, m],
                recv_sem=z_recv.at[c, m],
                device_id=peer,
                device_id_type=MESH,
            )
            for m, (place, peer) in enumerate(zip(z_places, z_peers))
        ]

    def back_z_copies(c):
        rows = pl.ds(pl.multiple_of(y * half + z * eighth, eighth), eighth)
        return [
            pltpu.make_async_remote_copy(
                src_ref=final.at[c, rows],
                dst_ref=final.at[c, rows],
                send_sem=back_z_send.at[c, m],
                recv_sem=back_z_recv.at[c, m],
                device_id=peer,
                device_id_type=MESH,
            )
            for m, peer in enumerate(z_peers)
        ]

    def back_y_copy(c):
        rows = pl.ds(pl.multiple_of(y * half, half), half)
        return pltpu.make_async_remote_copy(
            src_ref=final.at[c, rows],
            dst_ref=final.at[c, rows],
            send_sem=back_y_send.at[c],
            recv_sem=back_y_recv.at[c],
            device_id=y_peer,
            device_id_type=MESH,
        )

    def out_copy(c):
        return pltpu.make_async_copy(final.at[c], out_ref.at[c], out_sem.at[c])

    def block_loop(count, body):
        def step(i, carry):
            body(pl.ds(pl.multiple_of(i * eighth, eighth), eighth))
            return carry

        lax.fori_loop(0, count, step, 0)

    def make(c):
        def part(j, carry):
            r = 2 * j + 1 - 5 * (j // 2)

            def store(left, right):
                made[c % 2, j] = dot_rows(left, right).astype(BF)

            @pl.when(c < 4)
            def _():
                left = active[:, pl.ds(pl.multiple_of((r * 4 + c) * CHUNK, CHUNK), CHUNK)]
                store(left, grad_mixed[...])

            @pl.when((c >= 4) & (c < 8))
            def _():
                left = hidden[:, pl.ds(pl.multiple_of((c - 4) * CHUNK, CHUNK), CHUNK)]
                store(left, grad_pre[:, pl.ds(pl.multiple_of(r * width, width), width)])

            @pl.when(c == 8)
            def _():
                left = context[:, pl.ds(pl.multiple_of(r * CHUNK, CHUNK), CHUNK)]
                store(left, grad_attended[...])

            @pl.when(c > 8)
            def _():
                left = grad_qkv[:, pl.ds(pl.multiple_of((r * 3 + c - 9) * CHUNK, CHUNK), CHUNK)]
                store(left, normed[...])

            return carry

        lax.fori_loop(0, 4, part, 0)

    def add_pair(c):
        pair_copy(c).wait_recv()
        pair_copy(c).wait_send()

        def body(rows):
            for which in (1, 0):
                pair[c, which, rows, :] = (
                    pair[c, which, rows, :].astype(F32)
                    + made[c % 2, 2 + which, rows, :].astype(F32)
                ).astype(BF)

        block_loop(8, body)

    def add_across(c):
        across_copy(c).wait_recv()

        def body(rows):
            across[c, rows, :] = (
                across[c, rows, :].astype(F32) + pair[c, 0, rows, :].astype(F32)
            ).astype(BF)

        block_loop(8, body)

    def add_y(c):
        y_copy(c).wait_recv()

        def step(i, carry):
            rows = pl.ds(pl.multiple_of(i * eighth, eighth), eighth)
            own = pl.ds(pl.multiple_of(y * half + i * eighth, eighth), eighth)
            over_y[c, rows, :] = (
                over_y[c, rows, :].astype(F32) + across[c, own, :].astype(F32)
            ).astype(BF)
            return carry

        lax.fori_loop(0, 4, step, 0)

    def add_z(c):
        for copy in z_copies(c):
            copy.wait_recv()
        total = over_y[c, pl.ds(pl.multiple_of(z * eighth, eighth), eighth), :].astype(F32)
        for m in range(3):
            total = total + over_z[c, m].astype(F32)
        final[c, pl.ds(pl.multiple_of(y * half + z * eighth, eighth), eighth), :] = total.astype(BF)

    def wait_back_z(c):
        for copy in back_z_copies(c):
            copy.wait_recv()

    def wait_back_y(c):
        back_y_copy(c).wait_recv()

    def start_all(copies):
        for copy in copies:
            copy.start()

    handle = (make, add_pair, add_across, add_y, add_z, wait_back_z, wait_back_y)
    send = (
        lambda c: [pair_copy(c)],
        lambda c: [across_copy(c)],
        lambda c: [y_copy(c)],
        z_copies,
        back_z_copies,
        lambda c: [back_y_copy(c)],
        lambda c: [out_copy(c)],
    )

    def tick(k, carry):
        for when, count in ((0, 2), (4, 2), (8, 2), (9, 2)):
            first = {0: 0, 4: 2, 8: 4, 9: 6}[when]

            @pl.when(k == when)
            def _(first=first, count=count):
                for load in loads[first : first + count]:
                    load.wait()

        for stage in (6, 5, 4, 3, 2, 0, 1):
            c = k - STAGE_DELAY[stage]

            @pl.when((c >= 0) & (c < chunks))
            def _(stage=stage, c=c):
                handle[stage](c)

        for stage in (1, 2, 3, 4, 5, 0, 6):
            c = k - STAGE_DELAY[stage]

            @pl.when((c >= 0) & (c < chunks))
            def _(stage=stage, c=c):
                start_all(send[stage](c))

        return carry

    lax.fori_loop(0, chunks + STAGE_DELAY[-1], tick, 0)

    def finish(c, carry):
        across_copy(c).wait_send()
        y_copy(c).wait_send()
        for copy in z_copies(c) + back_z_copies(c):
            copy.wait_send()
        back_y_copy(c).wait_send()
        out_copy(c).wait()
        return carry

    lax.fori_loop(0, chunks, finish, 0)


def reduce_gradients(*inputs):
    chunks = 12
    return pl.pallas_call(
        gradient_kernel,
        out_shape=jax.ShapeDtypeStruct((chunks, CHUNK, D), BF),
        in_specs=[pl.BlockSpec(memory_space=pl.ANY)] * 8,
        out_specs=pl.BlockSpec(memory_space=pl.ANY),
        scratch_shapes=[pltpu.VMEM(v.shape, v.dtype) for v in inputs]
        + [
            pltpu.VMEM((2, 4, CHUNK, D), BF),
            pltpu.VMEM((chunks, 2, CHUNK, D), BF),
            pltpu.VMEM((chunks, CHUNK, D), BF),
            pltpu.VMEM((chunks, CHUNK // 2, D), BF),
            pltpu.VMEM((chunks, 3, CHUNK // 8, D), BF),
            pltpu.VMEM((chunks, CHUNK, D), BF),
            pltpu.SemaphoreType.DMA((8,)),
            pltpu.SemaphoreType.DMA((chunks,)),
            pltpu.SemaphoreType.DMA((chunks,)),
            pltpu.SemaphoreType.DMA((chunks,)),
            pltpu.SemaphoreType.DMA((chunks,)),
            pltpu.SemaphoreType.DMA((chunks,)),
            pltpu.SemaphoreType.DMA((chunks,)),
            pltpu.SemaphoreType.DMA((chunks, 3)),
            pltpu.SemaphoreType.DMA((chunks, 3)),
            pltpu.SemaphoreType.DMA((chunks, 3)),
            pltpu.SemaphoreType.DMA((chunks, 3)),
            pltpu.SemaphoreType.DMA((chunks,)),
            pltpu.SemaphoreType.DMA((chunks,)),
            pltpu.SemaphoreType.DMA((chunks,)),
        ],
        compiler_params=pltpu.CompilerParams(
            collective_id=0, has_side_effects=True, vmem_limit_bytes=67043328
        ),
        name="reduce_gradients",
    )(*inputs)


def general_shards(
    tokens,
    cotangent,
    item_lengths,
    item_group,
    group_count,
    grid_scale,
    norm_gain,
    norm_shift,
    query_weight,
    query_bias,
    key_weight,
    value_weight,
    value_bias,
    output_weight,
    output_bias,
    hidden_gain,
    hidden_shift,
    up_weight,
    up_bias,
    down_weight,
    down_bias,
):
    shard_count = lax.axis_size("mp")
    slice_count = lax.axis_size("dp")
    mp = lax.axis_index("mp")
    rows_here = tokens.shape[0]
    item_count = item_lengths.shape[0]
    pairs_here = PAIRS // shard_count
    own_rows = pairs_here * PAIR_LEN
    shift = rows_here - own_rows
    halo = shift * (shard_count - 1)
    padding = rows_here * shard_count - PAIRS * PAIR_LEN
    tail_block = -(-padding // 32) * 32
    rows = pairs_here * WINDOW + tail_block
    is_last = mp == shard_count - 1

    width = query_weight.shape[1]
    qkv_own = jnp.concatenate([query_weight, key_weight, value_weight], axis=1)
    bias_own = jnp.concatenate([query_bias, value_bias, up_bias])[None, :]
    bias_across = swap_mp(bias_own, 2)
    bias_pair = swap_mp(jnp.concatenate([bias_own, bias_across], axis=0), 1)
    biases = [bias_own[0], bias_pair[0], bias_across[0], bias_pair[1]]

    def gather(own, direct):
        across = swap_mp(own, 2) if direct else fetch_across(own)
        return [own, swap_mp(own, 1), across, swap_mp(across, 1)]

    tokens_f = tokens.astype(F32)
    slice_row = mp * rows_here + jnp.arange(rows_here, dtype=jnp.int32)
    weighted = tokens_f * (slice_row < PAIRS * PAIR_LEN).astype(F32)[:, None]
    chosen = item_group[:, None] == jnp.arange(group_count.shape[0], dtype=jnp.int32)[None, :]
    item_scale = jnp.sum(jnp.where(chosen, grid_scale[None, :], 0.0), axis=1)
    item_weight = jnp.sum(jnp.where(chosen, group_count[None, :], 0), axis=1).astype(F32)
    sums = all_sum(
        jnp.stack(
            [
                jnp.sum(weighted, axis=0),
                jnp.sum(weighted * tokens_f, axis=0),
                jnp.broadcast_to(jnp.sum(item_weight) / shard_count, (D,)),
            ]
        )
    )

    def windows(v):
        before = lax.ppermute(
            v[rows_here - halo :], "mp", [(i, i + 1) for i in range(shard_count - 1)]
        )
        joined = jnp.concatenate([before, v], axis=0)
        start = halo - shift * mp
        parts = []
        for pair in range(pairs_here):
            parts.append(
                lax.dynamic_slice_in_dim(joined, start + pair * PAIR_LEN, PAIR_LEN, axis=0)
            )
            parts.append(jnp.zeros((WINDOW - PAIR_LEN, D), v.dtype))
        parts.append(jnp.where(is_last, v[rows_here - padding :], jnp.zeros((), v.dtype)))
        parts.append(jnp.zeros((tail_block - padding, D), v.dtype))
        return jnp.concatenate(parts, axis=0)

    def unwindows(v):
        own = jnp.concatenate(
            [v[pair * WINDOW : pair * WINDOW + PAIR_LEN] for pair in range(pairs_here)], axis=0
        )
        after = lax.ppermute(own[:halo], "mp", [(i + 1, i) for i in range(shard_count - 1)])
        after = jnp.concatenate([after, jnp.zeros((padding - halo, D), v.dtype)], axis=0)
        tail = v[pairs_here * WINDOW : pairs_here * WINDOW + padding]
        joined = jnp.concatenate([own, jnp.where(is_last, tail, after)], axis=0)
        return lax.dynamic_slice_in_dim(joined, shift * mp, rows_here, axis=0)

    tokens_w = windows(tokens).astype(F32)
    cotangent_w = windows(cotangent).astype(F32)

    row = jnp.arange(rows, dtype=jnp.int32)
    window = row // WINDOW
    offset = row % WINDOW
    in_pair = (window < pairs_here) & (offset < PAIR_LEN)
    is_padding = (window == pairs_here) & (offset < padding) & is_last
    pair = pairs_here * mp + window
    item_ids = jnp.arange(item_count, dtype=jnp.int32)
    first_len = jnp.sum(
        jnp.where(item_ids[None, :] == (2 * pair)[:, None], item_lengths[None, :], 0), axis=1
    )
    second = (offset >= first_len).astype(jnp.int32)
    owner = jnp.where(in_pair, 2 * pair + second, jnp.where(is_padding, item_count, -1))
    position = offset - second * first_len
    member = owner[:, None] == item_ids[None, :]
    row_scale = jnp.sum(jnp.where(member, item_scale[None, :], 0.0), axis=1)
    row_count = jnp.sum(jnp.where(member, item_weight[None, :], 0.0), axis=1)
    valid = in_pair.astype(F32)[:, None]
    quarter = D // 4
    frequency = jnp.exp(-math.log(10000.0) * jnp.arange(quarter, dtype=F32) / quarter)
    across_angle = ((position // SIDE).astype(F32) * row_scale)[:, None] * frequency
    side_angle = ((position % SIDE).astype(F32) * row_scale)[:, None] * frequency
    grid_table = (
        jnp.concatenate(
            [
                jnp.sin(across_angle),
                jnp.cos(across_angle),
                jnp.sin(side_angle),
                jnp.cos(side_angle),
            ],
            axis=-1,
        )
        * valid
    )
    owner_col = owner[:, None]
    owner_row = owner[None, :]

    qkv_weights = jnp.concatenate(gather(qkv_own, True), axis=1)
    output_weights = jnp.concatenate(gather(output_weight, False), axis=0)
    up_weights = jnp.concatenate(gather(up_weight, False), axis=1)
    down_weights = jnp.concatenate(gather(down_weight, False), axis=0)
    hidden_width = up_weight.shape[1]
    no_bias = jnp.zeros((width,), F32)
    qkv_bias = jnp.concatenate(
        [v for b in biases for v in (b[:width], no_bias, b[width : 2 * width])]
    )
    up_biases = jnp.concatenate([b[2 * width :] for b in biases])

    count_valid = slice_count * PAIRS * PAIR_LEN
    column_mean = sums[0] / count_valid
    spread = sums[1] / count_valid - column_mean * column_mean
    inverse = lax.rsqrt(spread + 1e-05)
    row_weight = row_count / (sums[2, 0] / (slice_count * item_count))
    standard = (tokens_w - column_mean) * inverse
    stream = standard + grid_table
    unit, unit_inverse = stats(stream)
    normed = (unit * norm_gain + norm_shift).astype(BF)

    qkv = (dot(normed, qkv_weights) + qkv_bias).astype(BF)
    context = attend(qkv, owner_col, owner_row, shard_count)
    middle = stream + (dot(context, output_weights) + output_bias)
    middle_unit, middle_inverse = stats(middle)
    hidden_in = (middle_unit * hidden_gain + hidden_shift).astype(BF)

    grad_out = cotangent_w * row_weight[:, None]
    grad_mixed = grad_out.astype(BF)
    active, slope = gelu_parts(dot(hidden_in, up_weights) + up_biases)
    mixed = dot(active, down_weights) + down_bias
    grad_pre = (dot_cols(grad_mixed, down_weights) * slope).astype(BF)
    grad_hidden = dot_cols(grad_pre, up_weights)
    layer_output = unwindows((middle + mixed).astype(BF))
    grad_middle = grad_out + norm_back(grad_hidden, middle_unit, middle_inverse, hidden_gain)
    grad_attended = grad_middle.astype(BF)

    grad_context = dot_cols(grad_attended, output_weights).astype(BF)
    grad_qkv = attend_back(qkv, grad_context, owner_col, owner_row, shard_count)
    grad_normed = dot_cols(grad_qkv, qkv_weights)

    pieces = range(shard_count)
    def columns(v, r, size):
        return v[:, r * size : (r + 1) * size]

    def reduced(left, right):
        return reduce_pieces([dot_rows(left(r), right(r)).astype(BF) for r in pieces])

    down_weight_grad = reduced(
        lambda r: columns(active, r, hidden_width), lambda r: grad_mixed
    )
    up_weight_grad = reduced(
        lambda r: hidden_in, lambda r: columns(grad_pre, r, hidden_width)
    )
    output_weight_grad = reduced(
        lambda r: columns(context, r, width), lambda r: grad_attended
    )
    qkv_weight_grad = reduced(lambda r: normed, lambda r: columns(grad_qkv, r, 3 * width))
    qkv_weight_grads = [columns(qkv_weight_grad, i, width) for i in range(3)]
    grad_stream = grad_middle + norm_back(grad_normed, unit, unit_inverse, norm_gain)

    def column_sums(v):
        return jnp.sum(v.astype(F32), axis=0)

    qkv_sums = column_sums(grad_qkv)
    up_sums = column_sums(grad_pre)
    bias_grads = [
        jnp.concatenate(
            [
                qkv_sums[3 * r * width : (3 * r + 1) * width],
                qkv_sums[(3 * r + 2) * width : 3 * (r + 1) * width],
                up_sums[r * hidden_width : (r + 1) * hidden_width],
            ]
        )[None, :]
        for r in pieces
    ]
    got = swap_mp(jnp.concatenate([bias_grads[1], bias_grads[3]], axis=0), 1)
    bias_grad = bias_grads[0] + got[:1] + swap_mp(bias_grads[2] + got[1:], 2)
    for bit in range(dp_bits()):
        bias_grad = bias_grad + swap_dp(bias_grad, 1 << bit)
    bias_grad = bias_grad[0]
    finals = all_sum(
        jnp.stack(
            [
                column_sums(grad_stream),
                column_sums(grad_stream * standard),
                column_sums(grad_normed * unit),
                column_sums(grad_normed),
                column_sums(grad_hidden * middle_unit),
                column_sums(grad_hidden),
                column_sums(grad_attended),
                column_sums(grad_mixed),
            ]
        )
    )
    tokens_grad = unwindows(
        inverse * (grad_stream - valid / count_valid * (finals[0] + finals[1] * standard))
    )
    return (
        layer_output,
        tokens_grad,
        finals[2],
        finals[3],
        qkv_weight_grads[0],
        bias_grad[:width],
        qkv_weight_grads[1],
        qkv_weight_grads[2],
        bias_grad[width : 2 * width],
        output_weight_grad,
        finals[6],
        finals[4],
        finals[5],
        up_weight_grad,
        bias_grad[2 * width :],
        down_weight_grad,
        finals[7],
    )


def fast_shards(
    tokens,
    cotangent,
    item_lengths,
    item_group,
    group_count,
    grid_scale,
    norm_gain,
    norm_shift,
    query_weight,
    query_bias,
    key_weight,
    value_weight,
    value_bias,
    output_weight,
    output_bias,
    hidden_gain,
    hidden_shift,
    up_weight,
    up_bias,
    down_weight,
    down_bias,
):
    shard_count = lax.axis_size("mp")
    slice_count = lax.axis_size("dp")
    mp = lax.axis_index("mp")
    rows_here = tokens.shape[0]
    item_count = item_lengths.shape[0]
    pairs_here = PAIRS // shard_count
    shift = rows_here - pairs_here * PAIR_LEN
    halo = shift * (shard_count - 1)
    padding = rows_here * shard_count - PAIRS * PAIR_LEN
    tail_block = -(-padding // 32) * 32
    rows = pairs_here * WINDOW + tail_block
    is_last = mp == shard_count - 1
    width = query_weight.shape[1]
    hidden_width = up_weight.shape[1]
    chosen = item_group[:, None] == jnp.arange(group_count.shape[0], dtype=jnp.int32)[None, :]
    item_scale = jnp.sum(jnp.where(chosen, grid_scale[None, :], 0.0), axis=1)
    item_weight = jnp.sum(jnp.where(chosen, group_count[None, :], 0), axis=1).astype(F32)

    def unwindows(v):
        own = jnp.concatenate(
            [v[pair * WINDOW : pair * WINDOW + PAIR_LEN] for pair in range(pairs_here)], axis=0
        )
        after = lax.ppermute(own[:halo], "mp", [(i + 1, i) for i in range(shard_count - 1)])
        after = jnp.concatenate([after, jnp.zeros((padding - halo, D), v.dtype)], axis=0)
        tail = v[pairs_here * WINDOW : pairs_here * WINDOW + padding]
        joined = jnp.concatenate([own, jnp.where(is_last, tail, after)], axis=0)
        return lax.dynamic_slice_in_dim(joined, shift * mp, rows_here, axis=0)

    (
        tokens_w,
        cotangent_w,
        sums,
        stream,
        middle,
        normed,
        qkv,
        context,
        hidden_in,
        grad_mixed,
        active,
        grad_pre,
        qkv_weights,
        output_weights,
        up_weights,
        down_weights,
    ) = forward(
        (item_lengths, item_group, group_count, grid_scale),
        [
            v[None, :]
            for v in (
                norm_gain,
                norm_shift,
                output_bias,
                hidden_gain,
                hidden_shift,
                query_bias,
                value_bias,
                up_bias,
            )
        ],
        tokens,
        cotangent,
        (query_weight, key_weight, value_weight, output_weight, up_weight, down_weight),
        rows,
    )
    tokens_w = tokens_w.astype(F32)
    sums = sums.reshape(3, D)
    row = jnp.arange(rows, dtype=jnp.int32)
    window = row // WINDOW
    offset = row % WINDOW
    in_pair = (window < pairs_here) & (offset < PAIR_LEN)
    is_padding = (window == pairs_here) & (offset < padding) & is_last
    pair = pairs_here * mp + window
    item_ids = jnp.arange(item_count, dtype=jnp.int32)
    first_len = jnp.sum(
        jnp.where(item_ids[None, :] == (2 * pair)[:, None], item_lengths[None, :], 0), axis=1
    )
    second = (offset >= first_len).astype(jnp.int32)
    owner = jnp.where(in_pair, 2 * pair + second, jnp.where(is_padding, item_count, -1))
    position = offset - second * first_len
    member = owner[:, None] == item_ids[None, :]
    row_scale = jnp.sum(jnp.where(member, item_scale[None, :], 0.0), axis=1)
    row_count = jnp.sum(jnp.where(member, item_weight[None, :], 0.0), axis=1)
    valid = in_pair.astype(F32)[:, None]
    count_valid = slice_count * PAIRS * PAIR_LEN
    column_mean = sums[0] / count_valid
    spread = sums[1] / count_valid - column_mean * column_mean
    inverse = lax.rsqrt(spread + 1e-05)
    row_weight = row_count / (sums[2, 0] / (slice_count * item_count))
    standard = (tokens_w - column_mean) * inverse
    unit, unit_inverse = stats(stream)
    middle_unit, middle_inverse = stats(middle)
    grad_out = cotangent_w.astype(F32) * row_weight[:, None]
    mixed = dot(active, down_weights.reshape(-1, D)) + down_bias
    layer_output = unwindows((middle + mixed).astype(BF))
    pieces = range(shard_count)

    def columns(v, r, size):
        return v[:, r * size : (r + 1) * size]

    grad_hidden = sum(dot_cols(columns(grad_pre, r, hidden_width), up_weights[r]) for r in pieces)
    grad_middle = grad_out + norm_back(grad_hidden, middle_unit, middle_inverse, hidden_gain)
    grad_attended = grad_middle.astype(BF)

    owner_col = owner[:, None]
    owner_row = owner[None, :]
    grad_context = dot_cols(grad_attended, output_weights.reshape(-1, D)).astype(BF)
    grad_qkv = attend_back(qkv, grad_context, owner_col, owner_row, shard_count)
    grad_normed = sum(dot_cols(columns(grad_qkv, r, 3 * width), qkv_weights[r]) for r in pieces)

    reduced = reduce_gradients(
        active,
        grad_mixed,
        hidden_in,
        grad_pre,
        context,
        grad_attended,
        grad_qkv,
        normed,
    )
    down_weight_grad = reduced[:4].reshape(hidden_width, D).astype(F32)
    up_weight_grad = reduced[4:8].reshape(D, hidden_width).astype(F32)
    output_weight_grad = reduced[8].astype(F32)
    qkv_weight_grads = [reduced[9 + i].T.astype(F32) for i in range(3)]
    grad_stream = grad_middle + norm_back(grad_normed, unit, unit_inverse, norm_gain)

    def column_sums(v):
        return jnp.sum(v.astype(F32), axis=0)

    qkv_sums = column_sums(grad_qkv)
    up_sums = column_sums(grad_pre)
    bias_grads = [
        jnp.concatenate(
            [
                qkv_sums[3 * r * width : (3 * r + 1) * width],
                qkv_sums[(3 * r + 2) * width : 3 * (r + 1) * width],
                up_sums[r * hidden_width : (r + 1) * hidden_width],
            ]
        )[None, :]
        for r in pieces
    ]
    got = swap_mp(jnp.concatenate([bias_grads[1], bias_grads[3]], axis=0), 1)
    bias_grad = bias_grads[0] + got[:1] + swap_mp(bias_grads[2] + got[1:], 2)
    for bit in range(dp_bits()):
        bias_grad = bias_grad + swap_dp(bias_grad, 1 << bit)
    bias_grad = bias_grad[0]
    finals = all_sum(
        jnp.stack(
            [
                column_sums(grad_stream),
                column_sums(grad_stream * standard),
                column_sums(grad_normed * unit),
                column_sums(grad_normed),
                column_sums(grad_hidden * middle_unit),
                column_sums(grad_hidden),
                column_sums(grad_attended),
                column_sums(grad_mixed),
            ]
        )
    )
    tokens_grad = unwindows(
        inverse * (grad_stream - valid / count_valid * (finals[0] + finals[1] * standard))
    )
    return (
        layer_output,
        tokens_grad,
        finals[2],
        finals[3],
        qkv_weight_grads[0],
        bias_grad[:width],
        qkv_weight_grads[1],
        qkv_weight_grads[2],
        bias_grad[width : 2 * width],
        output_weight_grad,
        finals[6],
        finals[4],
        finals[5],
        up_weight_grad,
        bias_grad[2 * width :],
        down_weight_grad,
        finals[7],
    )


def shards(*args):
    if lax.axis_size("dp") == 8 and lax.axis_size("mp") == 4 and args[0].shape == (512, D):
        return fast_shards(*args)
    return general_shards(*args)


def solution(mesh):
    rows = P(("dp", "mp"), None)
    columns = P(None, "mp")
    return jax.shard_map(
        shards,
        mesh=mesh,
        in_specs=(
            rows,
            rows,
            P("dp"),
            P("dp"),
            P(),
            P(),
            P(),
            P(),
            columns,
            P("mp"),
            columns,
            columns,
            P("mp"),
            P("mp", None),
            P(),
            P(),
            P(),
            columns,
            P("mp"),
            P("mp", None),
            P(),
        ),
        out_specs=(
            rows,
            rows,
            P(),
            P(),
            columns,
            P("mp"),
            columns,
            columns,
            P("mp"),
            P("mp", None),
            P(),
            P(),
            P(),
            columns,
            P("mp"),
            P("mp", None),
            P(),
        ),
        check_vma=False,
    )
```

time: 946 us -> 480 us (0.51)
  waiting for transfers between devices: 591 us -> 4.92 us
  Pallas kernels: 0 us -> 337 us
  blocking collectives: 107 us -> 0 us
  matrix products: 119 us -> 48.2 us
  other arithmetic: 62.7 us -> 38.3 us
  starting transfers between devices: 1.54 us -> 25.8 us
  local copies, waits for them, and re-layouts: 41.6 us -> 17.8 us
  between operations: 16.5 us -> 2.35 us
    psum x1 -> x0, waiting for transfers between devices: 350 us -> none  [shards(): lax.psum((query_weight_grad, query_bias_grad, key_weight_grad, value_weig...]
    pallas_call x0 -> x3, Pallas kernels: none -> 337 us  [the longest x1 207 us: reduce_gradients(): pl.pallas_call(gradient_kernel, out_shape=jax.ShapeDtypeStruct((chunks, C...]
    all_gather x4 -> x0, waiting for transfers between devices: 128 us -> none  [the longest x1 35 us: shards(): grad_attended_all = lax.all_gather(grad_attended, 'mp', axis=0, tiled=True)]
    reduce_scatter x4 -> x0, waiting for transfers between devices: 113 us -> none  [the longest x1 44.2 us: shards(): lax.psum_scatter(jnp.dot(context_low, output_weight, preferred_element_ty...]
    psum x3 -> x0, blocking collectives: 107 us -> none  [the longest x1 46.4 us: shards(): lax.psum((jnp.sum(grad_stream, axis=0), jnp.sum(grad_stream * standard, a...]
    dot_general x24 -> x10, matrix products: 119 us -> 48.2 us  [the longest x9 38.2 us: dot_cols(): lax.dot_general(a, b, (((1,), (1,)), ((), ())), preferred_element_type=F32)]
    ppermute x0 -> x14, starting transfers between devices: none -> 25.8 us  [the longest x2 13 us: unwindows(): lax.ppermute(own[:halo], 'mp', [(i + 1, i) for i in range(shard_count - 1)])]
    unnamed x184 -> x75, local copies, waits for them, and re-layouts: 27.7 us -> 8.99 us
  transfers between devices with their start and end apart: 9 -> 14, of which waited for: 8 -> 2; matrix products, arithmetic and copies ran while one was open for 8% -> 10% of each run, Pallas kernels for 0% -> 44%
where the time goes in v1:
time: 480 us; the launch traced here: 474 us
  Pallas kernels  337 us (70%)
  matrix products  48.2 us (10%)
  other arithmetic  38.3 us (8%)
  starting transfers between devices  25.8 us (5%)
  local copies, waits for them, and re-layouts  17.8 us (4%)
  waiting for transfers between devices  4.92 us (1%)
    pallas_call x1, Pallas kernels, reduce_gradients(): pl.pallas_call(gradient_kernel, out_shape=jax.ShapeDtypeStruct((chunks, C...  207 us
    pallas_call x1, Pallas kernels, forward(): pl.pallas_call(forward_kernel, out_shape=outs, in_specs=[pl.BlockSpec(mem...  101 us
    dot_general x9, matrix products, dot_cols(): lax.dot_general(a, b, (((1,), (1,)), ((), ())), preferred_element_type=F32)  38.2 us
    pallas_call x1, Pallas kernels, attend_back(): pl.pallas_call(attend_back_kernel, grid=(groups,), in_specs=[pl.BlockSpec...  28.7 us
    ppermute x2, starting transfers between devices, unwindows(): lax.ppermute(own[:halo], 'mp', [(i + 1, i) for i in range(shard_count - 1)])  13 us
    ppermute x7, starting transfers between devices, swap_dp(): return lax.ppermute(v, 'dp', [(i, i ^ mask) for i in range(count)])  10.6 us
    dot_general x1, matrix products, dot(): lax.dot_general(a, b, (((1,), (0,)), ((), ())), preferred_element_type=F32)  10 us
    reduce_sum x5, other arithmetic, column_sums(): return jnp.sum(v.astype(F32), axis=0)  9.7 us
  transfers between devices with their start and end apart: 14, of which 2 were waited for; matrix products, arithmetic and copies ran while one was open for 10% of the time, Pallas kernels for 44%

profile of v1, /device:TPU:1, one launch (start us, length us, event | category | flops | bytes accessed | tf_op | source)
XLA Modules:
  0.0 474.1 jit_solution(11635081725385887925)
XLA Ops:
  0.7 100.9 %forward.1 = (bf16[608,1024]{1,0:T(8,128)(2,1)}, bf16[608,1024]{1,0:T(8,128)(2,1)}, f32[24,128]{1,0:T(8,128)}, f32[608,1024]{1,0:T(8,128)}, f32[608,1024]{1,0:T(...) custom-call(s32[16]{0:T(128)} %lengths.1, ...), custom_call_target="tpu_custom_call" | custom-call | tf_op jit(solution)/shard_map/forward/pallas_call | solution.py:814
  102.9 5.1 %fusion.2 = f32[608,1024]{1,0:T(8,128)} fusion(bf16[4,1024,1024]{2,1,0:T(8,128)(2,1)} %get-tuple-element.39, bf16[608,4096]{1,0:T(8,128)(2,1)} %get-tuple-element.38.grad_pre_ref), kind=kOutput, calls=%fused_computation.29 | convolution fusion | flops 1275068416 | bytes 5832704 | tf_op jit(solution)/shard_map/dot_general | solution.py:31
  109.7 2.9 fusion.4
  112.7 3.0 fusion.6
  119.3 6.0 %multiply_reduce_fusion = (f32[1024]{0:T(1024)S(1)}, f32[608]{0:T(1024)S(1)}, f32[608]{0:T(1024)S(1)}, f32[1024]{0:T(1024)S(1)}, f32[608,1024]{1,0:T(8,128)S(1)}) fusion(f32[608,1024]{1,0:T(8,128)S(1)} %copy-done, f32[608]{0:T(1024)S(1)} %add_rsqrt_fusion.1, f32[608]{0:T(1024)S(1)} %broadcast_multiply_fusion.5, f32[1024]{0:T(1024)S(1)} %copy-done.21, ...), kind=kOutput, calls=%fused_computation.5 | convolution fusion | flops 1282536192 | bytes 15816192 | tf_op jit(solution)/shard_map/dot_general | solution.py:31
  126.0 2.3 convert_reduce_fusion.3
  128.3 2.5 convolution_convert_fusion.grad_ref
  130.9 28.7 %attend_back.1.grad_qkv_ref = bf16[608,3072]{1,0:T(8,128)(2,1)} custom-call(bf16[608,3072]{1,0:T(8,128)(2,1)} %get-tuple-element.41.qkv_ref, bf16[608,1024]{1,0:T(8,128)(2,1)} %convolution_convert_fusion.grad_ref, s32[608,1]{1,0:T(8,128)} %fusion.52.col_ref, s32[1,608]{1,0:T(1,128)} %and_select_fusion.1.row_ref), custom_call_target="tpu_custom_call" | custom-call | tf_op jit(solution)/shard_map/attend_back/pallas_call | solution.py:190
  159.6 4.4 fusion.15
  164.0 4.1 fusion.19
  168.1 4.1 fusion.17
  172.2 1.9 reduce_sum.200
  174.1 2.8 convert_reduce_fusion.2
  177.0 6.0 %multiply_reduce_fusion.1 = (f32[1024]{0:T(1024)S(1)}, f32[608]{0:T(1024)S(1)}, f32[608]{0:T(1024)S(1)}, f32[1024]{0:T(1024)S(1)}, f32[608,1024]{1,0:T(8,128)S(1)}) fusion(f32[608,1024]{1,0:T(8,128)S(1)} %copy-done.1, f32[608]{0:T(1024)S(1)} %add_rsqrt_fusion, f32[608]{0:T(1024)S(1)} %broadcast_multiply_fusion.2, f32[1024]{0:T(1024)S(1)} %copy-done.22, ...), kind=kOutput, calls=%fused_computation.6 | convolution fusion | flops 963769088 | bytes 14980608 | tf_op jit(solution)/shard_map/dot_general | solution.py:31
  183.1 2.7 multiply_reduce_fusion.2
  188.5 10.0 %add_convert_fusion = bf16[608,1024]{1,0:T(8,128)(2,1)S(1)} fusion(f32[608,1024]{1,0:T(8,128)S(1)} %copy-done, bf16[608,4096]{1,0:T(8,128)(2,1)} %get-tuple-element.34.active_ref, bf16[4096,1024]{1,0:T(8,128)(2,1)} %bitcast.127, f32[1024]{0:T(1024)S(1)} %copy-done.33), kind=kOutput, calls=%fused_computation.17 | convolution fusion | flops 5102141440 | bytes 17108992 | tf_op jit(solution)/shard_map/dot_general | solution.py:23
  200.3 2.2 collective-permute-start
  206.4 207.2 %reduce_gradients.1 = bf16[12,256,1024]{2,1,0:T(8,128)(2,1)} custom-call(bf16[608,4096]{1,0:T(8,128)(2,1)} %get-tuple-element.34.active_ref, bf16[608,1024]{1,0:T(8,128)(2,1)} %get-tuple-element.45.grad_mixed_ref, bf16[608,1024]{1,0:T(8,128)(2,1)} %get-tuple-element.46.hidden_ref, bf16[608,4096]{1,0:T(8,128)(2,1)} %get-tuple-element.38.grad_pre_ref, ...), custom_call_target="tpu_custom_call" | custom-call | tf_op jit(solution)/shard_map/reduce_gradients/pallas_call | solution.py:1143
  413.5 2.7 fusion.75
  416.2 2.6 bitcast_convert_fusion.1
  418.9 2.6 bitcast_convert_fusion
  422.4 2.4 collective-permute-done.10
  425.8 3.3 bitcast_convert_fusion.2
  429.2 3.3 collective-permute-start.12
  433.6 4.2 collective-permute-start.13
  439.2 2.3 collective-permute-start.6
  443.8 2.7 copy.47
  450.6 2.5 collective-permute-done.7
  453.7 2.0 subtract_multiply_fusion
  456.0 10.8 %collective-permute-start.8 = (f32[66,1024]{1,0:T(8,128)S(1)}, f32[66,1024]{1,0:T(8,128)S(1)}, u32[]{:S(2)}, u32[]{:S(2)}) collective-permute-start(f32[66,1024]{1,0:T(8,128)S(1)} %slice.262), channel_id=1, source_target_pairs={{1,0},{2,1},{3,2},{5,4},{6,5},{7,6},{9,8},{10,9},{11,10},{13,12},{... | collective-permute-start | bytes 811016 | tf_op jit(solution)/shard_map/ppermute | solution.py:1471
  467.9 3.0 fusion.32
  470.9 2.7 fusion.1
  (148 shorter events, 27.8 us)
Async XLA Ops:
  102.2 80.8 %copy-start.19 = (f32[1024]{0:T(1024)}, f32[1024]{0:T(1024)S(1)}, u32[]{:S(2)}) copy-start(f32[1024]{0:T(1024)S(1)} %multiply_bitcast_fusion) | copy-start | bytes 12292
  102.9 80.1 %copy-start.17 = (f32[1024]{0:T(1024)}, f32[1024]{0:T(1024)S(1)}, u32[]{:S(2)}) copy-start(f32[1024]{0:T(1024)S(1)} %fusion.71) | copy-start | bytes 12292
  102.9 5.1 %copy-start.4 = (bf16[608,4096]{1,0:T(8,128)(2,1)S(1)}, bf16[608,4096]{1,0:T(8,128)(2,1)}, u32[]{:S(2)}) copy-start(bf16[608,4096]{1,0:T(8,128)(2,1)} %get-tuple-element.38.grad_pre_ref) | copy-start | bytes 14942212
  102.9 6.8 %copy-start.15 = (bf16[4,1024,1024]{2,1,0:T(8,128)(2,1)S(1)}, bf16[4,1024,1024]{2,1,0:T(8,128)(2,1)}, u32[]{:S(2)}) copy-start(bf16[4,1024,1024]{2,1,0:T(8,128)(2,1)} %get-tuple-element.39) | copy-start | bytes 25165828
  112.7 4.7 copy-start
  119.3 6.7 %copy-start.14 = (bf16[608,1024]{1,0:T(8,128)(2,1)S(1)}, bf16[608,1024]{1,0:T(8,128)(2,1)}, u32[]{:S(2)}) copy-start(bf16[608,1024]{1,0:T(8,128)(2,1)} %get-tuple-element.37) | copy-start | bytes 3735556
  159.6 4.4 copy-start.2
  176.9 6.1 %copy-start.6 = (f32[608,1024]{1,0:T(8,128)S(1)}, f32[608,1024]{1,0:T(8,128)}, u32[]{:S(2)}) copy-start(f32[608,1024]{1,0:T(8,128)} %get-tuple-element.112) | copy-start | bytes 7471108
  176.9 6.1 %copy-start.7 = (bf16[608,1024]{1,0:T(8,128)(2,1)S(1)}, bf16[608,1024]{1,0:T(8,128)(2,1)}, u32[]{:S(2)}) copy-start(bf16[608,1024]{1,0:T(8,128)(2,1)} %get-tuple-element.44) | copy-start | bytes 3735556
  183.1 5.5 %copy-start.33 = (f32[1024]{0:T(1024)S(1)}, f32[1024]{0:T(1024)}, u32[]{:S(2)}) copy-start(f32[1024]{0:T(1024)} %param.41) | copy-start | bytes 12292
  186.4 251.4 %collective-permute-start.3 = (f32[8,1024]{1,0:T(8,128)}, f32[8,1024]{1,0:T(8,128)}, u32[]{:S(2)}, u32[]{:S(2)}) collective-permute-start(f32[8,1024]{1,0:T(8,128)} %stack.35), channel_id=1, source_target_pairs={{0,3},{1,2},{2,1},{3,0},{4,7},{5,6},{6,5},{7,4},{8,11},{9,10},{10,... | collective-permute-start | bytes 98312 | tf_op jit(solution)/shard_map/ppermute | solution.py:36
  186.4 251.4 %collective-permute-start.2 = (f32[8,1024]{1,0:T(8,128)}, f32[8,1024]{1,0:T(8,128)}, u32[]{:S(2)}, u32[]{:S(2)}) collective-permute-start(f32[8,1024]{1,0:T(8,128)} %stack.35), channel_id=1, source_target_pairs={{0,2},{1,3},{2,0},{3,1},{4,6},{5,7},{6,4},{7,5},{8,10},{9,11},{10,... | collective-permute-start | bytes 98312 | tf_op jit(solution)/shard_map/ppermute | solution.py:36
  186.7 251.1 %collective-permute-start.1 = (f32[8,1024]{1,0:T(8,128)}, f32[8,1024]{1,0:T(8,128)}, u32[]{:S(2)}, u32[]{:S(2)}) collective-permute-start(f32[8,1024]{1,0:T(8,128)} %stack.35), channel_id=1, source_target_pairs={{0,1},{1,0},{2,3},{3,2},{4,5},{5,4},{6,7},{7,6},{8,9},{9,8},{10,11... | collective-permute-start | bytes 98312 | tf_op jit(solution)/shard_map/ppermute | solution.py:36
  188.5 14.0 %slice-start = ((s8[4980736]{0:T(1024)(128)(4,1)}), s8[4194304]{0:T(1024)(128)(4,1)S(1)}, s32[]{:S(2)}) async-start(s8[4980736]{0:T(1024)(128)(4,1)} %bitcast.98), calls=%async_computation | async-start | bytes 8388608
  188.5 14.0 %slice-start.1 = ((s8[4980736]{0:T(1024)(128)(4,1)}), s8[786432]{0:T(1024)(128)(4,1)S(1)}, s32[]{:S(2)}) async-start(s8[4980736]{0:T(1024)(128)(4,1)} %bitcast.98), calls=%async_computation.1 | async-start | bytes 1572864
  200.3 266.5 %collective-permute-start = (bf16[66,1024]{1,0:T(8,128)(2,1)}, bf16[66,1024]{1,0:T(8,128)(2,1)}, u32[]{:S(2)}, u32[]{:S(2)}) collective-permute-start(bf16[66,1024]{1,0:T(8,128)(2,1)} %slice.251), channel_id=1, source_target_pairs={{1,0},{2,1},{3,2},{5,4},{6,5},{7,6},{9,8},{10,9},{11,10},{13,12},{... | collective-permute-start | bytes 405512 | tf_op jit(solution)/shard_map/ppermute | solution.py:1471
  206.4 215.2 %collective-permute-start.9 = (f32[2,1536]{1,0:T(2,128)}, f32[2,1536]{1,0:T(2,128)}, u32[]{:S(2)}, u32[]{:S(2)}) collective-permute-start(f32[2,1536]{1,0:T(2,128)} %pad_maximum_fusion), channel_id=1, source_target_pairs={{0,1},{1,0},{2,3},{3,2},{4,5},{5,4},{6,7},{7,6},{8,9},{9,8},{10,11... | collective-permute-start | bytes 36872 | tf_op jit(solution)/shard_map/ppermute | solution.py:36
  422.3 2.5 collective-permute-start.10
  425.5 7.0 %copy-start.13 = (bf16[608,1024]{1,0:T(8,128)(2,1)S(1)}, bf16[608,1024]{1,0:T(8,128)(2,1)}, u32[]{:S(2)}) copy-start(bf16[608,1024]{1,0:T(8,128)(2,1)} %copy-done.12) | copy-start | bytes 3735556
  425.5 3.7 collective-permute-start.11
  429.2 4.4 collective-permute-start.12
  433.6 14.2 %collective-permute-start.13 = (f32[1,1536]{1,0:T(1,128)S(1)}, f32[1,1536]{1,0:T(1,128)}, u32[]{:S(2)}, u32[]{:S(2)}) collective-permute-start(f32[1,1536]{1,0:T(1,128)S(1)} %add.278), channel_id=1, source_target_pairs={{0,16},{4,20},{8,24},{12,28},{16,0},{20,4},{24,8},{28,12},{1,17},{... | collective-permute-start | bytes 18440 | tf_op jit(solution)/shard_map/ppermute | solution.py:41
  439.2 9.3 %collective-permute-start.6 = (f32[8,1024]{1,0:T(8,128)}, f32[8,1024]{1,0:T(8,128)}, u32[]{:S(2)}, u32[]{:S(2)}) collective-permute-start(f32[8,1024]{1,0:T(8,128)} %add_add_fusion.3), channel_id=1, source_target_pairs={{0,12},{4,8},{8,4},{12,0},{16,28},{20,24},{24,20},{28,16},{1,13},{... | collective-permute-start | bytes 98312 | tf_op jit(solution)/shard_map/ppermute | solution.py:41
  441.6 6.9 %collective-permute-start.5 = (f32[8,1024]{1,0:T(8,128)}, f32[8,1024]{1,0:T(8,128)}, u32[]{:S(2)}, u32[]{:S(2)}) collective-permute-start(f32[8,1024]{1,0:T(8,128)} %add_add_fusion.3), channel_id=1, source_target_pairs={{0,8},{4,12},{8,0},{12,4},{16,24},{20,28},{24,16},{28,20},{1,9},{5... | collective-permute-start | bytes 98312 | tf_op jit(solution)/shard_map/ppermute | solution.py:41
  441.6 6.9 %collective-permute-start.4 = (f32[8,1024]{1,0:T(8,128)}, f32[8,1024]{1,0:T(8,128)}, u32[]{:S(2)}, u32[]{:S(2)}) collective-permute-start(f32[8,1024]{1,0:T(8,128)} %add_add_fusion.3), channel_id=1, source_target_pairs={{0,4},{4,0},{8,12},{12,8},{16,20},{20,16},{24,28},{28,24},{1,5},{5... | collective-permute-start | bytes 98312 | tf_op jit(solution)/shard_map/ppermute | solution.py:41
  443.8 9.9 %copy-start.5 = (f32[608,1024]{1,0:T(8,128)S(1)}, f32[608,1024]{1,0:T(8,128)}, u32[]{:S(2)}) copy-start(f32[608,1024]{1,0:T(8,128)} %get-tuple-element.113) | copy-start | bytes 7471108
  443.8 9.9 %copy-start.18 = (f32[1024]{0:T(1024)S(1)}, f32[1024]{0:T(1024)}, u32[]{:S(2)}) copy-start(f32[1024]{0:T(1024)} %copy-done.17) | copy-start | bytes 12292
  443.8 9.9 %copy-start.20 = (f32[1024]{0:T(1024)S(1)}, f32[1024]{0:T(1024)}, u32[]{:S(2)}) copy-start(f32[1024]{0:T(1024)} %copy-done.19) | copy-start | bytes 12292
  449.3 3.7 collective-permute-start.7
  455.7 12.2 %copy-start.10 = (bf16[245,1024]{1,0:T(8,128)(2,1)S(1)}, bf16[245,1024]{1,0:T(8,128)(2,1)}, u32[]{:S(2)}) copy-start(bf16[245,1024]{1,0:T(8,128)(2,1)} %get-tuple-element.122) | copy-start | bytes 1505284
  455.7 12.2 %copy-start.11 = (bf16[245,1024]{1,0:T(8,128)(2,1)S(1)}, bf16[245,1024]{1,0:T(8,128)(2,1)}, u32[]{:S(2)}) copy-start(bf16[245,1024]{1,0:T(8,128)(2,1)} %get-tuple-element.123) | copy-start | bytes 1505284
  456.0 14.9 %collective-permute-start.8 = (f32[66,1024]{1,0:T(8,128)S(1)}, f32[66,1024]{1,0:T(8,128)S(1)}, u32[]{:S(2)}, u32[]{:S(2)}) collective-permute-start(f32[66,1024]{1,0:T(8,128)S(1)} %slice.262), channel_id=1, source_target_pairs={{1,0},{2,1},{3,2},{5,4},{6,5},{7,6},{9,8},{10,9},{11,10},{13,12},{... | collective-permute-start | bytes 811016 | tf_op jit(solution)/shard_map/ppermute | solution.py:1471
  (18 other events, 48.4 us)

commit v2 on v1

--- a/solution.py
+++ b/solution.py
@@ -845,35 +845,68 @@
     )(*smalls, *vectors, tokens, cotangent, *weights)
 
 
-CHUNK = 256
+CHUNK = 128
+CHUNKS = 24
 STAGE_DELAY = (0, 1, 3, 5, 7, 9, 11)
-
-
-def gradient_kernel(
+TICK_HIDDEN, TICK_SECOND, TICK_CONTEXT, TICK_HEADS = 0, 4, 5, 6
+TICK_NORMED, TICK_FIRST, TICK_MIXED = 14, 18, 19
+TICK_SUMS = (18, 20, 22, 24)
+
+
+def backward_kernel(
+    lengths,
+    groups,
+    counts,
+    gain,
+    hidden_gain,
+    down_bias,
+    sums,
+    tokens_ref,
+    cotangent_ref,
+    stream_ref,
+    middle_ref,
+    normed_ref,
+    qkv_ref,
+    context_ref,
+    hidden_ref,
+    grad_mixed_ref,
     active_ref,
-    grad_mixed_ref,
-    hidden_ref,
     grad_pre_ref,
-    context_ref,
-    grad_attended_ref,
-    grad_qkv_ref,
-    normed_ref,
-    out_ref,
-    active,
-    grad_mixed,
-    hidden,
-    grad_pre,
-    context,
-    grad_attended,
-    grad_qkv,
-    normed,
+    wqkv_ref,
+    wo_ref,
+    wup_ref,
+    wdown_ref,
+    reduced_out,
+    finals_out,
+    layer_out,
+    tokens_grad_out,
     made,
     pair,
     across,
     over_y,
     over_z,
     final,
+    act,
+    grad_pre,
+    hidden,
+    grad_mixed,
+    context,
+    normed,
+    grad_attended,
+    qkv,
+    grad_context,
+    rowbuf,
+    gradient,
+    trunk,
+    stream,
+    weight,
+    packet,
+    from_mp,
+    from_y,
+    from_z,
     load_sem,
+    act_sem,
+    weight_sem,
     pair_send,
     pair_recv,
     across_send,
@@ -887,208 +920,212 @@
     back_y_send,
     back_y_recv,
     out_sem,
+    stat_send,
+    stat_recv,
 ):
-    mp = lax.axis_index("mp")
-    dp = lax.axis_index("dp")
-    y = dp % 2
-    z = dp // 2
-    sibling = {"mp": mp + 1 - 2 * (mp % 2)}
-    opposite = {"mp": mp + 2 - 4 * (mp // 2)}
-    y_peer = {"dp": dp + 1 - 2 * y}
-    z_places = [(z + m) % 4 for m in (1, 2, 3)]
-    z_peers = [{"dp": place * 2 + y} for place in z_places]
+    mp, y, z, mp_peers, y_peer, z_places, z_peers = places()
+    sibling, opposite, _ = mp_peers
     half = CHUNK // 2
     eighth = CHUNK // 8
-    chunks = final.shape[0]
-    width = final.shape[2]
-
-    loads = [
-        pltpu.make_async_copy(source, target, load_sem.at[i])
-        for i, (source, target) in enumerate(
+    rows = normed.shape[0]
+    width = context.shape[1] // 4
+    blocks = rows // 32
+
+    loads = {
+        name: pltpu.make_async_copy(source, target, load_sem.at[i])
+        for i, (name, source, target) in enumerate(
             (
-                (active_ref, active),
-                (grad_mixed_ref, grad_mixed),
-                (hidden_ref, hidden),
-                (grad_pre_ref, grad_pre),
-                (context_ref, context),
-                (grad_attended_ref, grad_attended),
-                (grad_qkv_ref, grad_qkv),
-                (normed_ref, normed),
+                ("grad_mixed", grad_mixed_ref, grad_mixed),
+                ("grad_pre", grad_pre_ref, grad_pre),
+                ("middle", middle_ref, trunk),
+                ("cotangent", cotangent_ref, rowbuf),
+                ("qkv", qkv_ref, qkv),
+                ("hidden", hidden_ref, hidden),
+                ("context", context_ref, context),
+                ("normed", normed_ref, normed),
+                ("stream", stream_ref, stream),
+                ("tokens", tokens_ref, rowbuf),
+                ("active", active_ref, grad_pre),
+                ("middle again", middle_ref, stream),
+                ("layer", hidden, layer_out),
+                ("tokens_grad", gradient, tokens_grad_out),
             )
         )
-    ]
-    for load in loads:
-        load.start()
-    barrier = pltpu.get_barrier_semaphore()
-    for peer in [sibling, opposite, y_peer] + z_peers:
-        pl.semaphore_signal(barrier, inc=1, device_id=peer, device_id_type=MESH)
-    pl.semaphore_wait(barrier, 6)
+    }
+
+    def act_loads(c):
+        return [
+            pltpu.make_async_copy(
+                active_ref.at[:, pl.ds(pl.multiple_of(r * D + c * CHUNK, CHUNK), CHUNK)],
+                act.at[c % 2, r],
+                act_sem.at[c % 2, r],
+            )
+            for r in range(4)
+        ]
+
+    def weight_load(s):
+        if s < 4:
+            source = wup_ref.at[s]
+        elif s == 4:
+            source = wo_ref
+        elif s < 9:
+            source = wqkv_ref.at[s - 5]
+        else:
+            source = wdown_ref.at[s - 9]
+        target = weight.at[s % 2, :, pl.ds(0, 3 * width)] if 5 <= s < 9 else weight.at[s % 2]
+        return pltpu.make_async_copy(source, target, weight_sem.at[s % 2])
+
+    for c in range(2):
+        start_all(act_loads(c))
+    loads["grad_mixed"].start()
+    weight_load(0).start()
+    loads["grad_pre"].start()
+    weight_load(1).start()
+    for name in ("middle", "cotangent", "qkv", "hidden", "context", "normed", "stream"):
+        loads[name].start()
+    greet(mp_peers + [y_peer] + z_peers)
+
+    weights = [counts[groups[4 * mp + j]].astype(F32) for j in range(4)]
+    slices = lax.axis_size("dp")
+    count_valid = slices * PAIRS * PAIR_LEN
+    column_mean = joined(sums, 0) / count_valid
+    spread = joined(sums, 8) / count_valid - column_mean * column_mean
+    inverse = lax.rsqrt(spread + 1e-05)
+    mean_weight = sums[16:17, 0:1] / (slices * 16)
 
     def pair_copy(c):
-        return pltpu.make_async_remote_copy(
-            src_ref=made.at[c % 2, pl.ds(0, 2)],
-            dst_ref=pair.at[c],
-            send_sem=pair_send.at[c],
-            recv_sem=pair_recv.at[c],
-            device_id=sibling,
-            device_id_type=MESH,
+        return remote(
+            made.at[c % 2, pl.ds(0, 2)], pair.at[c], pair_send.at[c], pair_recv.at[c], sibling
         )
 
     def across_copy(c):
-        return pltpu.make_async_remote_copy(
-            src_ref=pair.at[c, 1],
-            dst_ref=across.at[c],
-            send_sem=across_send.at[c],
-            recv_sem=across_recv.at[c],
-            device_id=opposite,
-            device_id_type=MESH,
+        return remote(
+            pair.at[c, 1], across.at[c], across_send.at[c], across_recv.at[c], opposite
         )
 
     def y_copy(c):
-        return pltpu.make_async_remote_copy(
-            src_ref=across.at[c, pl.ds(pl.multiple_of((1 - y) * half, half), half)],
-            dst_ref=over_y.at[c],
-            send_sem=y_send.at[c],
-            recv_sem=y_recv.at[c],
-            device_id=y_peer,
-            device_id_type=MESH,
+        return remote(
+            across.at[c, pl.ds(pl.multiple_of((1 - y) * half, half), half)],
+            over_y.at[c],
+            y_send.at[c],
+            y_recv.at[c],
+            y_peer,
         )
 
     def z_copies(c):
         return [
-            pltpu.make_async_remote_copy(
-                src_ref=over_y.at[c, pl.ds(pl.multiple_of(place * eighth, eighth), eighth)],
-                dst_ref=over_z.at[c, m],
-                send_sem=z_send.at[c, m],
-                recv_sem=z_recv.at[c, m],
-                device_id=peer,
-                device_id_type=MESH,
+            remote(
+                over_y.at[c, pl.ds(pl.multiple_of(place * eighth, eighth), eighth)],
+                over_z.at[c, m],
+                z_send.at[c, m],
+                z_recv.at[c, m],
+                peer,
             )
             for m, (place, peer) in enumerate(zip(z_places, z_peers))
         ]
 
     def back_z_copies(c):
-        rows = pl.ds(pl.multiple_of(y * half + z * eighth, eighth), eighth)
+        view = final.at[c, pl.ds(pl.multiple_of(y * half + z * eighth, eighth), eighth)]
         return [
-            pltpu.make_async_remote_copy(
-                src_ref=final.at[c, rows],
-                dst_ref=final.at[c, rows],
-                send_sem=back_z_send.at[c, m],
-                recv_sem=back_z_recv.at[c, m],
-                device_id=peer,
-                device_id_type=MESH,
-            )
+            remote(view, view, back_z_send.at[c, m], back_z_recv.at[c, m], peer)
             for m, peer in enumerate(z_peers)
         ]
 
     def back_y_copy(c):
-        rows = pl.ds(pl.multiple_of(y * half, half), half)
-        return pltpu.make_async_remote_copy(
-            src_ref=final.at[c, rows],
-            dst_ref=final.at[c, rows],
-            send_sem=back_y_send.at[c],
-            recv_sem=back_y_recv.at[c],
-            device_id=y_peer,
-            device_id_type=MESH,
-        )
+        view = final.at[c, pl.ds(pl.multiple_of(y * half, half), half)]
+        return remote(view, view, back_y_send.at[c], back_y_recv.at[c], y_peer)
 
     def out_copy(c):
-        return pltpu.make_async_copy(final.at[c], out_ref.at[c], out_sem.at[c])
-
-    def block_loop(count, body):
-        def step(i, carry):
-            body(pl.ds(pl.multiple_of(i * eighth, eighth), eighth))
-            return carry
-
-        lax.fori_loop(0, count, step, 0)
+        return pltpu.make_async_copy(final.at[c], reduced_out.at[c], out_sem.at[c])
 
     def make(c):
-        def part(j, carry):
+        @pl.when(c < 8)
+        def _():
+            for copy in act_loads(c):
+                copy.wait()
+
+        def one(j):
             r = 2 * j + 1 - 5 * (j // 2)
 
             def store(left, right):
                 made[c % 2, j] = dot_rows(left, right).astype(BF)
 
-            @pl.when(c < 4)
+            @pl.when(c < 8)
             def _():
-                left = active[:, pl.ds(pl.multiple_of((r * 4 + c) * CHUNK, CHUNK), CHUNK)]
-                store(left, grad_mixed[...])
-
-            @pl.when((c >= 4) & (c < 8))
+                store(act[c % 2, r], grad_mixed[...])
+
+            @pl.when((c >= 8) & (c < 16))
             def _():
-                left = hidden[:, pl.ds(pl.multiple_of((c - 4) * CHUNK, CHUNK), CHUNK)]
-                store(left, grad_pre[:, pl.ds(pl.multiple_of(r * width, width), width)])
-
-            @pl.when(c == 8)
+                store(
+                    hidden[:, block_rows(c - 8, CHUNK)], grad_pre[:, block_rows(r, D)]
+                )
+
+            @pl.when((c >= 16) & (c < 18))
             def _():
-                left = context[:, pl.ds(pl.multiple_of(r * CHUNK, CHUNK), CHUNK)]
-                store(left, grad_attended[...])
-
-            @pl.when(c > 8)
+                store(context[:, block_rows(2 * r + c - 16, CHUNK)], grad_attended[...])
+
+            @pl.when(c >= 18)
             def _():
-                left = grad_qkv[:, pl.ds(pl.multiple_of((r * 3 + c - 9) * CHUNK, CHUNK), CHUNK)]
-                store(left, normed[...])
-
-            return carry
-
-        lax.fori_loop(0, 4, part, 0)
+                store(qkv[:, block_rows(6 * r + c - 18, CHUNK)], normed[...])
+
+        loop(4, one)
+
+        @pl.when(c < 6)
+        def _():
+            start_all(act_loads(c + 2))
 
     def add_pair(c):
-        pair_copy(c).wait_recv()
-        pair_copy(c).wait_send()
-
-        def body(rows):
+        pair_copy(c).wait()
+
+        def body(i):
+            here = block_rows(i, 32)
             for which in (1, 0):
-                pair[c, which, rows, :] = (
-                    pair[c, which, rows, :].astype(F32)
-                    + made[c % 2, 2 + which, rows, :].astype(F32)
+                pair[c, which, here, :] = (
+                    pair[c, which, here, :].astype(F32)
+                    + made[c % 2, 2 + which, here, :].astype(F32)
                 ).astype(BF)
 
-        block_loop(8, body)
+        loop(CHUNK // 32, body)
 
     def add_across(c):
         across_copy(c).wait_recv()
 
-        def body(rows):
-            across[c, rows, :] = (
-                across[c, rows, :].astype(F32) + pair[c, 0, rows, :].astype(F32)
+        def body(i):
+            here = block_rows(i, 32)
+            across[c, here, :] = (
+                across[c, here, :].astype(F32) + pair[c, 0, here, :].astype(F32)
             ).astype(BF)
 
-        block_loop(8, body)
+        loop(CHUNK // 32, body)
 
     def add_y(c):
         y_copy(c).wait_recv()
 
-        def step(i, carry):
-            rows = pl.ds(pl.multiple_of(i * eighth, eighth), eighth)
-            own = pl.ds(pl.multiple_of(y * half + i * eighth, eighth), eighth)
-            over_y[c, rows, :] = (
-                over_y[c, rows, :].astype(F32) + across[c, own, :].astype(F32)
+        def body(i):
+            here = block_rows(i, 32)
+            own = pl.ds(pl.multiple_of(y * half + i * 32, 32), 32)
+            over_y[c, here, :] = (
+                over_y[c, here, :].astype(F32) + across[c, own, :].astype(F32)
             ).astype(BF)
-            return carry
-
-        lax.fori_loop(0, 4, step, 0)
+
+        loop(half // 32, body)
 
     def add_z(c):
-        for copy in z_copies(c):
-            copy.wait_recv()
-        total = over_y[c, pl.ds(pl.multiple_of(z * eighth, eighth), eighth), :].astype(F32)
+        wait_recv_all(z_copies(c))
+        value = over_y[c, block_rows(z, eighth), :].astype(F32)
         for m in range(3):
-            total = total + over_z[c, m].astype(F32)
-        final[c, pl.ds(pl.multiple_of(y * half + z * eighth, eighth), eighth), :] = total.astype(BF)
-
-    def wait_back_z(c):
-        for copy in back_z_copies(c):
-            copy.wait_recv()
-
-    def wait_back_y(c):
-        back_y_copy(c).wait_recv()
-
-    def start_all(copies):
-        for copy in copies:
-            copy.start()
-
-    handle = (make, add_pair, add_across, add_y, add_z, wait_back_z, wait_back_y)
+            value = value + over_z[c, m].astype(F32)
+        final[c, pl.ds(pl.multiple_of(y * half + z * eighth, eighth), eighth), :] = value.astype(BF)
+
+    handle = (
+        make,
+        add_pair,
+        add_across,
+        add_y,
+        add_z,
+        lambda c: wait_recv_all(back_z_copies(c)),
+        lambda c: back_y_copy(c).wait_recv(),
+    )
     send = (
         lambda c: [pair_copy(c)],
         lambda c: [across_copy(c)],
@@ -1099,80 +1136,450 @@
         lambda c: [out_copy(c)],
     )
 
+    def hidden_step(r):
+        left = block_rows(r, D)
+
+        def tile(n):
+            columns = block_rows(n, 256)
+            value = dot_cols(grad_pre[:, left], weight[r % 2, columns, :])
+
+            @pl.when(r == 0)
+            def _():
+                gradient[:, columns] = value
+
+            @pl.when(r > 0)
+            def _():
+                gradient[:, columns] = gradient[:, columns] + value
+
+        loop(4, tile)
+
+    def fold(value):
+        return jnp.sum(value.reshape(4, 8, D), axis=0)
+
+    def put(index, value):
+        for j in range(8):
+            packet[0, 8 * index + j : 8 * index + j + 1, :] = value[:, j * 128 : (j + 1) * 128]
+
+    def put_all(first, values):
+        for i, value in enumerate(values):
+            put(first + i, jnp.sum(value, axis=0, keepdims=True))
+
+    def ones_dot(value):
+        return dot(jnp.ones((16, rows), BF), value)[0:1, :]
+
+    def row_weight_of(i):
+        row = i * 32 + lax.broadcasted_iota(jnp.int32, (32, 1), 0)
+        item, _, in_pair, _ = item_of_rows(row, lengths, mp)
+        return jnp.where(in_pair, choose_item(item, weights), 0.0) / mean_weight, in_pair
+
+    zero = jnp.zeros((8, D), F32)
+
+    def second_norm_back():
+        def body(i, carry):
+            here = block_rows(i, 32)
+            unit, scale = stats(trunk[here, :])
+            grad = gradient[here, :]
+            row_weight, _ = row_weight_of(i)
+            value = rowbuf[here, :].astype(F32) * row_weight + norm_back(
+                grad, unit, scale, hidden_gain[...]
+            )
+            trunk[here, :] = value
+            low = value.astype(BF)
+            grad_attended[here, :] = low
+            return (
+                carry[0] + fold(grad * unit),
+                carry[1] + fold(grad),
+                carry[2] + fold(low.astype(F32)),
+            )
+
+        put_all(4, lax.fori_loop(0, blocks, body, (zero, zero, zero)))
+        put(7, ones_dot(grad_mixed[...]))
+
+    def context_step():
+        def tile(n):
+            columns = block_rows(n, 256)
+            grad_context[:, columns] = dot_cols(grad_attended[...], weight[0, columns, :]).astype(BF)
+
+        loop(4, tile)
+
+    def head_pair_back(index):
+        r = index // 2
+        p = index % 2
+        lanes = [block_rows(6 * r + 2 * n + p, 128) for n in range(3)]
+        source = block_rows(2 * r + p, 128)
+        factor = 1.0 / math.sqrt(HEAD_DIM)
+        for first, size in blocks_of(rows):
+            here = pl.ds(first, size)
+            same = owner_of_rows(
+                first + lax.broadcasted_iota(jnp.int32, (size, 1), 0), lengths, mp
+            ) == owner_of_rows(first + lax.broadcasted_iota(jnp.int32, (1, size), 1), lengths, mp)
+            q, k, v = [qkv[here, lane] for lane in lanes]
+            g = grad_context[here, source]
+            results = []
+            for h in range(2):
+                cut = slice(h * HEAD_DIM, (h + 1) * HEAD_DIM)
+                soft = softmax_rows(q[:, cut], k[:, cut], same)
+                grad_soft = dot_cols(g[:, cut], v[:, cut])
+                center = jnp.sum(soft * grad_soft, axis=-1, keepdims=True)
+                grad_scores = (soft * (grad_soft - center)).astype(BF)
+                results.append(
+                    (
+                        (dot(grad_scores, k[:, cut]) * factor).astype(BF),
+                        (dot_rows(grad_scores, q[:, cut]) * factor).astype(BF),
+                        dot_rows(soft.astype(BF), g[:, cut]).astype(BF),
+                    )
+                )
+            for n in range(3):
+                qkv[here, lanes[n]] = jnp.concatenate([results[0][n], results[1][n]], axis=1)
+
+    def normed_step(r):
+        left = qkv[:, block_rows(r, 3 * width)]
+
+        def tile(n):
+            columns = block_rows(n, 256)
+            value = dot_cols(left, weight[(r + 1) % 2, columns, 0 : 3 * width])
+
+            @pl.when(r == 0)
+            def _():
+                gradient[:, columns] = value
+
+            @pl.when(r > 0)
+            def _():
+                gradient[:, columns] = gradient[:, columns] + value
+
+        loop(4, tile)
+
+    def first_norm_back():
+        def body(i, carry):
+            here = block_rows(i, 32)
+            unit, scale = stats(stream[here, :])
+            grad = gradient[here, :]
+            value = trunk[here, :] + norm_back(grad, unit, scale, gain[...])
+            standard = (rowbuf[here, :].astype(F32) - column_mean) * inverse
+            gradient[here, :] = value
+            return (
+                carry[0] + fold(value),
+                carry[1] + fold(value * standard),
+                carry[2] + fold(grad * unit),
+                carry[3] + fold(grad),
+            )
+
+        put_all(0, lax.fori_loop(0, blocks, body, (zero, zero, zero, zero)))
+        for r in range(4):
+            if r:
+                packet[r, 0:64, :] = packet[0, 0:64, :]
+            parts = [
+                ones_dot(qkv[:, (3 * r + n) * width : (3 * r + n + 1) * width]) for n in (0, 2)
+            ] + [
+                ones_dot(grad_pre[:, r * D + n * width : r * D + (n + 1) * width]) for n in range(4)
+            ]
+            for i, value in enumerate(parts):
+                for j in range(2):
+                    packet[r, 64 + 2 * i + j : 65 + 2 * i + j, :] = value[
+                        :, j * 128 : (j + 1) * 128
+                    ]
+            packet[r, 76:80, :] = jnp.zeros((4, 128), F32)
+
+    def mixed_step(r):
+        left = grad_pre[:, block_rows(r, D)]
+
+        def tile(n):
+            columns = block_rows(n, 256)
+            stream[:, columns] = stream[:, columns] + dot(left, weight[(r + 1) % 2, :, columns])
+
+        loop(4, tile)
+
+    def layer_step():
+        def body(i):
+            here = block_rows(i, 32)
+            hidden[here, :] = (stream[here, :] + down_bias[...]).astype(BF)
+
+        loop(blocks, body)
+
+    def exchange(stage, sources, peers, slots):
+        return [
+            remote(
+                source, slots.at[m], stat_send.at[stage, m], stat_recv.at[stage, m], peer
+            )
+            for m, (source, peer) in enumerate(zip(sources, peers))
+        ]
+
+    sums_a = exchange(0, [packet.at[r] for r in (1, 2, 3)], mp_peers, from_mp)
+    sums_b = exchange(1, [packet.at[4]], [y_peer], from_y)
+    sums_c = exchange(2, [packet.at[5]] * 3, z_peers, from_z)
+
+    def gather_sums(first, copies, slots, target):
+        value = packet[first]
+        for m, copy in enumerate(copies):
+            copy.wait_recv()
+            value = value + slots[m]
+        packet[target] = value
+
+    def tokens_step():
+        total = joined(packet[6], 0), joined(packet[6], 8)
+
+        def body(i):
+            here = block_rows(i, 32)
+            standard = (rowbuf[here, :].astype(F32) - column_mean) * inverse
+            _, in_pair = row_weight_of(i)
+            share = jnp.where(in_pair, 1.0 / count_valid, 0.0)
+            gradient[here, :] = inverse * (
+                gradient[here, :] - share * (total[0] + total[1] * standard)
+            )
+
+        loop(blocks, body)
+
+    def work(k):
+        for s in range(4):
+
+            @pl.when(k == TICK_HIDDEN + s)
+            def _(s=s):
+                if s == 0:
+                    loads["grad_pre"].wait()
+                weight_load(s).wait()
+
+        @pl.when((k >= TICK_HIDDEN) & (k < TICK_HIDDEN + 4))
+        def _():
+            hidden_step(k - TICK_HIDDEN)
+
+        for s in range(4):
+
+            @pl.when(k == TICK_HIDDEN + s)
+            def _(s=s):
+                weight_load(s + 2).start()
+
+        @pl.when(k == TICK_SECOND)
+        def _():
+            loads["middle"].wait()
+            loads["cotangent"].wait()
+            second_norm_back()
+            loads["tokens"].start()
+
+        @pl.when(k == TICK_CONTEXT)
+        def _():
+            weight_load(4).wait()
+            context_step()
+            weight_load(6).start()
+            loads["qkv"].wait()
+
+        @pl.when((k >= TICK_HEADS) & (k < TICK_HEADS + 8))
+        def _():
+            head_pair_back(k - TICK_HEADS)
+
+        for s in range(4):
+
+            @pl.when(k == TICK_NORMED + s)
+            def _(s=s):
+                weight_load(5 + s).wait()
+
+        @pl.when((k >= TICK_NORMED) & (k < TICK_NORMED + 4))
+        def _():
+            normed_step(k - TICK_NORMED)
+
+        for s in range(4):
+
+            @pl.when(k == TICK_NORMED + s)
+            def _(s=s):
+                weight_load(7 + s).start()
+
+        @pl.when(k == TICK_FIRST)
+        def _():
+            loads["stream"].wait()
+            loads["tokens"].wait()
+            first_norm_back()
+            loads["active"].start()
+            loads["middle again"].start()
+            start_all(sums_a)
+
+        for s in range(4):
+
+            @pl.when(k == TICK_MIXED + s)
+            def _(s=s):
+                if s == 0:
+                    loads["active"].wait()
+                    loads["middle again"].wait()
+                weight_load(9 + s).wait()
+
+        @pl.when((k >= TICK_MIXED) & (k < TICK_MIXED + 4))
+        def _():
+            mixed_step(k - TICK_MIXED)
+
+        for s in range(2):
+
+            @pl.when(k == TICK_MIXED + s)
+            def _(s=s):
+                weight_load(11 + s).start()
+
+        @pl.when(k == TICK_MIXED + 3)
+        def _():
+            layer_step()
+            loads["layer"].start()
+
+        @pl.when(k == TICK_SUMS[1])
+        def _():
+            gather_sums(0, sums_a, from_mp, 4)
+            start_all(sums_b)
+
+        @pl.when(k == TICK_SUMS[2])
+        def _():
+            gather_sums(4, sums_b, from_y, 5)
+            start_all(sums_c)
+
+        @pl.when(k == TICK_SUMS[3])
+        def _():
+            gather_sums(5, sums_c, from_z, 6)
+            finals_out[...] = packet[6]
+            tokens_step()
+            loads["tokens_grad"].start()
+
+    waits = {0: ("grad_mixed",), 8: ("hidden",), 16: ("context",), 18: ("normed",)}
+
     def tick(k, carry):
-        for when, count in ((0, 2), (4, 2), (8, 2), (9, 2)):
-            first = {0: 0, 4: 2, 8: 4, 9: 6}[when]
+        for when, names in waits.items():
 
             @pl.when(k == when)
-            def _(first=first, count=count):
-                for load in loads[first : first + count]:
-                    load.wait()
-
-        for stage in (6, 5, 4, 3, 2, 0, 1):
+            def _(names=names):
+                for name in names:
+                    loads[name].wait()
+
+        def staged(stage, actions):
             c = k - STAGE_DELAY[stage]
 
-            @pl.when((c >= 0) & (c < chunks))
-            def _(stage=stage, c=c):
-                handle[stage](c)
-
-        for stage in (1, 2, 3, 4, 5, 0, 6):
-            c = k - STAGE_DELAY[stage]
-
-            @pl.when((c >= 0) & (c < chunks))
-            def _(stage=stage, c=c):
-                start_all(send[stage](c))
-
+            @pl.when((c >= 0) & (c < CHUNKS))
+            def _():
+                actions[stage](c)
+
+        sends = tuple(lambda c, f=f: start_all(f(c)) for f in send)
+        for stage in (6, 5, 4, 3, 2):
+            staged(stage, handle)
+        for stage in (2, 3, 4, 5, 6):
+            staged(stage, sends)
+        staged(0, handle)
+        staged(1, handle)
+        staged(0, sends)
+        staged(1, sends)
+        work(k)
         return carry
 
-    lax.fori_loop(0, chunks + STAGE_DELAY[-1], tick, 0)
-
-    def finish(c, carry):
+    lax.fori_loop(0, CHUNKS + STAGE_DELAY[-1], tick, 0)
+
+    def finish(c):
         across_copy(c).wait_send()
         y_copy(c).wait_send()
         for copy in z_copies(c) + back_z_copies(c):
             copy.wait_send()
         back_y_copy(c).wait_send()
         out_copy(c).wait()
-        return carry
-
-    lax.fori_loop(0, chunks, finish, 0)
-
-
-def reduce_gradients(*inputs):
-    chunks = 12
+
+    loop(CHUNKS, finish)
+    for copy in sums_a + sums_b + sums_c:
+        copy.wait_send()
+    loads["layer"].wait()
+    loads["tokens_grad"].wait()
+
+
+def backward(smalls, vectors, sums, saved):
+    (
+        tokens,
+        cotangent,
+        stream,
+        middle,
+        normed,
+        qkv,
+        context,
+        hidden,
+        grad_mixed,
+        active,
+        grad_pre,
+        wqkv,
+        wo,
+        wup,
+        wdown,
+    ) = saved
+    rows = normed.shape[0]
+    shape = jax.ShapeDtypeStruct
+    low = shape((rows, D), BF)
+    full = shape((rows, D), F32)
+    packed = shape((80, 128), F32)
+    scratch = [
+        shape((2, 4, CHUNK, D), BF),
+        shape((CHUNKS, 2, CHUNK, D), BF),
+        shape((CHUNKS, CHUNK, D), BF),
+        shape((CHUNKS, CHUNK // 2, D), BF),
+        shape((CHUNKS, 3, CHUNK // 8, D), BF),
+        shape((CHUNKS, CHUNK, D), BF),
+        shape((2, 4, rows, CHUNK), BF),
+        shape(grad_pre.shape, BF),
+        low,
+        low,
+        low,
+        low,
+        low,
+        shape(qkv.shape, BF),
+        low,
+        low,
+        full,
+        full,
+        full,
+        shape((2, D, D), BF),
+        shape((7, 80, 128), F32),
+        shape((3, 80, 128), F32),
+        shape((1, 80, 128), F32),
+        shape((3, 80, 128), F32),
+    ]
+    dma = pltpu.SemaphoreType.DMA
+    any_space = pl.BlockSpec(memory_space=pl.ANY)
+    vmem = pl.BlockSpec(memory_space=pltpu.VMEM)
     return pl.pallas_call(
-        gradient_kernel,
-        out_shape=jax.ShapeDtypeStruct((chunks, CHUNK, D), BF),
-        in_specs=[pl.BlockSpec(memory_space=pl.ANY)] * 8,
-        out_specs=pl.BlockSpec(memory_space=pl.ANY),
-        scratch_shapes=[pltpu.VMEM(v.shape, v.dtype) for v in inputs]
+        backward_kernel,
+        out_shape=(shape((CHUNKS, CHUNK, D), BF), packed, low, full),
+        in_specs=[pl.BlockSpec(memory_space=pltpu.SMEM)] * 3 + [vmem] * 4 + [any_space] * 15,
+        out_specs=(any_space, vmem, any_space, any_space),
+        scratch_shapes=[pltpu.VMEM(v.shape, v.dtype) for v in scratch]
         + [
-            pltpu.VMEM((2, 4, CHUNK, D), BF),
-            pltpu.VMEM((chunks, 2, CHUNK, D), BF),
-            pltpu.VMEM((chunks, CHUNK, D), BF),
-            pltpu.VMEM((chunks, CHUNK // 2, D), BF),
-            pltpu.VMEM((chunks, 3, CHUNK // 8, D), BF),
-            pltpu.VMEM((chunks, CHUNK, D), BF),
-            pltpu.SemaphoreType.DMA((8,)),
-            pltpu.SemaphoreType.DMA((chunks,)),
-            pltpu.SemaphoreType.DMA((chunks,)),
-            pltpu.SemaphoreType.DMA((chunks,)),
-            pltpu.SemaphoreType.DMA((chunks,)),
-            pltpu.SemaphoreType.DMA((chunks,)),
-            pltpu.SemaphoreType.DMA((chunks,)),
-            pltpu.SemaphoreType.DMA((chunks, 3)),
-            pltpu.SemaphoreType.DMA((chunks, 3)),
-            pltpu.SemaphoreType.DMA((chunks, 3)),
-            pltpu.SemaphoreType.DMA((chunks, 3)),
-            pltpu.SemaphoreType.DMA((chunks,)),
-            pltpu.SemaphoreType.DMA((chunks,)),
-            pltpu.SemaphoreType.DMA((chunks,)),
+            dma((14,)),
+            dma((2, 4)),
+            dma((2,)),
+            dma((CHUNKS,)),
+            dma((CHUNKS,)),
+            dma((CHUNKS,)),
+            dma((CHUNKS,)),
+            dma((CHUNKS,)),
+            dma((CHUNKS,)),
+            dma((CHUNKS, 3)),
+            dma((CHUNKS, 3)),
+            dma((CHUNKS, 3)),
+            dma((CHUNKS, 3)),
+            dma((CHUNKS,)),
+            dma((CHUNKS,)),
+            dma((CHUNKS,)),
+            dma((3, 3)),
+            dma((3, 3)),
         ],
         compiler_params=pltpu.CompilerParams(
-            collective_id=0, has_side_effects=True, vmem_limit_bytes=67043328
+            collective_id=2, has_side_effects=True, vmem_limit_bytes=67043328
         ),
-        name="reduce_gradients",
-    )(*inputs)
+        name="backward",
+    )(
+        *smalls,
+        *vectors,
+        sums,
+        tokens,
+        cotangent,
+        stream,
+        middle,
+        normed,
+        qkv,
+        context,
+        hidden,
+        grad_mixed,
+        active,
+        grad_pre,
+        wqkv,
+        wo.reshape(D, D),
+        wup,
+        wdown,
+    )
 
 
 def general_shards(
@@ -1447,22 +1854,16 @@
     down_bias,
 ):
     shard_count = lax.axis_size("mp")
-    slice_count = lax.axis_size("dp")
     mp = lax.axis_index("mp")
     rows_here = tokens.shape[0]
-    item_count = item_lengths.shape[0]
     pairs_here = PAIRS // shard_count
     shift = rows_here - pairs_here * PAIR_LEN
     halo = shift * (shard_count - 1)
     padding = rows_here * shard_count - PAIRS * PAIR_LEN
-    tail_block = -(-padding // 32) * 32
-    rows = pairs_here * WINDOW + tail_block
+    rows = pairs_here * WINDOW + -(-padding // 32) * 32
     is_last = mp == shard_count - 1
     width = query_weight.shape[1]
     hidden_width = up_weight.shape[1]
-    chosen = item_group[:, None] == jnp.arange(group_count.shape[0], dtype=jnp.int32)[None, :]
-    item_scale = jnp.sum(jnp.where(chosen, grid_scale[None, :], 0.0), axis=1)
-    item_weight = jnp.sum(jnp.where(chosen, group_count[None, :], 0), axis=1).astype(F32)
 
     def unwindows(v):
         own = jnp.concatenate(
@@ -1474,24 +1875,7 @@
         joined = jnp.concatenate([own, jnp.where(is_last, tail, after)], axis=0)
         return lax.dynamic_slice_in_dim(joined, shift * mp, rows_here, axis=0)
 
-    (
-        tokens_w,
-        cotangent_w,
-        sums,
-        stream,
-        middle,
-        normed,
-        qkv,
-        context,
-        hidden_in,
-        grad_mixed,
-        active,
-        grad_pre,
-        qkv_weights,
-        output_weights,
-        up_weights,
-        down_weights,
-    ) = forward(
+    saved = forward(
         (item_lengths, item_group, group_count, grid_scale),
         [
             v[None, :]
@@ -1511,104 +1895,22 @@
         (query_weight, key_weight, value_weight, output_weight, up_weight, down_weight),
         rows,
     )
-    tokens_w = tokens_w.astype(F32)
-    sums = sums.reshape(3, D)
-    row = jnp.arange(rows, dtype=jnp.int32)
-    window = row // WINDOW
-    offset = row % WINDOW
-    in_pair = (window < pairs_here) & (offset < PAIR_LEN)
-    is_padding = (window == pairs_here) & (offset < padding) & is_last
-    pair = pairs_here * mp + window
-    item_ids = jnp.arange(item_count, dtype=jnp.int32)
-    first_len = jnp.sum(
-        jnp.where(item_ids[None, :] == (2 * pair)[:, None], item_lengths[None, :], 0), axis=1
-    )
-    second = (offset >= first_len).astype(jnp.int32)
-    owner = jnp.where(in_pair, 2 * pair + second, jnp.where(is_padding, item_count, -1))
-    position = offset - second * first_len
-    member = owner[:, None] == item_ids[None, :]
-    row_scale = jnp.sum(jnp.where(member, item_scale[None, :], 0.0), axis=1)
-    row_count = jnp.sum(jnp.where(member, item_weight[None, :], 0.0), axis=1)
-    valid = in_pair.astype(F32)[:, None]
-    count_valid = slice_count * PAIRS * PAIR_LEN
-    column_mean = sums[0] / count_valid
-    spread = sums[1] / count_valid - column_mean * column_mean
-    inverse = lax.rsqrt(spread + 1e-05)
-    row_weight = row_count / (sums[2, 0] / (slice_count * item_count))
-    standard = (tokens_w - column_mean) * inverse
-    unit, unit_inverse = stats(stream)
-    middle_unit, middle_inverse = stats(middle)
-    grad_out = cotangent_w.astype(F32) * row_weight[:, None]
-    mixed = dot(active, down_weights.reshape(-1, D)) + down_bias
-    layer_output = unwindows((middle + mixed).astype(BF))
-    pieces = range(shard_count)
-
-    def columns(v, r, size):
-        return v[:, r * size : (r + 1) * size]
-
-    grad_hidden = sum(dot_cols(columns(grad_pre, r, hidden_width), up_weights[r]) for r in pieces)
-    grad_middle = grad_out + norm_back(grad_hidden, middle_unit, middle_inverse, hidden_gain)
-    grad_attended = grad_middle.astype(BF)
-
-    owner_col = owner[:, None]
-    owner_row = owner[None, :]
-    grad_context = dot_cols(grad_attended, output_weights.reshape(-1, D)).astype(BF)
-    grad_qkv = attend_back(qkv, grad_context, owner_col, owner_row, shard_count)
-    grad_normed = sum(dot_cols(columns(grad_qkv, r, 3 * width), qkv_weights[r]) for r in pieces)
-
-    reduced = reduce_gradients(
-        active,
-        grad_mixed,
-        hidden_in,
-        grad_pre,
-        context,
-        grad_attended,
-        grad_qkv,
-        normed,
-    )
-    down_weight_grad = reduced[:4].reshape(hidden_width, D).astype(F32)
-    up_weight_grad = reduced[4:8].reshape(D, hidden_width).astype(F32)
-    output_weight_grad = reduced[8].astype(F32)
-    qkv_weight_grads = [reduced[9 + i].T.astype(F32) for i in range(3)]
-    grad_stream = grad_middle + norm_back(grad_normed, unit, unit_inverse, norm_gain)
-
-    def column_sums(v):
-        return jnp.sum(v.astype(F32), axis=0)
-
-    qkv_sums = column_sums(grad_qkv)
-    up_sums = column_sums(grad_pre)
-    bias_grads = [
-        jnp.concatenate(
-            [
-                qkv_sums[3 * r * width : (3 * r + 1) * width],
-                qkv_sums[(3 * r + 2) * width : 3 * (r + 1) * width],
-                up_sums[r * hidden_width : (r + 1) * hidden_width],
-            ]
-        )[None, :]
-        for r in pieces
+    reduced, finals, layer_output, tokens_grad = backward(
+        (item_lengths, item_group, group_count),
+        [v[None, :] for v in (norm_gain, hidden_gain, down_bias)],
+        saved[2],
+        saved[:2] + saved[3:],
+    )
+    down_weight_grad = reduced[:8].reshape(hidden_width, D).astype(F32)
+    up_weight_grad = reduced[8:16].reshape(D, hidden_width).astype(F32)
+    output_weight_grad = reduced[16:18].reshape(width, D).astype(F32)
+    qkv_weight_grads = [
+        reduced[18 + 2 * i : 20 + 2 * i].reshape(width, D).T.astype(F32) for i in range(3)
     ]
-    got = swap_mp(jnp.concatenate([bias_grads[1], bias_grads[3]], axis=0), 1)
-    bias_grad = bias_grads[0] + got[:1] + swap_mp(bias_grads[2] + got[1:], 2)
-    for bit in range(dp_bits()):
-        bias_grad = bias_grad + swap_dp(bias_grad, 1 << bit)
-    bias_grad = bias_grad[0]
-    finals = all_sum(
-        jnp.stack(
-            [
-                column_sums(grad_stream),
-                column_sums(grad_stream * standard),
-                column_sums(grad_normed * unit),
-                column_sums(grad_normed),
-                column_sums(grad_hidden * middle_unit),
-                column_sums(grad_hidden),
-                column_sums(grad_attended),
-                column_sums(grad_mixed),
-            ]
-        )
-    )
-    tokens_grad = unwindows(
-        inverse * (grad_stream - valid / count_valid * (finals[0] + finals[1] * standard))
-    )
+    bias_grad = finals[64:76].reshape(-1)
+    finals = finals[:64].reshape(8, D)
+    layer_output = unwindows(layer_output)
+    tokens_grad = unwindows(tokens_grad)
     return (
         layer_output,
         tokens_grad,

time: 480 us -> 345 us (0.72); the launches traced: 474 us -> 344 us
  matrix products: 48.2 us -> 0 us
  Pallas kernels: 337 us -> 296 us
  other arithmetic: 38.3 us -> 18.5 us
  starting transfers between devices: 25.8 us -> 9.17 us
  waiting for transfers between devices: 4.92 us -> 0.01 us
    dot_general x10 -> x0, matrix products: 48.2 us -> none  [the longest x9 38.2 us: dot_cols(): lax.dot_general(a, b, (((1,), (1,)), ((), ())), preferred_element_type=F32)]
    pallas_call x2 -> x1, Pallas kernels: 236 us -> 195 us  [backward(): pl.pallas_call(backward_kernel, out_shape=(shape((CHUNKS, CHUNK, D), BF),...]
    ppermute x12 -> x0, starting transfers between devices: 12.8 us -> none  [the longest x7 10.6 us: swap_dp(): return lax.ppermute(v, 'dp', [(i, i ^ mask) for i in range(count)])]
    reduce_sum x11 -> x0, other arithmetic: 12.4 us -> none  [the longest x5 9.7 us: column_sums(): return jnp.sum(v.astype(F32), axis=0)]
    unnamed x75 -> x14, local copies, waits for them, and re-layouts: 8.99 us -> 0.41 us
    convert_element_type x0 -> x3, local copies, waits for them, and re-layouts: none -> 5.14 us  [fast_shards(): reduced[18 + 2 * i:20 + 2 * i].reshape(width, D).T.astype(F32)]
    ppermute x12 -> x0, waiting for transfers between devices: 4.92 us -> none  [the longest x7 2.48 us: swap_dp(): return lax.ppermute(v, 'dp', [(i, i ^ mask) for i in range(count)])]
  transfers between devices with their start and end apart: 14 -> 2, of which waited for: 2 -> 0; matrix products, arithmetic and copies ran while one was open for 10% -> 9% of each run, Pallas kernels for 44% -> 0%
where the time goes in v2:
time: 345 us; the launch traced here: 344 us
  Pallas kernels  296 us (86%)
  local copies, waits for them, and re-layouts  19.5 us (6%)
  other arithmetic  18.5 us (5%)
  starting transfers between devices  9.17 us (3%)
    pallas_call x1, Pallas kernels, backward(): pl.pallas_call(backward_kernel, out_shape=(shape((CHUNKS, CHUNK, D), BF),...  195 us
    pallas_call x1, Pallas kernels, forward(): pl.pallas_call(forward_kernel, out_shape=outs, in_specs=[pl.BlockSpec(mem...  101 us
    ppermute x2, starting transfers between devices, unwindows(): lax.ppermute(own[:halo], 'mp', [(i + 1, i) for i in range(shard_count - 1)])  9.17 us
  transfers between devices with their start and end apart: 2, of which 0 were waited for; matrix products, arithmetic and copies ran while one was open for 9% of the time, Pallas kernels for 0%

profile of v2, /device:TPU:1, one launch (start us, length us, event | category | flops | bytes accessed | tf_op | source)
XLA Modules:
  0.0 344.1 jit_solution(5105474745812160330)
XLA Ops:
  0.7 100.7 %forward.1 = (bf16[608,1024]{1,0:T(8,128)(2,1)}, bf16[608,1024]{1,0:T(8,128)(2,1)}, f32[24,128]{1,0:T(8,128)}, f32[608,1024]{1,0:T(8,128)}, f32[608,1024]{1,0:T(...) custom-call(s32[16]{0:T(128)} %lengths.3, ...), custom_call_target="tpu_custom_call" | custom-call | tf_op jit(solution)/shard_map/forward/pallas_call | solution.py:814
  101.4 195.4 %backward.1 = (bf16[24,128,1024]{2,1,0:T(8,128)(2,1)}, f32[80,128]{1,0:T(8,128)}, bf16[608,1024]{1,0:T(8,128)(2,1)}, f32[608,1024]{1,0:T(8,128)}) custom-call(s32[16]{0:T(128)} %lengths.3, s32[16]{0:T(128)} %groups.3, s32[8]{0:T(128)} %counts.3, f32[1,1024]{1,0:T(1,128)} %bitcast.54, f32[1,1024]{1,0:T(1,128)} %bitcast.56, f32[1,1024]{1,0:T(1,128)} %bitcast.61, ...), custom_call_target="tpu_custom_call" | custom-call | tf_op jit(solution)/shard_map/backward/pallas_call | solution.py:1533
  296.7 1.7 slice.104
  298.5 7.0 %collective-permute-start.1 = (f32[66,1024]{1,0:T(8,128)}, f32[66,1024]{1,0:T(8,128)S(1)}, u32[]{:S(2)}, u32[]{:S(2)}) collective-permute-start(f32[66,1024]{1,0:T(8,128)} %slice.104), channel_id=1, source_target_pairs={{1,0},{2,1},{3,2},{5,4},{6,5},{7,6},{9,8},{10,9},{11,10},{13,12},{... | collective-permute-start | bytes 811016 | tf_op jit(solution)/shard_map/ppermute | solution.py:1872
  305.5 1.6 slice.100
  307.1 2.1 collective-permute-start
  309.2 4.2 %fusion.4 = (bf16[8,128,1024]{2,1,0:T(8,128)(2,1)S(1)}, bf16[8,128,1024]{2,1,0:T(8,128)(2,1)}) fusion(bf16[24,128,1024]{2,1,0:T(8,128)(2,1)} %get-tuple-element.56), kind=kLoop, calls=%fused_computation.27 | loop fusion | bytes 8388608 | tf_op jit(solution)/shard_map/slice | solution.py:1904
  313.4 2.8 fusion.5
  316.2 0.0 copy-done.2
  316.2 1.4 fusion.6
  317.7 0.4 copy-done.5
  318.1 1.0 fusion.7
  319.1 1.3 bitcast_convert_fusion.3
  320.4 2.5 copy.39
  322.9 1.3 copy.40
  324.2 1.1 bitcast_convert_fusion.5
  325.4 0.0 copy-start.6
  325.4 1.3 copy.38
  326.7 2.1 bitcast_convert_fusion.2
  328.8 0.0 copy-done.6
  328.8 0.6 slice_bitcast_fusion
  329.4 6.2 %bitcast_convert_fusion = (f32[1024,1024]{1,0:T(8,128)}, f32[1024,1024]{1,0:T(8,128)}) fusion(bf16[8,128,1024]{2,1,0:T(8,128)(2,1)S(1)} %get-tuple-element.57, bf16[8,128,1024]{2,1,0:T(8,128)(2,1)} %get-tuple-element.58), kind=kLoop, calls=%fused_computation.5 | loop fusion | flops 2097152 | bytes 12582912 | tf_op jit(solution)/shard_map/convert_element_type | solution.py:1904
  335.7 0.6 slice_bitcast_fusion.7
  336.2 0.0 collective-permute-done
  336.2 1.1 pad_select_fusion.1
  337.3 0.0 copy-done.3
  337.3 0.0 copy-done.4
  337.3 3.0 fusion.3
  340.3 0.0 collective-permute-done.1
  340.3 1.0 pad_select_fusion
  341.3 0.0 copy-done
  341.3 2.7 fusion.1
  (7 shorter events, 0.0 us)
Async XLA Ops:
  298.5 41.8 %collective-permute-start.1 = (f32[66,1024]{1,0:T(8,128)}, f32[66,1024]{1,0:T(8,128)S(1)}, u32[]{:S(2)}, u32[]{:S(2)}) collective-permute-start(f32[66,1024]{1,0:T(8,128)} %slice.104), channel_id=1, source_target_pairs={{1,0},{2,1},{3,2},{5,4},{6,5},{7,6},{9,8},{10,9},{11,10},{13,12},{... | collective-permute-start | bytes 811016 | tf_op jit(solution)/shard_map/ppermute | solution.py:1872
  307.1 29.2 %collective-permute-start = (bf16[66,1024]{1,0:T(8,128)(2,1)}, bf16[66,1024]{1,0:T(8,128)(2,1)}, u32[]{:S(2)}, u32[]{:S(2)}) collective-permute-start(bf16[66,1024]{1,0:T(8,128)(2,1)} %slice.100), channel_id=1, source_target_pairs={{1,0},{2,1},{3,2},{5,4},{6,5},{7,6},{9,8},{10,9},{11,10},{13,12},{... | collective-permute-start | bytes 405512 | tf_op jit(solution)/shard_map/ppermute | solution.py:1872
  313.4 2.9 copy-start.2
  316.2 1.8 copy-start.5
  325.4 3.4 %copy-start.6 = (f32[80,128]{1,0:T(8,128)S(1)}, f32[80,128]{1,0:T(8,128)}, u32[]{:S(2)}) copy-start(f32[80,128]{1,0:T(8,128)} %get-tuple-element.55) | copy-start | bytes 122884
  329.4 7.9 %copy-start.3 = (bf16[245,1024]{1,0:T(8,128)(2,1)S(1)}, bf16[245,1024]{1,0:T(8,128)(2,1)}, u32[]{:S(2)}) copy-start(bf16[245,1024]{1,0:T(8,128)(2,1)} %get-tuple-element.65) | copy-start | bytes 1505284
  329.4 7.9 %copy-start.4 = (bf16[245,1024]{1,0:T(8,128)(2,1)S(1)}, bf16[245,1024]{1,0:T(8,128)(2,1)}, u32[]{:S(2)}) copy-start(bf16[245,1024]{1,0:T(8,128)(2,1)} %get-tuple-element.66) | copy-start | bytes 1505284
  335.7 5.7 %copy-start = (f32[245,1024]{1,0:T(8,128)S(1)}, f32[245,1024]{1,0:T(8,128)}, u32[]{:S(2)}) copy-start(f32[245,1024]{1,0:T(8,128)} %get-tuple-element.63) | copy-start | bytes 3010564
  335.7 5.7 %copy-start.1 = (f32[245,1024]{1,0:T(8,128)S(1)}, f32[245,1024]{1,0:T(8,128)}, u32[]{:S(2)}) copy-start(f32[245,1024]{1,0:T(8,128)} %get-tuple-element.64) | copy-start | bytes 3010564

commit v3 on v2

--- a/solution.py
+++ b/solution.py
@@ -851,6 +851,7 @@
 TICK_HIDDEN, TICK_SECOND, TICK_CONTEXT, TICK_HEADS = 0, 4, 5, 6
 TICK_NORMED, TICK_FIRST, TICK_MIXED = 14, 18, 19
 TICK_SUMS = (18, 20, 22, 24)
+TICK_NEXT, TICK_LAYER, TICK_TOKENS = 25, 27, 28
 
 
 def backward_kernel(
@@ -904,6 +905,8 @@
     from_mp,
     from_y,
     from_z,
+    layer_next,
+    tokens_next,
     load_sem,
     act_sem,
     weight_sem,
@@ -922,12 +925,15 @@
     out_sem,
     stat_send,
     stat_recv,
+    next_send,
+    next_recv,
 ):
     mp, y, z, mp_peers, y_peer, z_places, z_peers = places()
     sibling, opposite, _ = mp_peers
     half = CHUNK // 2
     eighth = CHUNK // 8
     rows = normed.shape[0]
+    rows_here = layer_out.shape[0]
     width = context.shape[1] // 4
     blocks = rows // 32
 
@@ -947,8 +953,8 @@
                 ("tokens", tokens_ref, rowbuf),
                 ("active", active_ref, grad_pre),
                 ("middle again", middle_ref, stream),
-                ("layer", hidden, layer_out),
-                ("tokens_grad", gradient, tokens_grad_out),
+                ("layer", normed.at[pl.ds(0, rows_here)], layer_out),
+                ("tokens_grad", trunk.at[pl.ds(0, rows_here)], tokens_grad_out),
             )
         )
     }
@@ -1329,6 +1335,46 @@
 
         loop(blocks, body)
 
+    before = {"mp": (mp + 3) % 4}
+    layer_next_copy = remote(
+        hidden.at[pl.ds(0, HALO)], layer_next, next_send.at[0], next_recv.at[0], before
+    )
+    tokens_next_copy = remote(
+        gradient.at[pl.ds(0, HALO)], tokens_next, next_send.at[1], next_recv.at[1], before
+    )
+
+    def choose_rows(count, first):
+        row = lax.broadcasted_iota(jnp.int32, (rows_here, count), 0)
+        column = lax.broadcasted_iota(jnp.int32, (rows_here, count), 1) + first
+        place = row + (rows_here - 2 * PAIR_LEN) * mp
+        after = jnp.where(mp == 3, 2 * WINDOW, rows) - 2 * PAIR_LEN
+        wanted = jnp.where(
+            place < PAIR_LEN,
+            place,
+            jnp.where(place < 2 * PAIR_LEN, place + (WINDOW - PAIR_LEN), place + after),
+        )
+        return jnp.where(column == wanted, 1.0, 0.0).astype(BF)
+
+    def own_rows(value, following, target):
+        chosen, chosen_next = choose_rows(rows, 0), choose_rows(HALO, rows)
+        pairs = ((chosen, value), (chosen_next, following))
+
+        def tile(n):
+            columns = block_rows(n, 256)
+            total = jnp.zeros((rows_here, 256), F32)
+            for matrix, ref in pairs:
+                block = ref[:, columns]
+                high = block.astype(BF)
+                total = total + dot(matrix, high)
+                if ref.dtype == F32:
+                    middle_part = block - high.astype(F32)
+                    low = middle_part.astype(BF)
+                    total = total + dot(matrix, low)
+                    total = total + dot(matrix, (middle_part - low.astype(F32)).astype(BF))
+            target[0:rows_here, columns] = total.astype(target.dtype)
+
+        loop(4, tile)
+
     def work(k):
         for s in range(4):
 
@@ -1413,7 +1459,23 @@
         @pl.when(k == TICK_MIXED + 3)
         def _():
             layer_step()
+
+        @pl.when(k == TICK_NEXT)
+        def _():
+            layer_next_copy.start()
+            tokens_next_copy.start()
+
+        @pl.when(k == TICK_LAYER)
+        def _():
+            layer_next_copy.wait_recv()
+            own_rows(hidden, layer_next, normed)
             loads["layer"].start()
+
+        @pl.when(k == TICK_TOKENS)
+        def _():
+            tokens_next_copy.wait_recv()
+            own_rows(gradient, tokens_next, trunk)
+            loads["tokens_grad"].start()
 
         @pl.when(k == TICK_SUMS[1])
         def _():
@@ -1430,7 +1492,6 @@
             gather_sums(5, sums_c, from_z, 6)
             finals_out[...] = packet[6]
             tokens_step()
-            loads["tokens_grad"].start()
 
     waits = {0: ("grad_mixed",), 8: ("hidden",), 16: ("context",), 18: ("normed",)}
 
@@ -1474,11 +1535,13 @@
     loop(CHUNKS, finish)
     for copy in sums_a + sums_b + sums_c:
         copy.wait_send()
+    layer_next_copy.wait_send()
+    tokens_next_copy.wait_send()
     loads["layer"].wait()
     loads["tokens_grad"].wait()
 
 
-def backward(smalls, vectors, sums, saved):
+def backward(smalls, vectors, sums, saved, rows_here):
     (
         tokens,
         cotangent,
@@ -1526,13 +1589,20 @@
         shape((3, 80, 128), F32),
         shape((1, 80, 128), F32),
         shape((3, 80, 128), F32),
+        shape((HALO, D), BF),
+        shape((HALO, D), F32),
     ]
     dma = pltpu.SemaphoreType.DMA
     any_space = pl.BlockSpec(memory_space=pl.ANY)
     vmem = pl.BlockSpec(memory_space=pltpu.VMEM)
     return pl.pallas_call(
         backward_kernel,
-        out_shape=(shape((CHUNKS, CHUNK, D), BF), packed, low, full),
+        out_shape=(
+            shape((CHUNKS, CHUNK, D), BF),
+            packed,
+            shape((rows_here, D), BF),
+            shape((rows_here, D), F32),
+        ),
         in_specs=[pl.BlockSpec(memory_space=pltpu.SMEM)] * 3 + [vmem] * 4 + [any_space] * 15,
         out_specs=(any_space, vmem, any_space, any_space),
         scratch_shapes=[pltpu.VMEM(v.shape, v.dtype) for v in scratch]
@@ -1555,6 +1625,8 @@
             dma((CHUNKS,)),
             dma((3, 3)),
             dma((3, 3)),
+            dma((2,)),
+            dma((2,)),
         ],
         compiler_params=pltpu.CompilerParams(
             collective_id=2, has_side_effects=True, vmem_limit_bytes=67043328
@@ -1580,6 +1652,89 @@
         wup,
         wdown,
     )
+
+
+def finish_kernel(
+    down_ref,
+    up_ref,
+    output_ref,
+    query_ref,
+    key_ref,
+    value_ref,
+    finals_ref,
+    layer_ref,
+    tokens_ref,
+    down,
+    up,
+    output,
+    query,
+    key,
+    value,
+    layer,
+    tokens,
+    *vectors,
+):
+    down[...] = down_ref[0].astype(F32)
+    up[...] = up_ref[0].astype(F32)
+    output[...] = output_ref[0].astype(F32)
+    for source, target in ((query_ref, query), (key_ref, key), (value_ref, value)):
+        for half in range(2):
+            target[:, half * CHUNK : (half + 1) * CHUNK] = source[half].astype(F32).T
+    layer[...] = layer_ref[...]
+    tokens[...] = tokens_ref[...]
+
+    @pl.when(pl.program_id(0) == 0)
+    def _():
+        first = 0
+        for target in vectors:
+            size = target.shape[0]
+            target[...] = finals_ref[first : first + size, :]
+            first += size
+
+
+def finish(reduced, finals, layer, tokens, width):
+    shape = jax.ShapeDtypeStruct
+    rows_here = layer.shape[0]
+    share = rows_here // 8
+    sizes = (8,) * 8 + (2, 2, 8)
+    own = [pl.BlockSpec((share, D), lambda c: (c, 0))] * 2
+    specs = (
+        [
+            pl.BlockSpec((CHUNK, D), lambda c: (c, 0)),
+            pl.BlockSpec((CHUNK, D), lambda c: (c, 0)),
+            pl.BlockSpec((width // 8, D), lambda c: (c, 0)),
+        ]
+        + [pl.BlockSpec((CHUNK, width), lambda c: (c, 0))] * 3
+        + own
+    )
+    shapes = [
+        shape((D, D), F32),
+        shape((D, D), F32),
+        shape((width, D), F32),
+        shape((D, width), F32),
+        shape((D, width), F32),
+        shape((D, width), F32),
+        shape((rows_here, D), BF),
+        shape((rows_here, D), F32),
+    ]
+    return pl.pallas_call(
+        finish_kernel,
+        grid=(8,),
+        in_specs=[
+            pl.BlockSpec((1, CHUNK, D), lambda c: (c, 0, 0)),
+            pl.BlockSpec((1, CHUNK, D), lambda c: (8 + c, 0, 0)),
+            pl.BlockSpec((1, width // 8, D), lambda c: (16 + c // 4, c % 4, 0)),
+        ]
+        + [
+            pl.BlockSpec((2, CHUNK, CHUNK), lambda c, first=first: (first, 0, c))
+            for first in (9, 10, 11)
+        ]
+        + [pl.BlockSpec(finals.shape, lambda c: (0, 0))]
+        + own,
+        out_specs=specs + [pl.BlockSpec((size, 128), lambda c: (0, 0)) for size in sizes],
+        out_shape=shapes + [shape((size, 128), F32) for size in sizes],
+        name="finish",
+    )(*[reduced] * 6, finals, layer, tokens)
 
 
 def general_shards(
@@ -1853,28 +2008,7 @@
     down_weight,
     down_bias,
 ):
-    shard_count = lax.axis_size("mp")
-    mp = lax.axis_index("mp")
-    rows_here = tokens.shape[0]
-    pairs_here = PAIRS // shard_count
-    shift = rows_here - pairs_here * PAIR_LEN
-    halo = shift * (shard_count - 1)
-    padding = rows_here * shard_count - PAIRS * PAIR_LEN
-    rows = pairs_here * WINDOW + -(-padding // 32) * 32
-    is_last = mp == shard_count - 1
-    width = query_weight.shape[1]
-    hidden_width = up_weight.shape[1]
-
-    def unwindows(v):
-        own = jnp.concatenate(
-            [v[pair * WINDOW : pair * WINDOW + PAIR_LEN] for pair in range(pairs_here)], axis=0
-        )
-        after = lax.ppermute(own[:halo], "mp", [(i + 1, i) for i in range(shard_count - 1)])
-        after = jnp.concatenate([after, jnp.zeros((padding - halo, D), v.dtype)], axis=0)
-        tail = v[pairs_here * WINDOW : pairs_here * WINDOW + padding]
-        joined = jnp.concatenate([own, jnp.where(is_last, tail, after)], axis=0)
-        return lax.dynamic_slice_in_dim(joined, shift * mp, rows_here, axis=0)
-
+    rows = 2 * WINDOW + 96
     saved = forward(
         (item_lengths, item_group, group_count, grid_scale),
         [
@@ -1900,35 +2034,38 @@
         [v[None, :] for v in (norm_gain, hidden_gain, down_bias)],
         saved[2],
         saved[:2] + saved[3:],
-    )
-    down_weight_grad = reduced[:8].reshape(hidden_width, D).astype(F32)
-    up_weight_grad = reduced[8:16].reshape(D, hidden_width).astype(F32)
-    output_weight_grad = reduced[16:18].reshape(width, D).astype(F32)
-    qkv_weight_grads = [
-        reduced[18 + 2 * i : 20 + 2 * i].reshape(width, D).T.astype(F32) for i in range(3)
-    ]
-    bias_grad = finals[64:76].reshape(-1)
-    finals = finals[:64].reshape(8, D)
-    layer_output = unwindows(layer_output)
-    tokens_grad = unwindows(tokens_grad)
+        tokens.shape[0],
+    )
+    (
+        down_weight_grad,
+        up_weight_grad,
+        output_weight_grad,
+        query_weight_grad,
+        key_weight_grad,
+        value_weight_grad,
+        layer_output,
+        tokens_grad,
+        *vectors,
+    ) = finish(reduced, finals, layer_output, tokens_grad, query_weight.shape[1])
+    vectors = [v.reshape(-1) for v in vectors]
     return (
         layer_output,
         tokens_grad,
-        finals[2],
-        finals[3],
-        qkv_weight_grads[0],
-        bias_grad[:width],
-        qkv_weight_grads[1],
-        qkv_weight_grads[2],
-        bias_grad[width : 2 * width],
+        vectors[2],
+        vectors[3],
+        query_weight_grad,
+        vectors[8],
+        key_weight_grad,
+        value_weight_grad,
+        vectors[9],
         output_weight_grad,
-        finals[6],
-        finals[4],
-        finals[5],
+        vectors[6],
+        vectors[4],
+        vectors[5],
         up_weight_grad,
-        bias_grad[2 * width :],
+        vectors[10],
         down_weight_grad,
-        finals[7],
+        vectors[7],
     )
 
 

time: 345 us -> 312 us (0.904)
  local copies, waits for them, and re-layouts: 19.5 us -> 0 us
  other arithmetic: 18.5 us -> 0 us
  Pallas kernels: 296 us -> 308 us
  starting transfers between devices: 9.17 us -> 0 us
    slice x7 -> x0, local copies, waits for them, and re-layouts: 13.3 us -> none  [the longest x1 4.17 us: fast_shards(): down_weight_grad = reduced[:8].reshape(hidden_width, D).astype(F32)]
    pallas_call x0 -> x1, Pallas kernels: none -> 11.3 us  [finish(): pl.pallas_call(finish_kernel, grid=(8,), in_specs=[pl.BlockSpec((1, CHUNK...]
    convert_element_type x4 -> x0, other arithmetic: 10.8 us -> none  [the longest x1 6.23 us: fast_shards(): down_weight_grad = reduced[:8].reshape(hidden_width, D).astype(F32)]
    ppermute x2 -> x0, starting transfers between devices: 9.17 us -> none  [unwindows(): lax.ppermute(own[:halo], 'mp', [(i + 1, i) for i in range(shard_count - 1)])]
    concatenate x2 -> x0, other arithmetic: 5.66 us -> none  [unwindows(): joined = jnp.concatenate([own, jnp.where(is_last, tail, after)], axis=0)]
    convert_element_type x3 -> x0, local copies, waits for them, and re-layouts: 5.14 us -> none  [fast_shards(): reduced[18 + 2 * i:20 + 2 * i].reshape(width, D).T.astype(F32)]
  transfers between devices with their start and end apart: 2 -> 0, of which waited for: 0 -> 0; matrix products, arithmetic and copies ran while one was open for 9% -> 0% of each run, Pallas kernels for 0% -> 0%
where the time goes in v3:
time: 312 us; the launch traced here: 309 us
  Pallas kernels  308 us (99%)
    pallas_call x1, Pallas kernels, backward(): pl.pallas_call(backward_kernel, out_shape=(shape((CHUNKS, CHUNK, D), BF),...  196 us
    pallas_call x1, Pallas kernels, forward(): pl.pallas_call(forward_kernel, out_shape=outs, in_specs=[pl.BlockSpec(mem...  101 us
    pallas_call x1, Pallas kernels, finish(): pl.pallas_call(finish_kernel, grid=(8,), in_specs=[pl.BlockSpec((1, CHUNK...  11.3 us

profile of v3, /device:TPU:1, one launch (start us, length us, event | category | flops | bytes accessed | tf_op | source)
XLA Modules:
  0.0 308.6 jit_solution(12208550202431525243)
XLA Ops:
  0.7 100.7 %forward.1 = (bf16[608,1024]{1,0:T(8,128)(2,1)}, bf16[608,1024]{1,0:T(8,128)(2,1)}, f32[24,128]{1,0:T(8,128)}, f32[608,1024]{1,0:T(8,128)}, f32[608,1024]{1,0:T(...) custom-call(s32[16]{0:T(128)} %lengths.3, ...), custom_call_target="tpu_custom_call" | custom-call | tf_op jit(solution)/shard_map/forward/pallas_call | solution.py:814
  101.4 195.8 %backward.1 = (bf16[24,128,1024]{2,1,0:T(8,128)(2,1)}, f32[80,128]{1,0:T(8,128)}, bf16[512,1024]{1,0:T(8,128)(2,1)}, f32[512,1024]{1,0:T(8,128)}) custom-call(s32[16]{0:T(128)} %lengths.3, s32[16]{0:T(128)} %groups.3, s32[8]{0:T(128)} %counts.3, f32[1,1024]{1,0:T(1,128)} %bitcast.21, f32[1,1024]{1,0:T(1,128)} %bitcast.23, f32[1,1024]{1,0:T(1,128)} %bitcast.28, ...), custom_call_target="tpu_custom_call" | custom-call | tf_op jit(solution)/shard_map/backward/pallas_call | solution.py:1598
  297.1 11.3 %finish.1 = (f32[1024,1024]{1,0:T(8,128)}, f32[1024,1024]{1,0:T(8,128)}, f32[256,1024]{1,0:T(8,128)}, f32[1024,256]{1,0:T(8,128)}, f32[1024,256]{1,0:T(8,128)}, ...) custom-call(bf16[24,128,1024]{2,1,0:T(8,128)(2,1)} %get-tuple-elemen, ...), custom_call_target="tpu_custom_call" | custom-call | tf_op jit(solution)/shard_map/finish/pallas_call | solution.py:1720

commit v4 on v3

--- a/solution.py
+++ b/solution.py
@@ -209,6 +209,13 @@
 
 
 HALO = 80
+ROUTE_TICKS = (
+    (0, 0, 0, 0, 1, 1, 2, 2, 3, 4),
+    (1, 1, 1, 1, 2, 3, 4, 5, 6, 7),
+    (2, 2, 3, 3, 4, 5, 6, 7, 8, 9),
+    (5, 5, 6, 6, 9, 11, 13, 15, 17, 19),
+)
+AT_HEADS, AT_PAIRED, AT_QUERY, AT_OUTPUT, AT_HIDDEN, AT_DOWN = 4, 8, 10, 16, 19, 22
 MESH = pl.DeviceIdType.MESH
 
 
@@ -364,8 +371,10 @@
     pair_recv,
     x_send,
     x_recv,
-    z_send,
-    z_recv,
+    far_send,
+    far_recv,
+    near_send,
+    near_recv,
     y_send,
     y_recv,
     fwd_send,
@@ -378,17 +387,22 @@
     width = query_ref.shape[1]
     blocks = rows // 32
 
-    items = [
-        (key_ref, 0, D, wqkv, width, width, False),
-        (value_ref, 0, D, wqkv, 2 * width, width, False),
-        (query_ref, 0, D, wqkv, 0, width, True),
-        (output_ref, 0, width, wo, 0, D, False),
-        (up_ref, 0, D // 2, wup, 0, D, False),
-        (up_ref, D // 2, D // 2, wup, 0, D, False),
-        (down_ref, 3 * D // 4, D // 4, wdown, 0, D, False),
-        (down_ref, 0, 3 * D // 4, wdown, 0, D, True),
-    ]
-    KEY, VALUE, QUERY, OUTPUT, UP_A, UP_B, DOWN_A, DOWN_B = range(8)
+    items = (
+        [(key_ref, first, D // 2, wqkv, width, width, False) for first in (0, D // 2)]
+        + [(value_ref, first, D // 2, wqkv, 2 * width, width, False) for first in (0, D // 2)]
+        + [(output_ref, 0, width, wo, 0, D, False)]
+        + [(up_ref, first, D // 4, wup, 0, D, False) for first in range(0, D, D // 4)]
+        + [(down_ref, first, D // 4, wdown, 0, D, False) for first in (3 * D // 4,)]
+        + [(query_ref, 0, D, wqkv, 0, width, True), (down_ref, 0, 3 * D // 4, wdown, 0, D, True)]
+    )
+    relayed = range(10)
+    QUERY, DOWN = 10, 11
+    HEADS, OUTPUT, HIDDEN = (0, 1, 2, 3, QUERY), 4, (5, 6, 7, 8, 9, DOWN)
+    everything = range(len(items))
+    near = z % 2
+    far = z // 2
+    near_peer = {"dp": (z + 1 - 2 * near) * 2 + y}
+    far_peer = {"dp": ((z + 2) % 4) * 2 + y}
 
     def source(i, start, size):
         return items[i][0].at[pl.ds(items[i][1] + start, size)]
@@ -405,7 +419,7 @@
         pltpu.make_async_copy(
             source(i, 0, items[i][2]), place(i, 0, 0, items[i][2]), own_sem.at[i]
         )
-        for i in range(8)
+        for i in everything
     ]
     pair_copies = [
         remote(
@@ -415,27 +429,30 @@
             pair_recv.at[i],
             sibling,
         )
-        for i in range(8)
+        for i in everything
     ]
 
     def x_copy(i):
-        start, size = (0, items[i][2]) if items[i][6] else part_of(i, y * 4 + z, 1)
+        start, size = (
+            (0, items[i][2]) if items[i][6] else part_of(i, y * 4 + near * 2 + far, 1)
+        )
         return remote(
             source(i, start, size), place(i, 2, start, size), x_send.at[i], x_recv.at[i], opposite
         )
 
-    def z_copies(i):
-        start, size = part_of(i, y * 4 + z, 1)
+    def hop(i, first, eighths, send, recv, peer):
+        start, size = part_of(i, first, eighths)
         view = place(i, 2, start, size)
-        return [
-            remote(view, view, z_send.at[i, m], z_recv.at[i, m], peer)
-            for m, peer in enumerate(z_peers)
-        ]
+        return remote(view, view, send.at[i], recv.at[i], peer)
+
+    def far_copy(i):
+        return hop(i, y * 4 + near * 2 + far, 1, far_send, far_recv, far_peer)
+
+    def near_copy(i):
+        return hop(i, y * 4 + near * 2, 2, near_send, near_recv, near_peer)
 
     def y_copy(i):
-        start, size = part_of(i, y * 4, 4)
-        view = place(i, 2, start, size)
-        return remote(view, view, y_send.at[i], y_recv.at[i], y_peer)
+        return hop(i, y * 4, 4, y_send, y_recv, y_peer)
 
     def fwd_copy(i):
         size = items[i][2]
@@ -443,17 +460,7 @@
             place(i, 2, 0, size), place(i, 3, 0, size), fwd_send.at[i], fwd_recv.at[i], sibling
         )
 
-    def x_to_z(i):
-        x_copy(i).wait_recv()
-        start_all(z_copies(i))
-
-    def z_to_y(i):
-        wait_recv_all(z_copies(i))
-        y_copy(i).start()
-
-    def y_to_pair(i):
-        (x_copy(i) if items[i][6] else y_copy(i)).wait_recv()
-        fwd_copy(i).start()
+    route = (x_copy, far_copy, near_copy, y_copy, fwd_copy)
 
     keep = [
         pltpu.make_async_copy(ref, ext.at[pl.ds(HALO, rows_here)], halo_sem.at[which, 2])
@@ -489,28 +496,11 @@
     part[0, 16:24, :] = jnp.zeros((8, 128), F32) + weight_part
     greet(mp_peers + [y_peer] + z_peers)
 
-    def exchange(stage, peers, slots):
-        copies = [
-            remote(
-                part.at[stage],
-                slots.at[m],
-                stat_send.at[stage, m],
-                stat_recv.at[stage, m],
-                peer,
-            )
-            for m, peer in enumerate(peers)
-        ]
-        start_all(copies)
-        return copies
-
-    def total(stage, copies, slots):
-        value = part[stage]
-        for m, copy in enumerate(copies):
-            copy.wait_recv()
-            value = value + slots[m]
-        return value
-
-    sums_a = exchange(0, mp_peers, from_mp)
+    sums_a = [
+        remote(part.at[0], from_mp.at[m], stat_send.at[0, m], stat_recv.at[0, m], peer)
+        for m, peer in enumerate(mp_peers)
+    ]
+    start_all(sums_a)
     after = {"mp": (mp + 1) % 4}
     halo_copies = [
         remote(
@@ -529,124 +519,124 @@
         for r, peer in enumerate(mp_peers)
     ]
     start_all(halo_copies + bias_copies)
-    start_all([x_copy(i) for i in range(8)])
-    start_all([pair_copies[i] for i in (QUERY, KEY, VALUE, OUTPUT, UP_A, UP_B, DOWN_A, DOWN_B)])
-    part[1] = total(0, sums_a, from_mp)
-    sums_b = exchange(1, [y_peer], from_y)
-
-    place_id = lax.broadcasted_iota(jnp.int32, (64, 1), 0)
-    table_scale = choose_item(
-        place_id >> 4, [scales[groups[4 * mp + j]] for j in range(4)]
-    )
-    quarter = D // 4
-    lane = lax.broadcasted_iota(jnp.int32, (1, quarter), 1).astype(F32)
-    frequency = jnp.exp(-math.log(10000.0) * lane / quarter)
-    angle = ((place_id & 15).astype(F32) * table_scale) * frequency
-    table = jnp.concatenate([jnp.sin(angle), jnp.cos(angle)], axis=1)
-    row = lax.broadcasted_iota(jnp.int32, (rows, 64), 0)
-    column = lax.broadcasted_iota(jnp.int32, (rows, 64), 1)
-    item, position, in_pair, _ = item_of_rows(row, lengths, mp)
-    across = (position * 9363) >> 17
-    for half, code in enumerate((across, position - SIDE * across)):
-        chosen = jnp.where(in_pair & (column == item * 16 + code), 1.0, 0.0)
-        stream[:, half * 2 * quarter : (half + 1) * 2 * quarter] = lax.dot_general(
-            chosen,
-            table,
-            (((1,), (0,)), ((), ())),
-            precision=lax.Precision.HIGHEST,
-            preferred_element_type=F32,
+    start_all([x_copy(i) for i in everything])
+    start_all([pair_copies[i] for i in HEADS + (OUTPUT,) + HIDDEN])
+    sums_b = [
+        remote(part.at[1], from_y.at[0], stat_send.at[1, 0], stat_recv.at[1, 0], y_peer)
+    ]
+    sums_c = [
+        remote(part.at[2], from_z.at[m], stat_send.at[2, m], stat_recv.at[2, m], peer)
+        for m, peer in enumerate(z_peers)
+    ]
+
+    def position_table():
+        place_id = lax.broadcasted_iota(jnp.int32, (64, 1), 0)
+        table_scale = choose_item(
+            place_id >> 4, [scales[groups[4 * mp + j]] for j in range(4)]
         )
-    part[2] = total(1, sums_b, from_y)
-    sums_c = exchange(2, z_peers, from_z)
-    x_to_z(KEY)
-    x_to_z(VALUE)
-
-    wait_recv_all(halo_copies)
-    keep[1].wait()
-    own_len = 2 * PAIR_LEN
-    row = lax.broadcasted_iota(jnp.int32, (rows, HALO + rows_here), 0)
-    column = lax.broadcasted_iota(jnp.int32, (rows, HALO + rows_here), 1)
-    window = row >> 8
-    offset = row & (WINDOW - 1)
-    wanted = HALO - (rows_here - own_len) * mp + window * PAIR_LEN + offset
-    tail = jnp.where(mp == 3, HALO + rows_here - PADDING, 4096) + offset
-    wanted = jnp.where(window < 2, jnp.where(offset < PAIR_LEN, wanted, -1), tail)
-    chosen = jnp.where(column == wanted, 1.0, 0.0).astype(BF)
-    tokens[...] = dot(chosen, tokens_ext[...]).astype(BF)
-    cotangent[...] = dot(chosen, cotangent_ext[...]).astype(BF)
-    sums[...] = total(2, sums_c, from_z)
-
-    slices = lax.axis_size("dp")
-    count_valid = slices * PAIRS * PAIR_LEN
-    column_mean = joined(sums, 0) / count_valid
-    spread = joined(sums, 8) / count_valid - column_mean * column_mean
-    inverse = lax.rsqrt(spread + 1e-05)
-    mean_weight = sums[16:17, 0:1] / (slices * 16)
-
-    def first_norm(i):
-        here = block_rows(i, 32)
-        value = (tokens[here, :].astype(F32) - column_mean) * inverse + stream[here, :]
-        stream[here, :] = value
-        unit, _ = stats(value)
-        normed[here, :] = (unit * gain[...] + shift[...]).astype(BF)
-        row = i * 32 + lax.broadcasted_iota(jnp.int32, (32, 1), 0)
-        item, _, in_pair, _ = item_of_rows(row, lengths, mp)
-        row_weight = jnp.where(in_pair, choose_item(item, weights), 0.0) / mean_weight
-        grad_mixed[here, :] = (cotangent[here, :].astype(F32) * row_weight).astype(BF)
-
-    loop(blocks, first_norm)
-
-    def store(i, value, ref):
-        return pltpu.make_async_copy(value, ref, store_sem.at[i])
-
+        quarter = D // 4
+        lane = lax.broadcasted_iota(jnp.int32, (1, quarter), 1).astype(F32)
+        frequency = jnp.exp(-math.log(10000.0) * lane / quarter)
+        angle = ((place_id & 15).astype(F32) * table_scale) * frequency
+        table = jnp.concatenate([jnp.sin(angle), jnp.cos(angle)], axis=1)
+        row = lax.broadcasted_iota(jnp.int32, (rows, 64), 0)
+        column = lax.broadcasted_iota(jnp.int32, (rows, 64), 1)
+        item, position, in_pair, _ = item_of_rows(row, lengths, mp)
+        across = (position * 9363) >> 17
+        for half, code in enumerate((across, position - SIDE * across)):
+            chosen = jnp.where(in_pair & (column == item * 16 + code), 1.0, 0.0)
+            stream[:, half * 2 * quarter : (half + 1) * 2 * quarter] = lax.dot_general(
+                chosen,
+                table,
+                (((1,), (0,)), ((), ())),
+                precision=lax.Precision.HIGHEST,
+                preferred_element_type=F32,
+            )
+
+    def place_rows():
+        wait_recv_all(halo_copies)
+        keep[1].wait()
+        own_len = 2 * PAIR_LEN
+        row = lax.broadcasted_iota(jnp.int32, (rows, HALO + rows_here), 0)
+        column = lax.broadcasted_iota(jnp.int32, (rows, HALO + rows_here), 1)
+        window = row >> 8
+        offset = row & (WINDOW - 1)
+        wanted = HALO - (rows_here - own_len) * mp + window * PAIR_LEN + offset
+        tail = jnp.where(mp == 3, HALO + rows_here - PADDING, 4096) + offset
+        wanted = jnp.where(window < 2, jnp.where(offset < PAIR_LEN, wanted, -1), tail)
+        chosen = jnp.where(column == wanted, 1.0, 0.0).astype(BF)
+        tokens[...] = dot(chosen, tokens_ext[...]).astype(BF)
+        cotangent[...] = dot(chosen, cotangent_ext[...]).astype(BF)
+
+    def norm_rows(first, count):
+        slices = lax.axis_size("dp")
+        count_valid = slices * PAIRS * PAIR_LEN
+        column_mean = joined(sums, 0) / count_valid
+        spread = joined(sums, 8) / count_valid - column_mean * column_mean
+        inverse = lax.rsqrt(spread + 1e-05)
+        mean_weight = sums[16:17, 0:1] / (slices * 16)
+
+        def first_norm(i):
+            here = block_rows(i, 32)
+            value = (tokens[here, :].astype(F32) - column_mean) * inverse + stream[here, :]
+            stream[here, :] = value
+            unit, _ = stats(value)
+            normed[here, :] = (unit * gain[...] + shift[...]).astype(BF)
+            row = i * 32 + lax.broadcasted_iota(jnp.int32, (32, 1), 0)
+            item, _, in_pair, _ = item_of_rows(row, lengths, mp)
+            row_weight = jnp.where(in_pair, choose_item(item, weights), 0.0) / mean_weight
+            grad_mixed[here, :] = (cotangent[here, :].astype(F32) * row_weight).astype(BF)
+
+        def body(i):
+            first_norm(first + i)
+
+        loop(count, body)
+
+    def group_stores(value, target, r):
+        return value.at[r], target.at[r]
+
+    def column_stores(value, target, r):
+        columns = pl.ds(r * D, D)
+        return value.at[:, columns], target.at[:, columns]
+
+    plan = (
+        [
+            (AT_HEADS, ref, target)
+            for ref, target in (
+                (tokens, tokens_out),
+                (cotangent, cotangent_out),
+                (sums, sums_out),
+                (stream, stream_out),
+                (normed, normed_out),
+                (grad_mixed, grad_mixed_out),
+            )
+        ]
+        + [
+            (AT_OUTPUT, ref, target)
+            for ref, target in ((qkv, qkv_out), (context, context_out), (wqkv, wqkv_out))
+        ]
+        + [
+            (AT_HIDDEN, ref, target)
+            for ref, target in ((middle, middle_out), (hidden, hidden_out), (wo, wo_out))
+        ]
+        + [
+            (when,) + group_stores(ref, target, r)
+            for r, when in enumerate((AT_PAIRED, AT_PAIRED, AT_HIDDEN + 6, AT_HIDDEN + 6))
+            for ref, target in ((wup, wup_out), (wdown, wdown_out))
+        ]
+        + [
+            (AT_HIDDEN + 2 * r + 2,) + column_stores(ref, target, r)
+            for r in range(4)
+            for ref, target in ((active, active_out), (grad_pre, grad_pre_out))
+        ]
+    )
     stores = [
-        store(0, tokens, tokens_out),
-        store(1, cotangent, cotangent_out),
-        store(2, sums, sums_out),
-        store(3, stream, stream_out),
-        store(4, normed, normed_out),
-        store(5, grad_mixed, grad_mixed_out),
-        store(6, qkv, qkv_out),
-        store(7, context, context_out),
-        store(8, wqkv, wqkv_out),
-        store(9, middle, middle_out),
-        store(10, hidden, hidden_out),
-        store(11, wo, wo_out),
-        store(12, active, active_out),
-        store(13, grad_pre, grad_pre_out),
-        store(14, wup, wup_out),
-        store(15, wdown, wdown_out),
+        pltpu.make_async_copy(ref, target, store_sem.at[i])
+        for i, (_, ref, target) in enumerate(plan)
     ]
-    start_all(stores[:6])
-
-    for copy in bias_copies:
-        copy.wait_recv()
-
-    def head_group(r):
-        @pl.when(r == 0)
-        def _():
-            for i in (QUERY, KEY, VALUE):
-                own_copies[i].wait()
-
-        @pl.when(r == 1)
-        def _():
-            for i in (OUTPUT, UP_A, UP_B, DOWN_A):
-                x_to_z(i)
-            for i in (QUERY, KEY, VALUE):
-                pair_copies[i].wait_recv()
-
-        @pl.when(r == 2)
-        def _():
-            for i in (QUERY, KEY, VALUE):
-                y_to_pair(i)
-            z_to_y(OUTPUT)
-
-        @pl.when(r == 3)
-        def _():
-            for i in (QUERY, KEY, VALUE):
-                fwd_copy(i).wait_recv()
-            y_to_pair(OUTPUT)
-
+    last_tick = AT_HIDDEN + 8
+
+    def head_product(r):
         base = r * 3 * width
         for n in range(3):
             value = dot(normed[...], wqkv[r, :, n * width : (n + 1) * width])
@@ -654,40 +644,22 @@
                 value = value + bias[r, n // 2 : n // 2 + 1, :]
             qkv[:, pl.ds(pl.multiple_of(base + n * width, width), width)] = value.astype(BF)
 
-        @pl.when(r == 0)
-        def _():
-            z_to_y(KEY)
-            z_to_y(VALUE)
-
-        def head_pair(p):
-            lanes = [
-                pl.ds(pl.multiple_of(base + n * width + p * 128, 128), 128) for n in range(3)
-            ]
-            target = pl.ds(pl.multiple_of(r * width + p * 128, 128), 128)
-            for first, size in blocks_of(rows):
-                here = pl.ds(first, size)
-                same = owner_of_rows(
-                    first + lax.broadcasted_iota(jnp.int32, (size, 1), 0), lengths, mp
-                ) == owner_of_rows(
-                    first + lax.broadcasted_iota(jnp.int32, (1, size), 1), lengths, mp
-                )
-                q, k, v = [qkv[here, lane] for lane in lanes]
-                results = []
-                for h in range(2):
-                    cut = slice(h * HEAD_DIM, (h + 1) * HEAD_DIM)
-                    low = softmax_rows(q[:, cut], k[:, cut], same).astype(BF)
-                    results.append(dot(low, v[:, cut]).astype(BF))
-                context[here, target] = jnp.concatenate(results, axis=1)
-
-        loop(width // 128, head_pair)
-
-    loop(4, head_group)
-    start_all(stores[6:9])
-    z_to_y(UP_A)
-
-    own_copies[OUTPUT].wait()
-    pair_copies[OUTPUT].wait_recv()
-    fwd_copy(OUTPUT).wait_recv()
+    def head_pair(r, p):
+        base = r * 3 * width
+        lanes = [pl.ds(pl.multiple_of(base + n * width + p * 128, 128), 128) for n in range(3)]
+        target = pl.ds(pl.multiple_of(r * width + p * 128, 128), 128)
+        for first, size in blocks_of(rows):
+            here = pl.ds(first, size)
+            same = owner_of_rows(
+                first + lax.broadcasted_iota(jnp.int32, (size, 1), 0), lengths, mp
+            ) == owner_of_rows(first + lax.broadcasted_iota(jnp.int32, (1, size), 1), lengths, mp)
+            q, k, v = [qkv[here, lane] for lane in lanes]
+            results = []
+            for h in range(2):
+                cut = slice(h * HEAD_DIM, (h + 1) * HEAD_DIM)
+                low = softmax_rows(q[:, cut], k[:, cut], same).astype(BF)
+                results.append(dot(low, v[:, cut]).astype(BF))
+            context[here, target] = jnp.concatenate(results, axis=1)
 
     def attention_output(n):
         columns = block_rows(n, 256)
@@ -696,62 +668,147 @@
             value = value + dot(context[:, r * width : (r + 1) * width], wo[r, :, columns])
         middle[:, columns] = value
 
-    loop(4, attention_output)
-
     def second_norm(i):
         here = block_rows(i, 32)
         unit, _ = stats(middle[here, :])
         hidden[here, :] = (unit * hidden_gain[...] + hidden_shift[...]).astype(BF)
 
-    loop(blocks, second_norm)
-    start_all(stores[9:12])
-
-    def hidden_group(r):
-        @pl.when(r == 0)
-        def _():
-            for i in (UP_A, UP_B, DOWN_A, DOWN_B):
-                own_copies[i].wait()
-            z_to_y(UP_B)
-
-        @pl.when(r == 1)
-        def _():
-            y_to_pair(UP_A)
-            z_to_y(DOWN_A)
-            for i in (UP_A, UP_B, DOWN_A, DOWN_B):
-                pair_copies[i].wait_recv()
-
-        @pl.when(r == 2)
-        def _():
-            for i in (DOWN_B, UP_B, DOWN_A):
-                y_to_pair(i)
-
-        @pl.when(r == 3)
-        def _():
-            for i in (UP_A, UP_B, DOWN_A, DOWN_B):
-                fwd_copy(i).wait_recv()
-
-        def hidden_tile(n):
-            columns = block_rows(n, 256)
-            target = pl.ds(pl.multiple_of(r * D + n * 256, 256), 256)
-            preact = dot(hidden[...], wup[r, :, columns]) + bias[r, pl.ds(2 + n, 1), :]
-            value, slope = gelu_parts(preact)
-            active[:, target] = value
-            grad = dot_cols(grad_mixed[...], wdown[r, columns, :])
-            grad_pre[:, target] = (grad * slope).astype(BF)
-
-        loop(4, hidden_tile)
-
-    loop(4, hidden_group)
-    start_all(stores[12:])
-
-    for i in range(8):
+    def hidden_tile(r, n):
+        columns = block_rows(n, 256)
+        target = pl.ds(pl.multiple_of(r * D + n * 256, 256), 256)
+        preact = dot(hidden[...], wup[r, :, columns]) + bias[r, pl.ds(2 + n, 1), :]
+        value, slope = gelu_parts(preact)
+        active[:, target] = value
+        grad = dot_cols(grad_mixed[...], wdown[r, columns, :])
+        grad_pre[:, target] = (grad * slope).astype(BF)
+
+    actions = {}
+
+    def at(k, action):
+        actions.setdefault(k, []).append(action)
+
+    for stage in reversed(range(4)):
+        for i in relayed:
+
+            def advance(i=i, stage=stage):
+                route[stage](i).wait_recv()
+                route[stage + 1](i).start()
+
+            at(ROUTE_TICKS[stage][i], advance)
+
+    def pass_on(i):
+        x_copy(i).wait_recv()
+        fwd_copy(i).start()
+
+    def sums_stage(target, copies, slots, following):
+        def action():
+            value = part[target - 1]
+            for m, copy in enumerate(copies):
+                copy.wait_recv()
+                value = value + slots[m]
+            if following:
+                part[target] = value
+                start_all(following)
+            else:
+                sums[...] = value
+
+        return action
+
+    def received(indices, copies):
+        def action():
+            for i in indices:
+                copies(i)
+
+        return action
+
+    def own(i):
+        own_copies[i].wait()
+
+    def paired(i):
+        pair_copies[i].wait_recv()
+
+    def forwarded(i):
+        fwd_copy(i).wait_recv()
+
+    at(0, sums_stage(1, sums_a, from_mp, sums_b))
+    at(1, sums_stage(2, sums_b, from_y, sums_c))
+    at(2, sums_stage(3, sums_c, from_z, None))
+    at(AT_HEADS, lambda: wait_recv_all(bias_copies))
+    at(AT_HEADS, received(HEADS, own))
+    at(AT_HEADS + 3, received(HEADS, paired))
+    at(AT_QUERY, lambda: pass_on(QUERY))
+    at(AT_HEADS + 9, received(HEADS, forwarded))
+    at(AT_OUTPUT, received((OUTPUT,), own))
+    at(AT_OUTPUT, received((OUTPUT,), paired))
+    at(AT_OUTPUT, received((OUTPUT,), forwarded))
+    at(AT_PAIRED, received(HIDDEN, own))
+    at(AT_PAIRED, received(HIDDEN, paired))
+    at(AT_DOWN, lambda: pass_on(DOWN))
+    at(AT_HIDDEN + 6, received(HIDDEN, forwarded))
+    for copy, (when, _, _) in zip(stores, plan):
+        if when < last_tick:
+            at(when, copy.start)
+
+    def tick(k, carry):
+        for when, todo in sorted(actions.items()):
+
+            @pl.when(k == when)
+            def _(todo=todo):
+                for action in todo:
+                    action()
+
+        @pl.when(k == 0)
+        def _():
+            position_table()
+
+        @pl.when(k == 1)
+        def _():
+            place_rows()
+
+        @pl.when((k >= 2) & (k < 4))
+        def _():
+            norm_rows((k - 2) * 10, 10 - (k - 2))
+
+        step = k - AT_HEADS
+
+        @pl.when((step >= 0) & (step < 12) & (step % 3 == 0))
+        def _():
+            head_product(step // 3)
+
+        @pl.when((step >= 0) & (step < 12) & (step % 3 > 0))
+        def _():
+            head_pair(step // 3, step % 3 - 1)
+
+        @pl.when((k >= AT_OUTPUT) & (k < AT_OUTPUT + 2))
+        def _():
+            def body(n):
+                attention_output(2 * (k - AT_OUTPUT) + n)
+
+            loop(2, body)
+
+        @pl.when(k == AT_OUTPUT + 2)
+        def _():
+            loop(blocks, second_norm)
+
+        @pl.when((k >= AT_HIDDEN) & (k < AT_HIDDEN + 8))
+        def _():
+            def body(n):
+                j = 2 * (k - AT_HIDDEN) + n
+                hidden_tile(j // 4, j % 4)
+
+            loop(2, body)
+
+        return carry
+
+    lax.fori_loop(0, last_tick, tick, 0)
+    start_all([copy for copy, (when, _, _) in zip(stores, plan) if when >= last_tick])
+    for i in everything:
         pair_copies[i].wait_send()
         x_copy(i).wait_send()
         fwd_copy(i).wait_send()
         if not items[i][6]:
-            for copy in z_copies(i):
-                copy.wait_send()
-            y_copy(i).wait_send()
+            for copy in (far_copy, near_copy, y_copy):
+                copy(i).wait_send()
     for copy in bias_copies + halo_copies + sums_a + sums_b + sums_c:
         copy.wait_send()
     for copy in stores:
@@ -820,24 +877,15 @@
         out_specs=(any_space,) * len(outs),
         scratch_shapes=[pltpu.VMEM(v.shape, v.dtype) for v in scratch]
         + [
-            dma((8,)),
+            dma((13,)),
             dma((2, 3)),
-            dma((16,)),
+            dma((28,)),
             dma((3, 3)),
             dma((3, 3)),
             dma((3,)),
             dma((3,)),
-            dma((8,)),
-            dma((8,)),
-            dma((8,)),
-            dma((8,)),
-            dma((8, 3)),
-            dma((8, 3)),
-            dma((8,)),
-            dma((8,)),
-            dma((8,)),
-            dma((8,)),
-        ],
+        ]
+        + [dma((13,))] * 12,
         compiler_params=pltpu.CompilerParams(
             collective_id=1, has_side_effects=True, vmem_limit_bytes=67043328
         ),

time: 312 us -> 299 us (0.958)
  Pallas kernels: 308 us -> 298 us
    pallas_call x1, Pallas kernels: 196 us -> 190 us  [backward(): pl.pallas_call(backward_kernel, out_shape=(shape((CHUNKS, CHUNK, D), BF),...]
    pallas_call x1, Pallas kernels: 101 us -> 96.3 us  [forward(): pl.pallas_call(forward_kernel, out_shape=outs, in_specs=[pl.BlockSpec(mem...]
where the time goes in v4:
time: 299 us
  Pallas kernels  298 us (100%)
    pallas_call x1, Pallas kernels, backward(): pl.pallas_call(backward_kernel, out_shape=(shape((CHUNKS, CHUNK, D), BF),...  190 us
    pallas_call x1, Pallas kernels, forward(): pl.pallas_call(forward_kernel, out_shape=outs, in_specs=[pl.BlockSpec(mem...  96.3 us
    pallas_call x1, Pallas kernels, finish(): pl.pallas_call(finish_kernel, grid=(8,), in_specs=[pl.BlockSpec((1, CHUNK...  11.3 us

profile of v4, /device:TPU:1, one launch (start us, length us, event | category | flops | bytes accessed | tf_op | source)
XLA Modules:
  0.0 298.5 jit_solution(4471891659838439542)
XLA Ops:
  0.7 96.3 %forward.1 = (bf16[608,1024]{1,0:T(8,128)(2,1)}, bf16[608,1024]{1,0:T(8,128)(2,1)}, f32[24,128]{1,0:T(8,128)}, f32[608,1024]{1,0:T(8,128)}, f32[608,1024]{1,0:T(...) custom-call(s32[16]{0:T(128)} %lengths.3, ...), custom_call_target="tpu_custom_call" | custom-call | tf_op jit(solution)/shard_map/forward/pallas_call | solution.py:871
  96.9 190.1 %backward.1 = (bf16[24,128,1024]{2,1,0:T(8,128)(2,1)}, f32[80,128]{1,0:T(8,128)}, bf16[512,1024]{1,0:T(8,128)(2,1)}, f32[512,1024]{1,0:T(8,128)}) custom-call(s32[16]{0:T(128)} %lengths.3, s32[16]{0:T(128)} %groups.3, s32[8]{0:T(128)} %counts.3, f32[1,1024]{1,0:T(1,128)} %bitcast.21, f32[1,1024]{1,0:T(1,128)} %bitcast.23, f32[1,1024]{1,0:T(1,128)} %bitcast.28, ...), custom_call_target="tpu_custom_call" | custom-call | tf_op jit(solution)/shard_map/backward/pallas_call | solution.py:1646
  287.1 11.3 %finish.1 = (f32[1024,1024]{1,0:T(8,128)}, f32[1024,1024]{1,0:T(8,128)}, f32[256,1024]{1,0:T(8,128)}, f32[1024,256]{1,0:T(8,128)}, f32[1024,256]{1,0:T(8,128)}, ...) custom-call(bf16[24,128,1024]{2,1,0:T(8,128)(2,1)} %get-tuple-elemen, ...), custom_call_target="tpu_custom_call" | custom-call | tf_op jit(solution)/shard_map/finish/pallas_call | solution.py:1768

commit v5 on v4

--- a/solution.py
+++ b/solution.py
@@ -895,11 +895,12 @@
 
 CHUNK = 128
 CHUNKS = 24
+FINISH_STEPS = 2
 STAGE_DELAY = (0, 1, 3, 5, 7, 9, 11)
-TICK_HIDDEN, TICK_SECOND, TICK_CONTEXT, TICK_HEADS = 0, 4, 5, 6
-TICK_NORMED, TICK_FIRST, TICK_MIXED = 14, 18, 19
-TICK_SUMS = (18, 20, 22, 24)
-TICK_NEXT, TICK_LAYER, TICK_TOKENS = 25, 27, 28
+TICK_HIDDEN, TICK_SECOND, TICK_CONTEXT, TICK_HEADS = 1, 5, 6, 7
+TICK_NORMED, TICK_FIRST, TICK_MIXED = 15, 19, 20
+TICK_SUMS = (19, 21, 23, 25)
+TICK_NEXT, TICK_LAYER, TICK_TOKENS = 26, 28, 29
 
 
 def backward_kernel(
@@ -1722,8 +1723,9 @@
     tokens,
     *vectors,
 ):
-    down[...] = down_ref[0].astype(F32)
-    up[...] = up_ref[0].astype(F32)
+    for source, target in ((down_ref, down), (up_ref, up)):
+        for i in range(source.shape[0]):
+            target[i * CHUNK : (i + 1) * CHUNK, :] = source[i].astype(F32)
     output[...] = output_ref[0].astype(F32)
     for source, target in ((query_ref, query), (key_ref, key), (value_ref, value)):
         for half in range(2):
@@ -1743,16 +1745,18 @@
 def finish(reduced, finals, layer, tokens, width):
     shape = jax.ShapeDtypeStruct
     rows_here = layer.shape[0]
-    share = rows_here // 8
+    steps = FINISH_STEPS
+    share = rows_here // steps
+    taken = 8 // steps
     sizes = (8,) * 8 + (2, 2, 8)
     own = [pl.BlockSpec((share, D), lambda c: (c, 0))] * 2
     specs = (
         [
-            pl.BlockSpec((CHUNK, D), lambda c: (c, 0)),
-            pl.BlockSpec((CHUNK, D), lambda c: (c, 0)),
-            pl.BlockSpec((width // 8, D), lambda c: (c, 0)),
+            pl.BlockSpec((taken * CHUNK, D), lambda c: (c, 0)),
+            pl.BlockSpec((taken * CHUNK, D), lambda c: (c, 0)),
+            pl.BlockSpec((width // steps, D), lambda c: (c, 0)),
         ]
-        + [pl.BlockSpec((CHUNK, width), lambda c: (c, 0))] * 3
+        + [pl.BlockSpec((taken * CHUNK, width), lambda c: (c, 0))] * 3
         + own
     )
     shapes = [
@@ -1767,14 +1771,16 @@
     ]
     return pl.pallas_call(
         finish_kernel,
-        grid=(8,),
+        grid=(steps,),
         in_specs=[
-            pl.BlockSpec((1, CHUNK, D), lambda c: (c, 0, 0)),
-            pl.BlockSpec((1, CHUNK, D), lambda c: (8 + c, 0, 0)),
-            pl.BlockSpec((1, width // 8, D), lambda c: (16 + c // 4, c % 4, 0)),
+            pl.BlockSpec((taken, CHUNK, D), lambda c: (c, 0, 0)),
+            pl.BlockSpec((taken, CHUNK, D), lambda c: (steps + c, 0, 0)),
+            pl.BlockSpec(
+                (1, width // steps, D), lambda c: (16 + c // (steps // 2), c % (steps // 2), 0)
+            ),
         ]
         + [
-            pl.BlockSpec((2, CHUNK, CHUNK), lambda c, first=first: (first, 0, c))
+            pl.BlockSpec((2, CHUNK, taken * CHUNK), lambda c, first=first: (first, 0, c))
             for first in (9, 10, 11)
         ]
         + [pl.BlockSpec(finals.shape, lambda c: (0, 0))]

time: 299 us -> 296 us (0.990)
  Pallas kernels: 298 us -> 295 us
where the time goes in v5:
time: 296 us
  Pallas kernels  295 us (100%)
    pallas_call x1, Pallas kernels, backward(): pl.pallas_call(backward_kernel, out_shape=(shape((CHUNKS, CHUNK, D), BF),...  189 us
    pallas_call x1, Pallas kernels, forward(): pl.pallas_call(forward_kernel, out_shape=outs, in_specs=[pl.BlockSpec(mem...  96.3 us
    pallas_call x1, Pallas kernels, finish(): pl.pallas_call(finish_kernel, grid=(steps,), in_specs=[pl.BlockSpec((take...  9.25 us

profile of v5, /device:TPU:1, one launch (start us, length us, event | category | flops | bytes accessed | tf_op | source)
XLA Modules:
  0.0 295.8 jit_solution(3990024001563089171)
XLA Ops:
  0.7 96.3 %forward.1 = (bf16[608,1024]{1,0:T(8,128)(2,1)}, bf16[608,1024]{1,0:T(8,128)(2,1)}, f32[24,128]{1,0:T(8,128)}, f32[608,1024]{1,0:T(8,128)}, f32[608,1024]{1,0:T(...) custom-call(s32[16]{0:T(128)} %lengths.3, ...), custom_call_target="tpu_custom_call" | custom-call | tf_op jit(solution)/shard_map/forward/pallas_call | solution.py:871
  96.9 189.5 %backward.1 = (bf16[24,128,1024]{2,1,0:T(8,128)(2,1)}, f32[80,128]{1,0:T(8,128)}, bf16[512,1024]{1,0:T(8,128)(2,1)}, f32[512,1024]{1,0:T(8,128)}) custom-call(s32[16]{0:T(128)} %lengths.3, s32[16]{0:T(128)} %groups.3, s32[8]{0:T(128)} %counts.3, f32[1,1024]{1,0:T(1,128)} %bitcast.21, f32[1,1024]{1,0:T(1,128)} %bitcast.23, f32[1,1024]{1,0:T(1,128)} %bitcast.28, ...), custom_call_target="tpu_custom_call" | custom-call | tf_op jit(solution)/shard_map/backward/pallas_call | solution.py:1647
  286.4 9.3 %finish.1 = (f32[1024,1024]{1,0:T(8,128)}, f32[1024,1024]{1,0:T(8,128)}, f32[256,1024]{1,0:T(8,128)}, f32[1024,256]{1,0:T(8,128)}, f32[1024,256]{1,0:T(8,128)}, ...) custom-call(bf16[24,128,1024]{2,1,0:T(8,128)(2,1)} %get-tuple-elemen, ...), custom_call_target="tpu_custom_call" | custom-call | tf_op jit(solution)/shard_map/finish/pallas_call | solution.py:1772

commit v6 on v5

--- a/solution.py
+++ b/solution.py
@@ -213,9 +213,9 @@
     (0, 0, 0, 0, 1, 1, 2, 2, 3, 4),
     (1, 1, 1, 1, 2, 3, 4, 5, 6, 7),
     (2, 2, 3, 3, 4, 5, 6, 7, 8, 9),
-    (5, 5, 6, 6, 9, 11, 13, 15, 17, 19),
+    (6, 6, 7, 7, 10, 12, 14, 16, 18, 20),
 )
-AT_HEADS, AT_PAIRED, AT_QUERY, AT_OUTPUT, AT_HIDDEN, AT_DOWN = 4, 8, 10, 16, 19, 22
+AT_HEADS, AT_PAIRED, AT_QUERY, AT_OUTPUT, AT_HIDDEN, AT_DOWN = 4, 8, 10, 16, 19, 23
 MESH = pl.DeviceIdType.MESH
 
 
@@ -1562,7 +1562,6 @@
         sends = tuple(lambda c, f=f: start_all(f(c)) for f in send)
         for stage in (6, 5, 4, 3, 2):
             staged(stage, handle)
-        for stage in (2, 3, 4, 5, 6):
             staged(stage, sends)
         staged(0, handle)
         staged(1, handle)

time: 296 us -> 296 us (level)
  no operation moved by 1% of the time
where the time goes in v6:
time: 296 us; the launch traced here: 295 us
  Pallas kernels  294 us (99%)
    pallas_call x1, Pallas kernels, backward(): pl.pallas_call(backward_kernel, out_shape=(shape((CHUNKS, CHUNK, D), BF),...  190 us
    pallas_call x1, Pallas kernels, forward(): pl.pallas_call(forward_kernel, out_shape=outs, in_specs=[pl.BlockSpec(mem...  95 us
    pallas_call x1, Pallas kernels, finish(): pl.pallas_call(finish_kernel, grid=(steps,), in_specs=[pl.BlockSpec((take...  9.25 us

profile of v6, /device:TPU:1, one launch (start us, length us, event | category | flops | bytes accessed | tf_op | source)
XLA Modules:
  0.0 295.2 jit_solution(6024924394095008476)
XLA Ops:
  0.7 95.0 %forward.1 = (bf16[608,1024]{1,0:T(8,128)(2,1)}, bf16[608,1024]{1,0:T(8,128)(2,1)}, f32[24,128]{1,0:T(8,128)}, f32[608,1024]{1,0:T(8,128)}, f32[608,1024]{1,0:T(...) custom-call(s32[16]{0:T(128)} %lengths.3, ...), custom_call_target="tpu_custom_call" | custom-call | tf_op jit(solution)/shard_map/forward/pallas_call | solution.py:871
  95.7 190.1 %backward.1 = (bf16[24,128,1024]{2,1,0:T(8,128)(2,1)}, f32[80,128]{1,0:T(8,128)}, bf16[512,1024]{1,0:T(8,128)(2,1)}, f32[512,1024]{1,0:T(8,128)}) custom-call(s32[16]{0:T(128)} %lengths.3, s32[16]{0:T(128)} %groups.3, s32[8]{0:T(128)} %counts.3, f32[1,1024]{1,0:T(1,128)} %bitcast.21, f32[1,1024]{1,0:T(1,128)} %bitcast.23, f32[1,1024]{1,0:T(1,128)} %bitcast.28, ...), custom_call_target="tpu_custom_call" | custom-call | tf_op jit(solution)/shard_map/backward/pallas_call | solution.py:1646
  285.8 9.3 %finish.1 = (f32[1024,1024]{1,0:T(8,128)}, f32[1024,1024]{1,0:T(8,128)}, f32[256,1024]{1,0:T(8,128)}, f32[1024,256]{1,0:T(8,128)}, f32[1024,256]{1,0:T(8,128)}, ...) custom-call(bf16[24,128,1024]{2,1,0:T(8,128)(2,1)} %get-tuple-elemen, ...), custom_call_target="tpu_custom_call" | custom-call | tf_op jit(solution)/shard_map/finish/pallas_call | solution.py:1771

commit v7 on v5

--- a/solution.py
+++ b/solution.py
@@ -215,7 +215,7 @@
     (2, 2, 3, 3, 4, 5, 6, 7, 8, 9),
     (5, 5, 6, 6, 9, 11, 13, 15, 17, 19),
 )
-AT_HEADS, AT_PAIRED, AT_QUERY, AT_OUTPUT, AT_HIDDEN, AT_DOWN = 4, 8, 10, 16, 19, 22
+AT_HEADS, AT_PAIRED, AT_QUERY, AT_OUTPUT, AT_HIDDEN, AT_DOWN = 4, 12, 10, 16, 19, 22
 MESH = pl.DeviceIdType.MESH
 
 

time: 296 us -> 296 us (level)
  no operation moved by 1% of the time
where the time goes in v7:
time: 296 us
  Pallas kernels  295 us (100%)
    pallas_call x1, Pallas kernels, backward(): pl.pallas_call(backward_kernel, out_shape=(shape((CHUNKS, CHUNK, D), BF),...  189 us
    pallas_call x1, Pallas kernels, forward(): pl.pallas_call(forward_kernel, out_shape=outs, in_specs=[pl.BlockSpec(mem...  96.3 us
    pallas_call x1, Pallas kernels, finish(): pl.pallas_call(finish_kernel, grid=(steps,), in_specs=[pl.BlockSpec((take...  9.25 us

profile of v7, /device:TPU:1, one launch (start us, length us, event | category | flops | bytes accessed | tf_op | source)
XLA Modules:
  0.0 295.8 jit_solution(11246653656437449803)
XLA Ops:
  0.7 96.3 %forward.1 = (bf16[608,1024]{1,0:T(8,128)(2,1)}, bf16[608,1024]{1,0:T(8,128)(2,1)}, f32[24,128]{1,0:T(8,128)}, f32[608,1024]{1,0:T(8,128)}, f32[608,1024]{1,0:T(...) custom-call(s32[16]{0:T(128)} %lengths.3, ...), custom_call_target="tpu_custom_call" | custom-call | tf_op jit(solution)/shard_map/forward/pallas_call | solution.py:871
  96.9 189.5 %backward.1 = (bf16[24,128,1024]{2,1,0:T(8,128)(2,1)}, f32[80,128]{1,0:T(8,128)}, bf16[512,1024]{1,0:T(8,128)(2,1)}, f32[512,1024]{1,0:T(8,128)}) custom-call(s32[16]{0:T(128)} %lengths.3, s32[16]{0:T(128)} %groups.3, s32[8]{0:T(128)} %counts.3, f32[1,1024]{1,0:T(1,128)} %bitcast.21, f32[1,1024]{1,0:T(1,128)} %bitcast.23, f32[1,1024]{1,0:T(1,128)} %bitcast.28, ...), custom_call_target="tpu_custom_call" | custom-call | tf_op jit(solution)/shard_map/backward/pallas_call | solution.py:1647
  286.4 9.3 %finish.1 = (f32[1024,1024]{1,0:T(8,128)}, f32[1024,1024]{1,0:T(8,128)}, f32[256,1024]{1,0:T(8,128)}, f32[1024,256]{1,0:T(8,128)}, f32[1024,256]{1,0:T(8,128)}, ...) custom-call(bf16[24,128,1024]{2,1,0:T(8,128)(2,1)} %get-tuple-elemen, ...), custom_call_target="tpu_custom_call" | custom-call | tf_op jit(solution)/shard_map/finish/pallas_call | solution.py:1772
